TPU v7x, 32 devices: a whole 2x2x4 slice. The times are simulated.
32 devices in a mesh: groups: 2 (over x), ep: 16 (over z, y, core).
Axes of the slice: x: 2, y: 2, z: 4, core: 2. Of those that a mesh axis runs over, the one named last changes fastest.
Arguments:
- tokens: bfloat16 [2048, 2048], P(('groups', 'ep')), parts along dimension 0, may hold values from -6 to 6
- expert_ids: int32 [2048, 8], P(('groups', 'ep')), parts along dimension 0, may hold values from 0 to 15, as said below
- gate_values: float32 [2048, 8], P(('groups', 'ep')), parts along dimension 0, may hold values from 0.1 to 1
- expert_weights: bfloat16 [32, 2048, 3072], P(('groups', 'ep')), parts along dimension 0, as said below
- home_slot: int32 [32], P('groups'), parts along dimension 0, may hold values from 0 to 15, as said below
- spare_expert: int32 [32], P('groups'), parts along dimension 0, may hold values from -1 to 15, as said below
Outputs:
- moe_out: bfloat16 [2048, 2048], P(('groups', 'ep')), parts along dimension 0
There are 2 independent parts, one for each index of `groups`. A program takes and returns all parts, laid end to end along the dimension named above; each array names one. Nothing has to cross between parts.
Inputs may be any that keep to these rules, and one draw needn't show every extreme that they name: `expert_ids`: each row names 8 different experts. `home_slot`: a permutation of the experts. `spare_expert`: each expert is named a multiple of 3 times, at most 6, and some expert exactly 3 * 2 times; -1 stands in as many entries as the remainder of 16 divided by 3. `expert_weights`: the second slot of the device holding the k-th third of a split copy of expert e equals the matching gate, up and down columns (hidden units k * 256 to (k + 1) * 256 - 1) of e's home block.
All inputs are finite; a program needn't handle non-finite values.
Results may differ from a plain program's by a relative error of at most 0.0058.
Values may be sent and summed in bfloat16 or wider, within the bound.
No kernel may reach another device: no remote copies, remote signals or barrier semaphores. Data moves between devices by JAX's collectives and lax.ppermute only.
A program may use at most 128 MiB of HBM per device.

v0:
```python
import jax
import jax.numpy as jnp
from jax import lax
from jax.sharding import PartitionSpec as P


def expert_rows(token_rows, weight_block):
    hidden_width = weight_block.shape[1] // 3
    gate_up = jnp.dot(
        token_rows, weight_block[:, : 2 * hidden_width], preferred_element_type=jnp.float32
    )
    hidden = (jax.nn.silu(gate_up[:, :hidden_width]) * gate_up[:, hidden_width:]).astype(
        jnp.bfloat16
    )
    answer = lax.dot_general(
        hidden,
        weight_block[:, 2 * hidden_width :],
        (((1,), (1,)), ((), ())),
        preferred_element_type=jnp.float32,
    )
    return answer.astype(jnp.bfloat16)


def third_rows(token_rows, third_block):
    third_width = third_block.shape[1] // 3
    gate_up = jnp.dot(
        token_rows, third_block[:, : 2 * third_width], preferred_element_type=jnp.float32
    )
    hidden = (jax.nn.silu(gate_up[:, :third_width]) * gate_up[:, third_width:]).astype(jnp.bfloat16)
    return lax.dot_general(
        hidden,
        third_block[:, 2 * third_width :],
        (((1,), (1,)), ((), ())),
        preferred_element_type=jnp.float32,
    )


def routing(expert_ids, home_slot, spare_expert):
    experts = home_slot.shape[0]
    flat_ids = expert_ids.reshape(-1)
    expert_range = jnp.arange(experts, dtype=jnp.int32)
    holders = (spare_expert[None, :] == expert_range[:, None]).astype(jnp.int32)
    copies = 1 + jnp.sum(holders, axis=1) // 3
    holder_rank = jnp.cumsum(holders, axis=1) * holders
    chosen = (flat_ids[:, None] == expert_range[None, :]).astype(jnp.int32)
    earlier = jnp.cumsum(chosen, axis=0) - chosen
    arrival = jnp.sum(earlier * chosen, axis=1)
    copy_count = jnp.sum(chosen * copies[None, :], axis=1)
    home_device = jnp.sum(chosen * home_slot[None, :], axis=1)
    copy_index = arrival % copy_count
    position = arrival // copy_count
    rank_rows = jnp.dot(chosen, holder_rank)
    return (home_device, copy_index, position, rank_rows)


def shards(tokens, expert_ids, gate_values, expert_weights, home_slot, spare_expert):
    devices = lax.axis_size("ep")
    local_tokens = tokens.shape[0]
    feature = tokens.shape[1]
    top_count = expert_ids.shape[1]
    capacity = local_tokens * top_count // devices
    hidden_width = expert_weights.shape[2] // 4
    home_block = expert_weights[0, :, : 3 * hidden_width]
    repeated = jnp.repeat(tokens, top_count, axis=0)
    home_device, copy_index, position, rank_rows = routing(expert_ids, home_slot, spare_expert)
    served = position < capacity
    gate_flat = gate_values.reshape(-1)
    spare_block = expert_weights[0, :, 3 * hidden_width :]
    overflow = devices * capacity
    first_copy = served & (copy_index == 0)
    split_copy = served & (copy_index > 0)
    device_range = jnp.arange(devices, dtype=jnp.int32)
    home_target = jnp.where(first_copy, home_device * capacity + position, overflow)
    home_box = (
        jnp.zeros((overflow, feature), jnp.bfloat16).at[home_target].set(repeated, mode="drop")
    )
    spare_box = jnp.zeros((overflow, feature), jnp.bfloat16)
    third_targets = []
    for third_index in range(3):
        wanted = 3 * copy_index - 2 + third_index
        holder = jnp.sum(jnp.where(rank_rows == wanted[:, None], device_range[None, :], 0), axis=1)
        third_target = jnp.where(split_copy, holder * capacity + position, overflow)
        spare_box = spare_box.at[third_target].set(repeated, mode="drop")
        third_targets.append(third_target)
    outbox = (
        home_box.reshape(devices, capacity, feature),
        spare_box.reshape(devices, capacity, feature),
    )
    home_rows = lax.all_to_all(outbox[0], "ep", split_axis=0, concat_axis=0, tiled=True)
    spare_rows = lax.all_to_all(outbox[1], "ep", split_axis=0, concat_axis=0, tiled=True)
    answers = expert_rows(home_rows.reshape(-1, feature), home_block).reshape(home_rows.shape)
    partials = third_rows(spare_rows.reshape(-1, feature), spare_block).reshape(spare_rows.shape)
    answers_back = lax.all_to_all(answers, "ep", split_axis=0, concat_axis=0, tiled=True)
    partials_back = lax.all_to_all(partials, "ep", split_axis=0, concat_axis=0, tiled=True)
    answers_back, partials_back = (answers_back, partials_back)
    home_values = jnp.take(
        answers_back.reshape(-1, feature), home_target, axis=0, mode="fill", fill_value=0
    ).astype(jnp.float32)
    flat_partials = partials_back.reshape(-1, feature)
    split_sum = jnp.zeros((home_target.shape[0], feature), jnp.float32)
    for third_target in third_targets:
        split_sum = split_sum + jnp.take(
            flat_partials, third_target, axis=0, mode="fill", fill_value=0
        )
    split_rounded = lax.optimization_barrier(split_sum.astype(jnp.bfloat16))
    split_values = split_rounded.astype(jnp.float32)
    values = jnp.where(first_copy[:, None], home_values, split_values)
    weighted = values * gate_flat[:, None]
    return jnp.sum(weighted.reshape(local_tokens, top_count, feature), axis=1).astype(jnp.bfloat16)


def solution(mesh):
    in_specs = (
        P(("groups", "ep"), None),
        P(("groups", "ep"), None),
        P(("groups", "ep"), None),
        P(("groups", "ep"), None, None),
        P("groups"),
        P("groups"),
    )
    out_specs = P(("groups", "ep"), None)
    return jax.shard_map(shards, mesh=mesh, in_specs=in_specs, out_specs=out_specs, check_vma=False)
```

profile of v0, /device:TPU:13, one launch (start us, length us, event | category | flops | bytes accessed | tf_op | source)
XLA Modules:
  0.0 296.7 jit_solution(1587522894917769411)
XLA Ops:
  0.0 0.0 copy-start
  0.0 0.8 copy.8
  0.8 0.1 eq.128
  0.9 0.1 eq.124
  1.0 1.2 reduce-window.6
  2.2 0.2 slice_reduce_fusion
  2.4 0.8 fusion.42
  3.2 0.8 select_reduce_fusion.3
  4.0 0.4 compare_select_fusion.3
  4.4 0.0 copy-done
  4.4 5.1 %scatter_custom_fusion = bf16[512,2048]{1,0:T(8,128)(2,1)} fusion(s32[512]{0:T(512)S(1)} %bitcast.60, bf16[64,2048]{1,0:T(8,128)(2,1)S(1)} %copy-done, bf16[]{:T(256)} %constant.73.clone.1), kind=kCustom, calls=%fused_computation.17 | custom fusion | bytes 2359298 | tf_op jit(solution)/shard_map/scatter | solution.py:75
  9.5 0.0 copy-start.4
  9.5 6.7 %all-to-all-start = ((bf16[16,32,2048]{2,1,0:T(8,128)(2,1)}), bf16[16,32,2048]{2,1,0:T(8,128)(2,1)S(1)}, u32[]{:S(2)}, u32[]{:S(2)}) async-start(bf16[16,32,2048]{2,1,0:T(8,128)(2,1)} %bitcast.6), calls=%async_computation | async-start | bytes 4194304 | tf_op jit(solution)/shard_map/all_to_all | solution.py:89
  16.2 0.0 copy-done.4
  16.2 0.2 reduce_window_sum.28
  16.3 0.1 compare_and_fusion.5
  16.5 0.2 select_reduce_fusion
  16.8 5.1 %scatter_custom_fusion.1 = bf16[512,2048]{1,0:T(8,128)(2,1)} fusion(s32[512]{0:T(512)S(1)} %bitcast.68, bf16[64,2048]{1,0:T(8,128)(2,1)S(1)} %copy-done, bf16[]{:T(256)} %constant.73.clone.1), kind=kCustom, calls=%fused_computation.15 | custom fusion | bytes 2359298 | tf_op jit(solution)/shard_map/scatter | solution.py:83
  21.9 6.7 %scatter_custom_fusion.2 = bf16[512,2048]{1,0:T(8,128)(2,1)} fusion(bf16[512,2048]{1,0:T(8,128)(2,1)} %scatter_custom_fusion.1, s32[512]{0:T(512)S(1)} %bitcast.67, bf16[64,2048]{1,0:T(8,128)(2,1)S(1)} %copy-done), kind=kCustom, calls=%fused_computation.13 | custom fusion | bytes 2359296 | tf_op jit(solution)/shard_map/scatter | solution.py:83
  28.5 6.7 %scatter_custom_fusion.3 = bf16[512,2048]{1,0:T(8,128)(2,1)} fusion(bf16[512,2048]{1,0:T(8,128)(2,1)} %scatter_custom_fusion.2, s32[512]{0:T(512)S(1)} %bitcast.66, bf16[64,2048]{1,0:T(8,128)(2,1)S(1)} %copy-done), kind=kCustom, calls=%fused_computation.11 | custom fusion | bytes 2359296 | tf_op jit(solution)/shard_map/scatter | solution.py:83
  35.2 28.4 %all-to-all-done = bf16[16,32,2048]{2,1,0:T(8,128)(2,1)S(1)} async-done(((bf16[16,32,2048]{2,1,0:T(8,128)(2,1)}), bf16[16,32,2048]{2,1,0:T(8,128)(2,1)S(1)}, u32[]{:S(2)}, u32[]{:S(2)}) %all-to-all-start) | async-done | bytes 2097184 | tf_op jit(solution)/shard_map/all_to_all | solution.py:89
  63.6 4.8 %all-to-all-start.2 = ((bf16[16,32,2048]{2,1,0:T(8,128)(2,1)}), bf16[16,32,2048]{2,1,0:T(8,128)(2,1)}, u32[]{:S(2)}, u32[]{:S(2)}) async-start(bf16[16,32,2048]{2,1,0:T(8,128)(2,1)} %bitcast.17), calls=%async_computation.2 | async-start | bytes 4194304 | tf_op jit(solution)/shard_map/all_to_all | solution.py:90
  68.4 7.9 %slice_bitcast_fusion = bf16[2048,2304]{1,0:T(8,128)(2,1)} fusion(bf16[1,2048,3072]{2,1,0:T(8,128)(2,1)} %param.11), kind=kLoop, calls=%fused_computation.8 | loop fusion | bytes 18874368 | tf_op jit(solution)/shard_map/squeeze | solution.py:63
  76.3 5.5 %fusion = f32[512,1536]{1,0:T(8,128)S(1)} fusion(bf16[512,2048]{1,0:T(8,128)(2,1)S(1)} %bitcast.56, bf16[2048,2304]{1,0:T(8,128)(2,1)} %slice_bitcast_fusion), kind=kOutput, calls=%fused_computation.9 | convolution fusion | flops 3221225472 | bytes 11534336 | tf_op jit(solution)/shard_map/dot_general | solution.py:9
  81.8 5.2 %fusion.13 = bf16[512,2048]{1,0:T(8,128)(2,1)} fusion(bf16[2048,2304]{1,0:T(8,128)(2,1)} %slice_bitcast_fusion, f32[512,1536]{1,0:T(8,128)S(1)} %fusion), kind=kOutput, calls=%fused_computation.26 | convolution fusion | flops 1614020608 | bytes 8388608 | tf_op jit(solution)/shard_map/dot_general | solution.py:15
  86.9 28.9 %all-to-all-done.2 = bf16[16,32,2048]{2,1,0:T(8,128)(2,1)} async-done(((bf16[16,32,2048]{2,1,0:T(8,128)(2,1)}), bf16[16,32,2048]{2,1,0:T(8,128)(2,1)}, u32[]{:S(2)}, u32[]{:S(2)}) %all-to-all-start.2) | async-done | bytes 2097184 | tf_op jit(solution)/shard_map/all_to_all | solution.py:90
  115.9 4.8 %all-to-all-start.1 = ((bf16[16,32,2048]{2,1,0:T(8,128)(2,1)}), bf16[16,32,2048]{2,1,0:T(8,128)(2,1)S(1)}, u32[]{:S(2)}, u32[]{:S(2)}) async-start(bf16[16,32,2048]{2,1,0:T(8,128)(2,1)} %bitcast.57), calls=%async_computation.1 | async-start | bytes 4194304 | tf_op jit(solution)/shard_map/all_to_all | solution.py:93
  120.7 2.1 slice_bitcast_fusion.1
  122.8 2.8 fusion.16
  125.6 2.7 fusion.19
  128.3 39.7 %all-to-all-done.1 = bf16[16,32,2048]{2,1,0:T(8,128)(2,1)S(1)} async-done(((bf16[16,32,2048]{2,1,0:T(8,128)(2,1)}), bf16[16,32,2048]{2,1,0:T(8,128)(2,1)S(1)}, u32[]{:S(2)}, u32[]{:S(2)}) %all-to-all-start.1) | async-done | bytes 2097184 | tf_op jit(solution)/shard_map/all_to_all | solution.py:93
  168.1 0.0 copy-start.3
  168.1 4.9 %all-to-all-start.3 = ((f32[16,32,2048]{2,1,0:T(8,128)}), f32[16,32,2048]{2,1,0:T(8,128)}, u32[]{:S(2)}, u32[]{:S(2)}) async-start(f32[16,32,2048]{2,1,0:T(8,128)} %bitcast.55), calls=%async_computation.3 | async-start | bytes 8388608 | tf_op jit(solution)/shard_map/all_to_all | solution.py:94
  173.0 0.0 copy-done.3
  173.0 0.1 copy.11
  173.1 0.1 mul.134
  173.3 3.3 %gather_fusion = bf16[512,2048]{1,0:T(8,128)(2,1)} fusion(bf16[512,2048]{1,0:T(8,128)(2,1)S(1)} %bitcast.54, s32[1024]{0:T(1024)S(1)} %pad_clamp_fusion.3), kind=kCustom, calls=%fused_computation.3 | custom fusion | bytes 4196352 | tf_op jit(solution)/shard_map/jit(_take)/gather | solution.py:96
  176.6 88.9 %all-to-all-done.3 = f32[16,32,2048]{2,1,0:T(8,128)} async-done(((f32[16,32,2048]{2,1,0:T(8,128)}), f32[16,32,2048]{2,1,0:T(8,128)}, u32[]{:S(2)}, u32[]{:S(2)}) %all-to-all-start.3) | async-done | bytes 4194336 | tf_op jit(solution)/shard_map/all_to_all | solution.py:94
  265.5 7.6 %gather_fusion.1 = f32[512,2048]{1,0:T(8,128)} fusion(f32[512,2048]{1,0:T(8,128)} %bitcast.21, s32[1024]{0:T(1024)S(1)} %pad_clamp_fusion.2), kind=kCustom, calls=%fused_computation.clone | custom fusion | bytes 8390656 | tf_op jit(solution)/shard_map/jit(_take)/gather | solution.py:102
  273.1 7.6 %gather_fusion.2 = f32[512,2048]{1,0:T(8,128)} fusion(f32[512,2048]{1,0:T(8,128)} %bitcast.21, s32[1024]{0:T(1024)S(1)} %get-tuple-element.38), kind=kCustom, calls=%fused_computation.1.clone | custom fusion | bytes 8390656 | tf_op jit(solution)/shard_map/jit(_take)/gather | solution.py:102
  280.6 7.6 %gather_fusion.3 = f32[512,2048]{1,0:T(8,128)} fusion(f32[512,2048]{1,0:T(8,128)} %bitcast.21, s32[1024]{0:T(1024)S(1)} %get-tuple-element.37), kind=kCustom, calls=%fused_computation.2.clone | custom fusion | bytes 8390656 | tf_op jit(solution)/shard_map/jit(_take)/gather | solution.py:102
  288.2 0.0 copy-start.2
  288.2 5.4 %fusion.10 = bf16[512,2048]{1,0:T(8,128)(2,1)S(1)} fusion(f32[512,2048]{1,0:T(8,128)} %gather_fusion.3, f32[512,2048]{1,0:T(8,128)} %gather_fusion.2, f32[512,2048]{1,0:T(8,128)} %gather_fusion.1, pred[512]{0:T(512)(128)(4,1)S(1)} %get-tuple-element.30, pred[512]{0:T(512)(128)(4,1)S(1)} %get-tuple-element.23, pred[512]{0:T(512)(128)(4,1)S(1)} %get-tuple-element.20), kind=kLoop, calls=%fused_computation.21 | loop fusion | flops 6291456 | bytes 14681600 | tf_op jit(solution)/shard_map/convert_element_type | solution.py:105
  293.6 0.0 copy-start.1
  293.6 0.0 copy-done.2
  293.6 3.0 %bitcast_reduce_fusion = bf16[64,2048]{1,0:T(8,128)(2,1)} fusion(bf16[512,2048]{1,0:T(8,128)(2,1)S(1)} %fusion.10, f32[512]{0:T(512)S(1)} %mul.134, bf16[512,2048]{1,0:T(8,128)(2,1)S(1)} %copy-done.2, pred[512]{0:T(512)(128)(4,1)S(1)} %get-tuple-element.12, pred[512]{0:T(512)(128)(4,1)S(1)} %get-tuple-element.13), kind=kLoop, calls=%fused_computation.19 | loop fusion | flops 6160384 | bytes 4459520 | tf_op jit(solution)/shard_map/reduce_sum | solution.py:109
  296.7 0.0 copy-done.1
  (15 shorter events, 0.1 us)
Async XLA Ops:
  0.0 4.4 %copy-start = (bf16[64,2048]{1,0:T(8,128)(2,1)S(1)}, bf16[64,2048]{1,0:T(8,128)(2,1)}, u32[]{:S(2)}) copy-start(bf16[64,2048]{1,0:T(8,128)(2,1)} %param.8) | copy-start | bytes 786436
  9.5 6.7 %copy-start.4 = (s32[16]{0:T(128)S(1)}, s32[16]{0:T(128)}, u32[]{:S(2)}) copy-start(s32[16]{0:T(128)} %param.13) | copy-start | bytes 196
  9.5 54.1 %all-to-all-start = ((bf16[16,32,2048]{2,1,0:T(8,128)(2,1)}), bf16[16,32,2048]{2,1,0:T(8,128)(2,1)S(1)}, u32[]{:S(2)}, u32[]{:S(2)}) async-start(bf16[16,32,2048]{2,1,0:T(8,128)(2,1)} %bitcast.6), calls=%async_computation | async-start | bytes 4194304 | tf_op jit(solution)/shard_map/all_to_all | solution.py:89
  63.6 52.3 %all-to-all-start.2 = ((bf16[16,32,2048]{2,1,0:T(8,128)(2,1)}), bf16[16,32,2048]{2,1,0:T(8,128)(2,1)}, u32[]{:S(2)}, u32[]{:S(2)}) async-start(bf16[16,32,2048]{2,1,0:T(8,128)(2,1)} %bitcast.17), calls=%async_computation.2 | async-start | bytes 4194304 | tf_op jit(solution)/shard_map/all_to_all | solution.py:90
  115.9 52.2 %all-to-all-start.1 = ((bf16[16,32,2048]{2,1,0:T(8,128)(2,1)}), bf16[16,32,2048]{2,1,0:T(8,128)(2,1)S(1)}, u32[]{:S(2)}, u32[]{:S(2)}) async-start(bf16[16,32,2048]{2,1,0:T(8,128)(2,1)} %bitcast.57), calls=%async_computation.1 | async-start | bytes 4194304 | tf_op jit(solution)/shard_map/all_to_all | solution.py:93
  168.1 4.9 %copy-start.3 = (f32[64,8]{0,1:T(8,128)S(1)}, f32[64,8]{0,1:T(8,128)}, u32[]{:S(2)}) copy-start(f32[64,8]{0,1:T(8,128)} %param.10) | copy-start | bytes 6148
  168.1 97.4 %all-to-all-start.3 = ((f32[16,32,2048]{2,1,0:T(8,128)}), f32[16,32,2048]{2,1,0:T(8,128)}, u32[]{:S(2)}, u32[]{:S(2)}) async-start(f32[16,32,2048]{2,1,0:T(8,128)} %bitcast.55), calls=%async_computation.3 | async-start | bytes 8388608 | tf_op jit(solution)/shard_map/all_to_all | solution.py:94
  288.2 5.4 %copy-start.2 = (bf16[512,2048]{1,0:T(8,128)(2,1)S(1)}, bf16[512,2048]{1,0:T(8,128)(2,1)}, u32[]{:S(2)}) copy-start(bf16[512,2048]{1,0:T(8,128)(2,1)} %gather_fusion) | copy-start | bytes 6291460
  293.6 3.1 %copy-start.1 = (bf16[64,2048]{1,0:T(8,128)(2,1)S(1)}, bf16[64,2048]{1,0:T(8,128)(2,1)}, u32[]{:S(2)}) copy-start(bf16[64,2048]{1,0:T(8,128)(2,1)} %param.8) | copy-start | bytes 786436
where the time goes:
time: 297 us
  waiting for transfers between devices  186 us (63%)
  local copies, waits for them, and re-layouts  61.1 us (21%)
  starting transfers between devices  21.1 us (7%)
  matrix products  16.5 us (6%)
  other arithmetic  11.9 us (4%)
    all_to_all x1, waiting for transfers between devices, shards(): lax.all_to_all(partials, 'ep', split_axis=0, concat_axis=0, tiled=True)  88.9 us
    all_to_all x1, waiting for transfers between devices, shards(): lax.all_to_all(answers, 'ep', split_axis=0, concat_axis=0, tiled=True)  39.7 us
    all_to_all x1, waiting for transfers between devices, shards(): lax.all_to_all(outbox[1], 'ep', split_axis=0, concat_axis=0, tiled=True)  28.9 us
    all_to_all x1, waiting for transfers between devices, shards(): lax.all_to_all(outbox[0], 'ep', split_axis=0, concat_axis=0, tiled=True)  28.4 us
    gather x3, local copies, waits for them, and re-layouts, shards(): jnp.take(flat_partials, third_target, axis=0, mode='fill', fill_value=0)  22.8 us
    scatter x3, local copies, waits for them, and re-layouts, shards(): spare_box = spare_box.at[third_target].set(repeated, mode='drop')  18.4 us
    squeeze x1, local copies, waits for them, and re-layouts, shards(): home_block = expert_weights[0, :, :3 * hidden_width]  7.91 us
    all_to_all x1, starting transfers between devices, shards(): lax.all_to_all(outbox[0], 'ep', split_axis=0, concat_axis=0, tiled=True)  6.65 us
  transfers between devices with their start and end apart: 4, of which 4 were waited for; matrix products, arithmetic and copies ran while one was open for 16% of the time, Pallas kernels for 0%

commit v1 on v0

v1 whole, which is shorter than its diff:
```python
import functools

import jax
import jax.numpy as jnp
from jax import lax
from jax.experimental import pallas as pl
from jax.experimental.pallas import tpu as pltpu
from jax.sharding import PartitionSpec as P

LANES = 128
SUBS = 16
THIRD = 3
VMEM = pl.BlockSpec(memory_space=pltpu.VMEM)
SMEM = pl.BlockSpec(memory_space=pltpu.SMEM)


class Packing:
    def __init__(self, local_tokens, feature, experts):
        self.local_tokens = local_tokens
        self.feature = feature
        self.experts = experts
        self.cols = feature // LANES
        self.groups = local_tokens // SUBS
        self.half = self.groups // 2
        self.per_tile = max(1, LANES // (2 * experts))
        self.gate_tiles = pl.cdiv(self.groups, self.per_tile)
        self.tiles = self.groups * self.cols + self.gate_tiles
        self.split = self.half * self.cols

    def tile(self, group):
        return group * self.cols + (self.gate_tiles if group >= self.half else 0)


def pack_body(pk, capacity, devices, tokens_ref, ids_ref, gates_ref, spare_ref, out_ref):
    for group in range(pk.groups):
        for col in range(pk.cols):
            out_ref[pk.tile(group) + col] = tokens_ref[
                group * SUBS : (group + 1) * SUBS, col * LANES : (col + 1) * LANES
            ]
    rows = pk.local_tokens
    lane = lax.broadcasted_iota(jnp.int32, (1, LANES), 1)
    expert = lax.rem(lane, pk.experts)
    chosen = jnp.zeros((rows, LANES), jnp.float32)
    gate = jnp.zeros((rows, LANES), jnp.float32)
    for k in range(ids_ref.shape[1]):
        match = ids_ref[:, k : k + 1] == expert
        chosen = jnp.where(match, 1.0, chosen)
        gate = jnp.where(match, gates_ref[:, k : k + 1], gate)
    before = (
        lax.broadcasted_iota(jnp.int32, (rows, rows), 0)
        > lax.broadcasted_iota(jnp.int32, (rows, rows), 1)
    ).astype(jnp.float32).astype(jnp.bfloat16)
    arrival = jnp.dot(before, chosen.astype(jnp.bfloat16), preferred_element_type=jnp.float32)
    named = jnp.zeros((1, LANES), jnp.int32)
    for device in range(devices):
        named = named + (expert == spare_ref[device]).astype(jnp.int32)
    count = jnp.ones((1, LANES), jnp.int32)
    for copy in range(1, devices // THIRD + 1):
        count = count + (named >= THIRD * copy).astype(jnp.int32)
    gate = jnp.where(arrival < (count * capacity).astype(jnp.float32), gate, 0.0)
    high = gate.astype(jnp.bfloat16).astype(jnp.float32)
    low = gate - high
    value = jnp.where(lax.rem(lane // pk.experts, 2) == 0, high, low)
    slot = lane // (2 * pk.experts)
    for index in range(pk.gate_tiles):
        tile = jnp.zeros((SUBS, LANES), jnp.float32)
        for part in range(pk.per_tile):
            group = index * pk.per_tile + part
            if group < pk.groups:
                tile = jnp.where(slot == part, value[group * SUBS : (group + 1) * SUBS], tile)
        out_ref[pk.split + index] = tile.astype(jnp.bfloat16)


def pack(pk, capacity, devices, tokens, ids, gates, spare):
    return pl.pallas_call(
        functools.partial(pack_body, pk, capacity, devices),
        out_shape=jax.ShapeDtypeStruct((pk.tiles, SUBS, LANES), jnp.bfloat16),
        in_specs=[VMEM, VMEM, VMEM, SMEM],
        out_specs=VMEM,
        name="pack",
    )(tokens, ids, gates, spare)


def chunk_body(pk, pieces, outs, steps, *refs):
    count = len(pieces)
    home_ref, me_ref = refs[:2]
    buffers = refs[2 : 2 + count]
    gate_w, up_w, down_w = refs[2 + count : 5 + count]
    out_refs = refs[5 + count : 5 + count + len(outs)]
    x_ref, acc_ref = refs[5 + count + len(outs) :]
    step = pl.program_id(0)

    @pl.when(step == 0)
    def _():
        row = 0
        for buffer, groups in zip(buffers, pieces):
            for first, _, _ in groups:
                for col in range(pk.cols):
                    x_ref[row : row + SUBS, col * LANES : (col + 1) * LANES] = buffer[first + col]
                row += SUBS

    rows = x_ref[...]
    gate = jnp.dot(rows, gate_w[0], preferred_element_type=jnp.float32)
    up = jnp.dot(rows, up_w[0], preferred_element_type=jnp.float32)
    hidden = (gate / (1.0 + jnp.exp(-gate)) * up).astype(jnp.bfloat16)
    part = lax.dot_general(
        hidden, down_w[0], (((1,), (1,)), ((), ())), preferred_element_type=jnp.float32
    )

    @pl.when(step == 0)
    def _():
        acc_ref[...] = part

    @pl.when(step > 0)
    def _():
        acc_ref[...] += part

    @pl.when(step == steps - 1)
    def _():
        mine = jnp.int32(0)
        for e in range(pk.experts):
            mine = jnp.where(home_ref[e] == me_ref[0], e, mine)
        lane = lax.broadcasted_iota(jnp.int32, (1, LANES), 1)
        scales = []
        for buffer, groups in zip(buffers, pieces):
            for _, gate_tile, slot in groups:
                place = slot * 2 * pk.experts + mine
                wanted = (lane == place) | (lane == place + pk.experts)
                table = buffer[gate_tile].astype(jnp.float32)
                scales.append(jnp.sum(jnp.where(wanted, table, 0.0), axis=1, keepdims=True))
        row = 0
        for out_ref in out_refs:
            for start in range(0, out_ref.shape[0], SUBS):
                scaled = acc_ref[row : row + SUBS, :] * scales[row // SUBS]
                out_ref[start : start + SUBS, :] = scaled.astype(out_ref.dtype)
                row += SUBS


def chunk(pk, weights, home, me, own, crossed, outs):
    hidden_width = weights.shape[2] // 4
    block = hidden_width // THIRD
    steps = hidden_width // block
    pieces = []
    for buffer, kind in own + crossed:
        if kind == "first":
            picked, shift = range(pk.half), 0
        elif kind == "second":
            picked, shift = range(pk.half, pk.groups), pk.split
        else:
            picked, shift = range(pk.groups), 0
        pieces.append(
            [
                (
                    pk.tile(g) - shift,
                    pk.split - shift + g // pk.per_tile,
                    g % pk.per_tile,
                )
                for g in picked
            ]
        )
    buffers = [buffer for buffer, _ in own + crossed]
    total = SUBS * sum(len(groups) for groups in pieces)
    width = pk.feature

    def weight_spec(offset):
        return pl.BlockSpec((1, width, block), lambda j: (0, 0, offset * steps + j))

    flops = 2 * total * width * 3 * hidden_width
    moved = 2 * width * 3 * hidden_width + 4 * total * width
    return pl.pallas_call(
        functools.partial(chunk_body, pk, pieces, outs, steps),
        grid=(steps,),
        out_shape=[jax.ShapeDtypeStruct((r, width), d) for r, d in outs],
        in_specs=[SMEM, SMEM]
        + [pl.BlockSpec(b.shape, lambda j: (0, 0, 0)) for b in buffers]
        + [weight_spec(0), weight_spec(1), weight_spec(2)],
        out_specs=[pl.BlockSpec((r, width), lambda j: (0, 0)) for r, _ in outs],
        scratch_shapes=[
            pltpu.VMEM((total, width), jnp.bfloat16),
            pltpu.VMEM((total, width), jnp.float32),
        ],
        compiler_params=pltpu.CompilerParams(dimension_semantics=("arbitrary",)),
        cost_estimate=pl.CostEstimate(
            flops=flops, transcendentals=total * hidden_width, bytes_accessed=moved
        ),
        name="chunk",
    )(home, me, *buffers, weights, weights, weights)


def shards(tokens, expert_ids, gate_values, expert_weights, home_slot, spare_expert):
    devices = lax.axis_size("ep")
    local_tokens, feature = tokens.shape
    capacity = local_tokens * expert_ids.shape[1] // devices
    pk = Packing(local_tokens, feature, home_slot.shape[0])
    chips = devices // 2
    far = chips // 2
    ring = list(range(0, chips, 2)) + list(range(chips - 1, 0, -2))
    ahead = [
        (2 * ring[i] + c, 2 * ring[(i + 1) % chips] + c) for i in range(chips) for c in range(2)
    ]
    back = [(t, s) for s, t in ahead]
    pair = [(d, d ^ 1) for d in range(devices)]
    wire = jnp.bfloat16 if chips <= 8 else jnp.float32

    def send(x, where):
        return lax.ppermute(x, "ep", where)

    me = lax.axis_index("ep").astype(jnp.int32).reshape(1)
    run = functools.partial(chunk, pk, expert_weights, home_slot, me)
    packed = pack(pk, capacity, devices, tokens, expert_ids, gate_values, spare_expert)

    half_rows = pk.half * SUBS
    keep, give = {}, {}
    f = b = packed
    keep_own, give_own = run(
        [(packed, "all")],
        [(send(packed, pair), "all")],
        [(local_tokens, jnp.float32), (local_tokens, jnp.bfloat16)],
    )
    for r in range(1, far):
        f, b = send(f, ahead), send(b, back)
        fx, bx = send(f, pair), send(b, pair)
        keep_f, keep_b, gave = run(
            [(f, "all"), (b, "all")],
            [(fx, "all"), (bx, "all")],
            [
                (local_tokens, jnp.float32),
                (local_tokens, jnp.float32),
                (2 * local_tokens, jnp.bfloat16),
            ],
        )
        keep[r] = (keep_f, keep_b)
        give[r] = send(gave, pair)
    give_own = send(give_own, pair)
    cut = pk.split + pk.gate_tiles
    f, b = send(f[:cut], ahead), send(b[pk.split :], back)
    fx, bx = send(f, pair), send(b, pair)
    keep_far, gave = run(
        [(f, "first"), (b, "second")],
        [(fx, "first"), (bx, "second")],
        [(local_tokens, jnp.float32), (local_tokens, jnp.bfloat16)],
    )
    total = keep_far + send(gave, pair).astype(jnp.float32)
    to_back = send(total[:half_rows].astype(wire), back)
    to_ahead = send(total[half_rows:].astype(wire), ahead)
    pad_back = jnp.pad(to_back.astype(jnp.float32), ((0, local_tokens - half_rows), (0, 0)))
    pad_ahead = jnp.pad(to_ahead.astype(jnp.float32), ((half_rows, 0), (0, 0)))
    for r in range(far - 1, 0, -1):
        keep_f, keep_b = keep[r]
        gave = give[r].astype(jnp.float32)
        to_back = send((keep_f + gave[:local_tokens] + pad_back).astype(wire), back)
        to_ahead = send((keep_b + gave[local_tokens:] + pad_ahead).astype(wire), ahead)
        pad_back, pad_ahead = to_back.astype(jnp.float32), to_ahead.astype(jnp.float32)
    total = keep_own + give_own.astype(jnp.float32) + pad_back + pad_ahead
    return total.astype(jnp.bfloat16)


def solution(mesh):
    in_specs = (
        P(("groups", "ep"), None),
        P(("groups", "ep"), None),
        P(("groups", "ep"), None),
        P(("groups", "ep"), None, None),
        P("groups"),
        P("groups"),
    )
    out_specs = P(("groups", "ep"), None)
    return jax.shard_map(shards, mesh=mesh, in_specs=in_specs, out_specs=out_specs, check_vma=False)
```

time: 297 us -> 102 us (0.34)
  the two profiles are of different devices: /device:TPU:13 before, /device:TPU:0 now
where the time goes in v1:
time: 102 us
  Pallas kernels  41.8 us (41%)
  waiting for transfers between devices  29 us (28%)
  starting transfers between devices  20.3 us (20%)
  other arithmetic  5.44 us (5%)
  local copies, waits for them, and re-layouts  4.79 us (5%)
    pallas_call x5, Pallas kernels, chunk(): pl.pallas_call(functools.partial(chunk_body, pk, pieces, outs, steps), gr...  39.9 us
    ppermute x30, waiting for transfers between devices, send(): return lax.ppermute(x, 'ep', where)  29 us
    ppermute x30, starting transfers between devices, send(): return lax.ppermute(x, 'ep', where)  20.3 us
    unnamed x48, local copies, waits for them, and re-layouts  4.75 us
    convert_element_type x3, other arithmetic, shards(): to_back = send((keep_f + gave[:local_tokens] + pad_back).astype(wire), back)  3.23 us
  transfers between devices with their start and end apart: 30, of which 9 were waited for; matrix products, arithmetic and copies ran while one was open for 4% of the time, Pallas kernels for 39%

profile of v1, /device:TPU:0, one launch (start us, length us, event | category | flops | bytes accessed | tf_op | source)
XLA Modules:
  0.0 101.6 jit_solution(17428500413527326196)
XLA Ops:
  0.0 1.4 %copy.7.ids_ref = s32[64,8]{1,0:T(8,128)} copy(s32[64,8]{0,1:T(8,128)} %param.7) | data formatting | bytes 4096 | tf_op args[1]
  1.4 1.4 %copy.8.gates_ref = f32[64,8]{1,0:T(8,128)} copy(f32[64,8]{0,1:T(8,128)} %param.8) | data formatting | bytes 4096 | tf_op args[2]
  2.8 2.0 %pack.1.refs_2_ = bf16[65,16,128]{2,1,0:T(8,128)(2,1)} custom-call(bf16[64,2048]{1,0:T(8,128)(2,1)} %tokens_ref.1, s32[64,8]{1,0:T(8,128)} %copy.7.ids_ref, f32[64,8]{1,0:T(8,128)} %copy.8.gates_ref, s32[16]{0:T(128)} %spare_ref.1), custom_call_target="tpu_custom_call" | custom-call | tf_op jit(solution)/shard_map/pack/pallas_call | solution.py:75
  4.7 3.1 %collective-permute-start.2 = (bf16[65,16,128]{2,1,0:T(8,128)(2,1)}, bf16[65,16,128]{2,1,0:T(8,128)(2,1)S(1)}, u32[]{:S(2)}, u32[]{:S(2)}) collective-permute-start(bf16[65,16,128]{2,1,0:T(8,128)(2,1)} %pack.1.refs_2_), channel_id=1, source_target_pairs={{0,4},{1,5},{4,8},{5,9},{8,12},{9,13},{12,14},{13,15},{14,10},{15,... | collective-permute-start | bytes 798728 | tf_op jit(solution)/shard_map/ppermute | solution.py:206
  7.8 6.5 %collective-permute-done.2.refs_2_ = bf16[65,16,128]{2,1,0:T(8,128)(2,1)S(1)} collective-permute-done((bf16[65,16,128]{2,1,0:T(8,128)(2,1)}, bf16[65,16,128]{2,1,0:T(8,128)(2,1)S(1)}, u32[]{:S(2)}, u32[]{:S(2)}) %collective-permute-start.2) | collective-permute-done | bytes 266272 | tf_op jit(solution)/shard_map/ppermute | solution.py:206
  14.3 1.8 %collective-permute-start.7 = (bf16[65,16,128]{2,1,0:T(8,128)(2,1)S(1)}, bf16[65,16,128]{2,1,0:T(8,128)(2,1)S(1)}, u32[]{:S(2)}, u32[]{:S(2)}) collective-permute-start(bf16[65,16,128]{2,1,0:T(8,128)(2,1)S(1)} %collective-permute-done.2.refs_2_), channel_id=1, source_target_pairs={{0,4},{1,5},{4,8},{5,9},{8,12},{9,13},{12,14},{13,15},{14,10},{15,... | collective-permute-start | bytes 798728 | tf_op jit(solution)/shard_map/ppermute | solution.py:206
  16.1 0.0 collective-permute-done.3.refs_3_
  16.1 0.2 collective-permute-start.8
  16.4 5.5 %collective-permute-done.7.refs_2_ = bf16[65,16,128]{2,1,0:T(8,128)(2,1)S(1)} collective-permute-done((bf16[65,16,128]{2,1,0:T(8,128)(2,1)S(1)}, bf16[65,16,128]{2,1,0:T(8,128)(2,1)S(1)}, u32[]{:S(2)}, u32[]{:S(2)}) %collective-permute-start.7) | collective-permute-done | bytes 266272 | tf_op jit(solution)/shard_map/ppermute | solution.py:206
  21.9 1.5 %collective-permute-start.12 = (bf16[65,16,128]{2,1,0:T(8,128)(2,1)S(1)}, bf16[65,16,128]{2,1,0:T(8,128)(2,1)S(1)}, u32[]{:S(2)}, u32[]{:S(2)}) collective-permute-start(bf16[65,16,128]{2,1,0:T(8,128)(2,1)S(1)} %collective-permute-done.7.refs_2_), channel_id=1, source_target_pairs={{0,4},{1,5},{4,8},{5,9},{8,12},{9,13},{12,14},{13,15},{14,10},{15,... | collective-permute-start | bytes 798728 | tf_op jit(solution)/shard_map/ppermute | solution.py:206
  23.4 0.5 collective-permute-start.13
  23.9 4.7 %collective-permute-done.12.refs_2_ = bf16[65,16,128]{2,1,0:T(8,128)(2,1)S(1)} collective-permute-done((bf16[65,16,128]{2,1,0:T(8,128)(2,1)S(1)}, bf16[65,16,128]{2,1,0:T(8,128)(2,1)S(1)}, u32[]{:S(2)}, u32[]{:S(2)}) %collective-permute-start.12) | collective-permute-done | bytes 266272 | tf_op jit(solution)/shard_map/ppermute | solution.py:206
  28.6 1.4 %collective-permute-start.17 = (bf16[33,16,128]{2,1,0:T(8,128)(2,1)S(1)}, bf16[33,16,128]{2,1,0:T(8,128)(2,1)S(1)}, u32[]{:S(2)}, u32[]{:S(2)}) collective-permute-start(bf16[33,16,128]{2,1,0:T(8,128)(2,1)S(1)} %slice.45), channel_id=1, source_target_pairs={{0,4},{1,5},{4,8},{5,9},{8,12},{9,13},{12,14},{13,15},{14,10},{15,... | collective-permute-start | bytes 405512 | tf_op jit(solution)/shard_map/ppermute | solution.py:206
  30.0 0.1 collective-permute-done.13.refs_3_
  30.1 0.6 collective-permute-start.18
  30.8 2.9 %collective-permute-done.17.refs_2_ = bf16[33,16,128]{2,1,0:T(8,128)(2,1)S(1)} collective-permute-done((bf16[33,16,128]{2,1,0:T(8,128)(2,1)S(1)}, bf16[33,16,128]{2,1,0:T(8,128)(2,1)S(1)}, u32[]{:S(2)}, u32[]{:S(2)}) %collective-permute-start.17) | collective-permute-done | bytes 135200 | tf_op jit(solution)/shard_map/ppermute | solution.py:206
  33.7 0.0 collective-permute-start.19
  33.7 1.5 %collective-permute-done.18.refs_3_ = bf16[33,16,128]{2,1,0:T(8,128)(2,1)S(1)} collective-permute-done((bf16[33,16,128]{2,1,0:T(8,128)(2,1)S(1)}, bf16[33,16,128]{2,1,0:T(8,128)(2,1)S(1)}, u32[]{:S(2)}, u32[]{:S(2)}) %collective-permute-start.18) | collective-permute-done | bytes 135200 | tf_op jit(solution)/shard_map/ppermute | solution.py:206
  35.2 0.0 collective-permute-start.20
  35.2 0.5 collective-permute-start.14
  35.7 0.0 collective-permute-start.15
  35.7 0.0 collective-permute-done.19.refs_4_
  35.7 0.8 collective-permute-done.20.refs_5_
  36.6 0.7 copy-done.22
  37.2 7.2 %chunk.9 = (f32[64,2048]{1,0:T(8,128)}, bf16[64,2048]{1,0:T(8,128)(2,1)}) custom-call(s32[16]{0:T(128)} %refs_0_.9, s32[1]{0:T(128)} %bitcast.refs_1_, bf16[33,16,128]{2,1,0:T(8,128)(2,1)} %copy-done.19, bf16[33,16,128]{2,1,0:T(8,128)(2,1)} %copy-done.20, bf16[33,16,128]{2,1,0:T(8,128)(2,1)} %copy-done.21, bf16[33,16,128]{2,1,0:T(8,128)(2,1)} %copy-done.22, ...), custom_call_target="tpu_custom_call" | custom-call | flops 1207959552 | bytes 10485760 | tf_op jit(solution)/shard_map/chunk/pallas_call | solution.py:170
  44.5 0.2 collective-permute-start.21
  44.7 0.4 collective-permute-start.4
  45.1 0.1 collective-permute-start.5
  45.2 0.4 collective-permute-start.10
  45.6 0.0 collective-permute-done.15.refs_5_
  45.6 0.2 collective-permute-start.9
  45.8 0.1 copy-done.15
  46.0 0.4 copy-done.16
  46.3 8.4 %chunk.8 = (f32[64,2048]{1,0:T(8,128)}, f32[64,2048]{1,0:T(8,128)}, bf16[128,2048]{1,0:T(8,128)(2,1)}) custom-call(s32[16]{0:T(128)} %refs_0_.9, s32[1]{0:T(128)} %bitcast.refs_1_, bf16[65,16,128]{2,1,0:T(8,128)(2,1)} %copy-done.1, bf16[65,16,128]{2,1,0:T(8,128)(2,1)} %copy-done.2, bf16[65,16,128]{2,1,0:T(8,128)(2,1)} %copy-done.15, ...), custom_call_target="tpu_custom_call" | custom-call | flops 2415919104 | bytes 11534336 | tf_op jit(solution)/shard_map/chunk/pallas_call | solution.py:170
  54.8 0.0 collective-permute-done.21
  54.8 0.2 collective-permute-start.16
  55.1 0.0 collective-permute-done.10.refs_5_
  55.1 0.6 collective-permute-start.22
  55.7 0.0 collective-permute-done.9.refs_4_
  55.7 0.1 copy-done.17
  55.8 1.6 %collective-permute-start.26 = (bf16[32,2048]{1,0:T(8,128)(2,1)S(1)}, bf16[32,2048]{1,0:T(8,128)(2,1)}, u32[]{:S(2)}, u32[]{:S(2)}) collective-permute-start(bf16[32,2048]{1,0:T(8,128)(2,1)S(1)} %get-tuple-element.38), channel_id=1, source_target_pairs={{0,4},{1,5},{4,8},{5,9},{8,12},{9,13},{12,14},{13,15},{14,10},{15,... | collective-permute-start | bytes 393224 | tf_op jit(solution)/shard_map/ppermute | solution.py:206
  57.4 8.5 %chunk.7 = (f32[64,2048]{1,0:T(8,128)}, f32[64,2048]{1,0:T(8,128)}, bf16[128,2048]{1,0:T(8,128)(2,1)}) custom-call(s32[16]{0:T(128)} %refs_0_.9, s32[1]{0:T(128)} %bitcast.refs_1_, bf16[65,16,128]{2,1,0:T(8,128)(2,1)} %copy-done.13, bf16[65,16,128]{2,1,0:T(8,128)(2,1)} %copy-done.14, bf16[65,16,128]{2,1,0:T(8,128)(2,1)} %copy-done.18, ...), custom_call_target="tpu_custom_call" | custom-call | flops 2415919104 | bytes 11534336 | tf_op jit(solution)/shard_map/chunk/pallas_call | solution.py:170
  65.9 0.0 collective-permute-done.16
  65.9 0.1 collective-permute-start.11
  66.1 0.1 convert_element_type.65
  66.2 0.0 collective-permute-done.26
  66.2 1.8 %fusion.7 = (bf16[64,2048]{1,0:T(8,128)(2,1)}, bf16[64,2048]{1,0:T(8,128)(2,1)S(1)}) fusion(f32[64,2048]{1,0:T(8,128)S(1)} %copy-done.8, f32[128,2048]{1,0:T(8,128)S(1)} %convert_element_type.65, bf16[32,2048]{1,0:T(8,128)(2,1)} %collective-permute-done.22, bf16[32,2048]{1,0:T(8,128)(2,1)} %collective-permute-done.26, f32[64,2048]{1,0:T(8,128)S(1)} %copy-done.9), kind=kLoop, calls=%fused_computation.11 | loop fusion | flops 1048576 | bytes 2883584 | tf_op jit(solution)/shard_map/convert_element_type | solution.py:251
  68.1 0.5 collective-permute-start.23
  68.5 1.6 %collective-permute-start.27 = (bf16[64,2048]{1,0:T(8,128)(2,1)S(1)}, bf16[64,2048]{1,0:T(8,128)(2,1)}, u32[]{:S(2)}, u32[]{:S(2)}) collective-permute-start(bf16[64,2048]{1,0:T(8,128)(2,1)S(1)} %get-tuple-element.36), channel_id=1, source_target_pairs={{0,4},{1,5},{4,8},{5,9},{8,12},{9,13},{12,14},{13,15},{14,10},{15,... | collective-permute-start | bytes 786440 | tf_op jit(solution)/shard_map/ppermute | solution.py:206
  70.1 8.5 %chunk.6 = (f32[64,2048]{1,0:T(8,128)}, f32[64,2048]{1,0:T(8,128)}, bf16[128,2048]{1,0:T(8,128)(2,1)}) custom-call(s32[16]{0:T(128)} %refs_0_.9, s32[1]{0:T(128)} %bitcast.refs_1_, bf16[65,16,128]{2,1,0:T(8,128)(2,1)} %copy-done.11, bf16[65,16,128]{2,1,0:T(8,128)(2,1)} %copy-done.12, bf16[65,16,128]{2,1,0:T(8,128)(2,1)} %collective-permute-done.4.refs_4_, ...), custom_call_target="tpu_custom_call" | custom-call | flops 2415919104 | bytes 11534336 | tf_op jit(solution)/shard_map/chunk/pallas_call | solution.py:170
  78.6 0.5 collective-permute-start.6
  79.1 0.1 convert_element_type.64
  79.2 1.2 %fusion.9 = (bf16[64,2048]{1,0:T(8,128)(2,1)S(1)}, bf16[64,2048]{1,0:T(8,128)(2,1)S(1)}) fusion(f32[64,2048]{1,0:T(8,128)S(1)} %copy-done.4, f32[128,2048]{1,0:T(8,128)S(1)} %convert_element_type.64, bf16[64,2048]{1,0:T(8,128)(2,1)S(1)} %collective-permute-done.23, bf16[64,2048]{1,0:T(8,128)(2,1)} %collective-permute-done.27, f32[64,2048]{1,0:T(8,128)S(1)} %copy-done.5), kind=kLoop, calls=%fused_computation.14 | loop fusion | flops 1048576 | bytes 3145728 | tf_op jit(solution)/shard_map/convert_element_type | solution.py:251
  80.4 0.5 collective-permute-start.24
  80.9 1.6 %collective-permute-start.28 = (bf16[64,2048]{1,0:T(8,128)(2,1)S(1)}, bf16[64,2048]{1,0:T(8,128)(2,1)S(1)}, u32[]{:S(2)}, u32[]{:S(2)}) collective-permute-start(bf16[64,2048]{1,0:T(8,128)(2,1)S(1)} %get-tuple-element.34), channel_id=1, source_target_pairs={{0,4},{1,5},{4,8},{5,9},{8,12},{9,13},{12,14},{13,15},{14,10},{15,... | collective-permute-start | bytes 786440 | tf_op jit(solution)/shard_map/ppermute | solution.py:206
  82.5 0.7 copy-done.10
  83.2 7.2 %chunk.5 = (f32[64,2048]{1,0:T(8,128)}, bf16[64,2048]{1,0:T(8,128)(2,1)}) custom-call(s32[16]{0:T(128)} %refs_0_.9, s32[1]{0:T(128)} %bitcast.refs_1_, bf16[65,16,128]{2,1,0:T(8,128)(2,1)} %pack.1.refs_2_, bf16[65,16,128]{2,1,0:T(8,128)(2,1)} %copy-done.10, bf16[1,2048,3072]{2,1,0:T(8,128)(2,1)} %refs_8_.7, bf16[1,2048,3072]{2,1,0:T(8,128)(2,1)} %refs_8_.7, ...), custom_call_target="tpu_custom_call" | custom-call | flops 1207959552 | bytes 10485760 | tf_op jit(solution)/shard_map/chunk/pallas_call | solution.py:170
  90.4 0.1 convert_element_type.63
  90.6 0.2 fusion.11
  90.8 0.5 collective-permute-start.25
  91.3 1.6 %collective-permute-start.29 = (bf16[64,2048]{1,0:T(8,128)(2,1)S(1)}, bf16[64,2048]{1,0:T(8,128)(2,1)S(1)}, u32[]{:S(2)}, u32[]{:S(2)}) collective-permute-start(bf16[64,2048]{1,0:T(8,128)(2,1)S(1)} %get-tuple-element.32), channel_id=1, source_target_pairs={{0,4},{1,5},{4,8},{5,9},{8,12},{9,13},{12,14},{13,15},{14,10},{15,... | collective-permute-start | bytes 786440 | tf_op jit(solution)/shard_map/ppermute | solution.py:206
  92.9 6.7 %collective-permute-done.25 = bf16[64,2048]{1,0:T(8,128)(2,1)S(1)} collective-permute-done((bf16[64,2048]{1,0:T(8,128)(2,1)S(1)}, bf16[64,2048]{1,0:T(8,128)(2,1)S(1)}, u32[]{:S(2)}, u32[]{:S(2)}) %collective-permute-start.25) | collective-permute-done | bytes 262176 | tf_op jit(solution)/shard_map/ppermute | solution.py:206
  99.6 0.2 collective-permute-done.29
  99.7 1.9 %add_convert_fusion = bf16[64,2048]{1,0:T(8,128)(2,1)} fusion(bf16[64,2048]{1,0:T(8,128)(2,1)S(1)} %collective-permute-done.29, bf16[64,2048]{1,0:T(8,128)(2,1)S(1)} %collective-permute-done.25, f32[64,2048]{1,0:T(8,128)} %get-tuple-element.18, bf16[64,2048]{1,0:T(8,128)(2,1)S(1)} %collective-permute-done.1), kind=kLoop, calls=%fused_computation.18 | loop fusion | flops 917504 | bytes 1572864 | tf_op jit(solution)/shard_map/convert_element_type | solution.py:255
  (61 shorter events, 0.2 us)
Async XLA Ops:
  4.7 9.6 %collective-permute-start.2 = (bf16[65,16,128]{2,1,0:T(8,128)(2,1)}, bf16[65,16,128]{2,1,0:T(8,128)(2,1)S(1)}, u32[]{:S(2)}, u32[]{:S(2)}) collective-permute-start(bf16[65,16,128]{2,1,0:T(8,128)(2,1)} %pack.1.refs_2_), channel_id=1, source_target_pairs={{0,4},{1,5},{4,8},{5,9},{8,12},{9,13},{12,14},{13,15},{14,10},{15,... | collective-permute-start | bytes 798728 | tf_op jit(solution)/shard_map/ppermute | solution.py:206
  7.8 8.3 %collective-permute-start.3 = (bf16[65,16,128]{2,1,0:T(8,128)(2,1)}, bf16[65,16,128]{2,1,0:T(8,128)(2,1)S(1)}, u32[]{:S(2)}, u32[]{:S(2)}) collective-permute-start(bf16[65,16,128]{2,1,0:T(8,128)(2,1)} %pack.1.refs_2_), channel_id=1, source_target_pairs={{4,0},{5,1},{8,4},{9,5},{12,8},{13,9},{14,12},{15,13},{10,14},{11,... | collective-permute-start | bytes 798728 | tf_op jit(solution)/shard_map/ppermute | solution.py:206
  14.3 30.4 %copy-start.11 = (bf16[65,16,128]{2,1,0:T(8,128)(2,1)}, bf16[65,16,128]{2,1,0:T(8,128)(2,1)S(1)}, u32[]{:S(2)}) copy-start(bf16[65,16,128]{2,1,0:T(8,128)(2,1)S(1)} %collective-permute-done.2.refs_2_) | copy-start | bytes 798724
  14.3 7.6 %collective-permute-start.7 = (bf16[65,16,128]{2,1,0:T(8,128)(2,1)S(1)}, bf16[65,16,128]{2,1,0:T(8,128)(2,1)S(1)}, u32[]{:S(2)}, u32[]{:S(2)}) collective-permute-start(bf16[65,16,128]{2,1,0:T(8,128)(2,1)S(1)} %collective-permute-done.2.refs_2_), channel_id=1, source_target_pairs={{0,4},{1,5},{4,8},{5,9},{8,12},{9,13},{12,14},{13,15},{14,10},{15,... | collective-permute-start | bytes 798728 | tf_op jit(solution)/shard_map/ppermute | solution.py:206
  16.1 28.9 %copy-start.12 = (bf16[65,16,128]{2,1,0:T(8,128)(2,1)}, bf16[65,16,128]{2,1,0:T(8,128)(2,1)S(1)}, u32[]{:S(2)}) copy-start(bf16[65,16,128]{2,1,0:T(8,128)(2,1)S(1)} %collective-permute-done.3.refs_3_) | copy-start | bytes 798724
  16.1 7.3 %collective-permute-start.8 = (bf16[65,16,128]{2,1,0:T(8,128)(2,1)S(1)}, bf16[65,16,128]{2,1,0:T(8,128)(2,1)S(1)}, u32[]{:S(2)}, u32[]{:S(2)}) collective-permute-start(bf16[65,16,128]{2,1,0:T(8,128)(2,1)S(1)} %collective-permute-done.3.refs_3_), channel_id=1, source_target_pairs={{4,0},{5,1},{8,4},{9,5},{12,8},{13,9},{14,12},{15,13},{10,14},{11,... | collective-permute-start | bytes 798728 | tf_op jit(solution)/shard_map/ppermute | solution.py:206
  21.9 23.7 %copy-start.13 = (bf16[65,16,128]{2,1,0:T(8,128)(2,1)}, bf16[65,16,128]{2,1,0:T(8,128)(2,1)S(1)}, u32[]{:S(2)}) copy-start(bf16[65,16,128]{2,1,0:T(8,128)(2,1)S(1)} %collective-permute-done.7.refs_2_) | copy-start | bytes 798724
  21.9 6.7 %collective-permute-start.12 = (bf16[65,16,128]{2,1,0:T(8,128)(2,1)S(1)}, bf16[65,16,128]{2,1,0:T(8,128)(2,1)S(1)}, u32[]{:S(2)}, u32[]{:S(2)}) collective-permute-start(bf16[65,16,128]{2,1,0:T(8,128)(2,1)S(1)} %collective-permute-done.7.refs_2_), channel_id=1, source_target_pairs={{0,4},{1,5},{4,8},{5,9},{8,12},{9,13},{12,14},{13,15},{14,10},{15,... | collective-permute-start | bytes 798728 | tf_op jit(solution)/shard_map/ppermute | solution.py:206
  23.4 21.8 %copy-start.14 = (bf16[65,16,128]{2,1,0:T(8,128)(2,1)}, bf16[65,16,128]{2,1,0:T(8,128)(2,1)S(1)}, u32[]{:S(2)}) copy-start(bf16[65,16,128]{2,1,0:T(8,128)(2,1)S(1)} %collective-permute-done.8.refs_3_) | copy-start | bytes 798724
  23.4 6.7 %collective-permute-start.13 = (bf16[65,16,128]{2,1,0:T(8,128)(2,1)S(1)}, bf16[65,16,128]{2,1,0:T(8,128)(2,1)S(1)}, u32[]{:S(2)}, u32[]{:S(2)}) collective-permute-start(bf16[65,16,128]{2,1,0:T(8,128)(2,1)S(1)} %collective-permute-done.8.refs_3_), channel_id=1, source_target_pairs={{4,0},{5,1},{8,4},{9,5},{12,8},{13,9},{14,12},{15,13},{10,14},{11,... | collective-permute-start | bytes 798728 | tf_op jit(solution)/shard_map/ppermute | solution.py:206
  28.6 15.9 %copy-start.1 = (bf16[65,16,128]{2,1,0:T(8,128)(2,1)}, bf16[65,16,128]{2,1,0:T(8,128)(2,1)S(1)}, u32[]{:S(2)}) copy-start(bf16[65,16,128]{2,1,0:T(8,128)(2,1)S(1)} %collective-permute-done.12.refs_2_) | copy-start | bytes 798724
  28.6 5.1 %collective-permute-start.17 = (bf16[33,16,128]{2,1,0:T(8,128)(2,1)S(1)}, bf16[33,16,128]{2,1,0:T(8,128)(2,1)S(1)}, u32[]{:S(2)}, u32[]{:S(2)}) collective-permute-start(bf16[33,16,128]{2,1,0:T(8,128)(2,1)S(1)} %slice.45), channel_id=1, source_target_pairs={{0,4},{1,5},{4,8},{5,9},{8,12},{9,13},{12,14},{13,15},{14,10},{15,... | collective-permute-start | bytes 405512 | tf_op jit(solution)/shard_map/ppermute | solution.py:206
  30.1 14.3 %copy-start.2 = (bf16[65,16,128]{2,1,0:T(8,128)(2,1)}, bf16[65,16,128]{2,1,0:T(8,128)(2,1)S(1)}, u32[]{:S(2)}) copy-start(bf16[65,16,128]{2,1,0:T(8,128)(2,1)S(1)} %collective-permute-done.13.refs_3_) | copy-start | bytes 798724
  30.1 5.1 %collective-permute-start.18 = (bf16[33,16,128]{2,1,0:T(8,128)(2,1)S(1)}, bf16[33,16,128]{2,1,0:T(8,128)(2,1)S(1)}, u32[]{:S(2)}, u32[]{:S(2)}) collective-permute-start(bf16[33,16,128]{2,1,0:T(8,128)(2,1)S(1)} %slice.46), channel_id=1, source_target_pairs={{4,0},{5,1},{8,4},{9,5},{12,8},{13,9},{14,12},{15,13},{10,14},{11,... | collective-permute-start | bytes 405512 | tf_op jit(solution)/shard_map/ppermute | solution.py:206
  33.7 2.9 %copy-start.19 = (bf16[33,16,128]{2,1,0:T(8,128)(2,1)}, bf16[33,16,128]{2,1,0:T(8,128)(2,1)S(1)}, u32[]{:S(2)}) copy-start(bf16[33,16,128]{2,1,0:T(8,128)(2,1)S(1)} %collective-permute-done.17.refs_2_) | copy-start | bytes 405508
  33.7 2.0 %collective-permute-start.19 = (bf16[33,16,128]{2,1,0:T(8,128)(2,1)S(1)}, bf16[33,16,128]{2,1,0:T(8,128)(2,1)S(1)}, u32[]{:S(2)}, u32[]{:S(2)}) collective-permute-start(bf16[33,16,128]{2,1,0:T(8,128)(2,1)S(1)} %collective-permute-done.17.refs_2_), channel_id=1, source_target_pairs={{0,1},{1,0},{2,3},{3,2},{4,5},{5,4},{6,7},{7,6},{8,9},{9,8},{10,11... | collective-permute-start | bytes 405512 | tf_op jit(solution)/shard_map/ppermute | solution.py:206
  35.2 1.4 %copy-start.20 = (bf16[33,16,128]{2,1,0:T(8,128)(2,1)}, bf16[33,16,128]{2,1,0:T(8,128)(2,1)S(1)}, u32[]{:S(2)}) copy-start(bf16[33,16,128]{2,1,0:T(8,128)(2,1)S(1)} %collective-permute-done.18.refs_3_) | copy-start | bytes 405508
  35.2 1.4 %collective-permute-start.20 = (bf16[33,16,128]{2,1,0:T(8,128)(2,1)S(1)}, bf16[33,16,128]{2,1,0:T(8,128)(2,1)S(1)}, u32[]{:S(2)}, u32[]{:S(2)}) collective-permute-start(bf16[33,16,128]{2,1,0:T(8,128)(2,1)S(1)} %collective-permute-done.18.refs_3_), channel_id=1, source_target_pairs={{0,1},{1,0},{2,3},{3,2},{4,5},{5,4},{6,7},{7,6},{8,9},{9,8},{10,11... | collective-permute-start | bytes 405512 | tf_op jit(solution)/shard_map/ppermute | solution.py:206
  35.2 10.0 %collective-permute-start.14 = (bf16[65,16,128]{2,1,0:T(8,128)(2,1)S(1)}, bf16[65,16,128]{2,1,0:T(8,128)(2,1)S(1)}, u32[]{:S(2)}, u32[]{:S(2)}) collective-permute-start(bf16[65,16,128]{2,1,0:T(8,128)(2,1)S(1)} %collective-permute-done.12.refs_2_), channel_id=1, source_target_pairs={{0,1},{1,0},{2,3},{3,2},{4,5},{5,4},{6,7},{7,6},{8,9},{9,8},{10,11... | collective-permute-start | bytes 798728 | tf_op jit(solution)/shard_map/ppermute | solution.py:206
  35.7 9.9 %collective-permute-start.15 = (bf16[65,16,128]{2,1,0:T(8,128)(2,1)S(1)}, bf16[65,16,128]{2,1,0:T(8,128)(2,1)S(1)}, u32[]{:S(2)}, u32[]{:S(2)}) collective-permute-start(bf16[65,16,128]{2,1,0:T(8,128)(2,1)S(1)} %collective-permute-done.13.refs_3_), channel_id=1, source_target_pairs={{0,1},{1,0},{2,3},{3,2},{4,5},{5,4},{6,7},{7,6},{8,9},{9,8},{10,11... | collective-permute-start | bytes 798728 | tf_op jit(solution)/shard_map/ppermute | solution.py:206
  35.7 0.8 copy-start.21
  36.5 0.7 copy-start.22
  44.5 10.5 %copy-start.3 = (f32[64,2048]{1,0:T(8,128)S(1)}, f32[64,2048]{1,0:T(8,128)}, u32[]{:S(2)}) copy-start(f32[64,2048]{1,0:T(8,128)} %get-tuple-element.26) | copy-start | bytes 1572868
  44.5 10.3 %collective-permute-start.21 = (bf16[64,2048]{1,0:T(8,128)(2,1)}, bf16[64,2048]{1,0:T(8,128)(2,1)S(1)}, u32[]{:S(2)}, u32[]{:S(2)}) collective-permute-start(bf16[64,2048]{1,0:T(8,128)(2,1)} %get-tuple-element.27), channel_id=1, source_target_pairs={{0,1},{1,0},{2,3},{3,2},{4,5},{5,4},{6,7},{7,6},{8,9},{9,8},{10,11... | collective-permute-start | bytes 786440 | tf_op jit(solution)/shard_map/ppermute | solution.py:206
  44.7 25.4 %collective-permute-start.4 = (bf16[65,16,128]{2,1,0:T(8,128)(2,1)S(1)}, bf16[65,16,128]{2,1,0:T(8,128)(2,1)}, u32[]{:S(2)}, u32[]{:S(2)}) collective-permute-start(bf16[65,16,128]{2,1,0:T(8,128)(2,1)S(1)} %collective-permute-done.2.refs_2_), channel_id=1, source_target_pairs={{0,1},{1,0},{2,3},{3,2},{4,5},{5,4},{6,7},{7,6},{8,9},{9,8},{10,11... | collective-permute-start | bytes 798728 | tf_op jit(solution)/shard_map/ppermute | solution.py:206
  45.1 25.1 %collective-permute-start.5 = (bf16[65,16,128]{2,1,0:T(8,128)(2,1)S(1)}, bf16[65,16,128]{2,1,0:T(8,128)(2,1)}, u32[]{:S(2)}, u32[]{:S(2)}) collective-permute-start(bf16[65,16,128]{2,1,0:T(8,128)(2,1)S(1)} %collective-permute-done.3.refs_3_), channel_id=1, source_target_pairs={{0,1},{1,0},{2,3},{3,2},{4,5},{5,4},{6,7},{7,6},{8,9},{9,8},{10,11... | collective-permute-start | bytes 798728 | tf_op jit(solution)/shard_map/ppermute | solution.py:206
  45.2 0.7 copy-start.15
  45.2 9.9 %collective-permute-start.10 = (bf16[65,16,128]{2,1,0:T(8,128)(2,1)S(1)}, bf16[65,16,128]{2,1,0:T(8,128)(2,1)S(1)}, u32[]{:S(2)}, u32[]{:S(2)}) collective-permute-start(bf16[65,16,128]{2,1,0:T(8,128)(2,1)S(1)} %collective-permute-done.8.refs_3_), channel_id=1, source_target_pairs={{0,1},{1,0},{2,3},{3,2},{4,5},{5,4},{6,7},{7,6},{8,9},{9,8},{10,11... | collective-permute-start | bytes 798728 | tf_op jit(solution)/shard_map/ppermute | solution.py:206
  45.6 0.7 copy-start.16
  45.6 10.1 %collective-permute-start.9 = (bf16[65,16,128]{2,1,0:T(8,128)(2,1)S(1)}, bf16[65,16,128]{2,1,0:T(8,128)(2,1)S(1)}, u32[]{:S(2)}, u32[]{:S(2)}) collective-permute-start(bf16[65,16,128]{2,1,0:T(8,128)(2,1)S(1)} %collective-permute-done.7.refs_2_), channel_id=1, source_target_pairs={{0,1},{1,0},{2,3},{3,2},{4,5},{5,4},{6,7},{7,6},{8,9},{9,8},{10,11... | collective-permute-start | bytes 798728 | tf_op jit(solution)/shard_map/ppermute | solution.py:206
  54.8 11.1 %collective-permute-start.16 = (bf16[128,2048]{1,0:T(8,128)(2,1)}, bf16[128,2048]{1,0:T(8,128)(2,1)S(1)}, u32[]{:S(2)}, u32[]{:S(2)}) collective-permute-start(bf16[128,2048]{1,0:T(8,128)(2,1)} %get-tuple-element.25), channel_id=1, source_target_pairs={{0,1},{1,0},{2,3},{3,2},{4,5},{5,4},{6,7},{7,6},{8,9},{9,8},{10,11... | collective-permute-start | bytes 1572872 | tf_op jit(solution)/shard_map/ppermute | solution.py:206
  55.1 0.7 copy-start.17
  55.1 11.1 %collective-permute-start.22 = (bf16[32,2048]{1,0:T(8,128)(2,1)S(1)}, bf16[32,2048]{1,0:T(8,128)(2,1)}, u32[]{:S(2)}, u32[]{:S(2)}) collective-permute-start(bf16[32,2048]{1,0:T(8,128)(2,1)S(1)} %get-tuple-element.37), channel_id=1, source_target_pairs={{4,0},{5,1},{8,4},{9,5},{12,8},{13,9},{14,12},{15,13},{10,14},{11,... | collective-permute-start | bytes 393224 | tf_op jit(solution)/shard_map/ppermute | solution.py:206
  55.8 1.6 %copy-start.18 = (bf16[65,16,128]{2,1,0:T(8,128)(2,1)}, bf16[65,16,128]{2,1,0:T(8,128)(2,1)S(1)}, u32[]{:S(2)}) copy-start(bf16[65,16,128]{2,1,0:T(8,128)(2,1)S(1)} %collective-permute-done.9.refs_4_) | copy-start | bytes 798724
  55.8 10.4 %copy-start.8 = (f32[64,2048]{1,0:T(8,128)S(1)}, f32[64,2048]{1,0:T(8,128)}, u32[]{:S(2)}) copy-start(f32[64,2048]{1,0:T(8,128)} %get-tuple-element.24) | copy-start | bytes 1572868
  55.8 10.4 %copy-start.9 = (f32[64,2048]{1,0:T(8,128)S(1)}, f32[64,2048]{1,0:T(8,128)}, u32[]{:S(2)}) copy-start(f32[64,2048]{1,0:T(8,128)} %get-tuple-element.30) | copy-start | bytes 1572868
  55.8 14.3 %copy-start = (bf16[65,16,128]{2,1,0:T(8,128)(2,1)S(1)}, bf16[65,16,128]{2,1,0:T(8,128)(2,1)}, u32[]{:S(2)}) copy-start(bf16[65,16,128]{2,1,0:T(8,128)(2,1)} %pack.1.refs_2_) | copy-start | bytes 798724
  55.8 10.4 %collective-permute-start.26 = (bf16[32,2048]{1,0:T(8,128)(2,1)S(1)}, bf16[32,2048]{1,0:T(8,128)(2,1)}, u32[]{:S(2)}, u32[]{:S(2)}) collective-permute-start(bf16[32,2048]{1,0:T(8,128)(2,1)S(1)} %get-tuple-element.38), channel_id=1, source_target_pairs={{0,4},{1,5},{4,8},{5,9},{8,12},{9,13},{12,14},{13,15},{14,10},{15,... | collective-permute-start | bytes 393224 | tf_op jit(solution)/shard_map/ppermute | solution.py:206
  65.9 13.1 %collective-permute-start.11 = (bf16[128,2048]{1,0:T(8,128)(2,1)}, bf16[128,2048]{1,0:T(8,128)(2,1)S(1)}, u32[]{:S(2)}, u32[]{:S(2)}) collective-permute-start(bf16[128,2048]{1,0:T(8,128)(2,1)} %get-tuple-element.23), channel_id=1, source_target_pairs={{0,1},{1,0},{2,3},{3,2},{4,5},{5,4},{6,7},{7,6},{8,9},{9,8},{10,11... | collective-permute-start | bytes 1572872 | tf_op jit(solution)/shard_map/ppermute | solution.py:206
  68.1 11.1 %collective-permute-start.23 = (bf16[64,2048]{1,0:T(8,128)(2,1)}, bf16[64,2048]{1,0:T(8,128)(2,1)S(1)}, u32[]{:S(2)}, u32[]{:S(2)}) collective-permute-start(bf16[64,2048]{1,0:T(8,128)(2,1)} %get-tuple-element.35), channel_id=1, source_target_pairs={{4,0},{5,1},{8,4},{9,5},{12,8},{13,9},{14,12},{15,13},{10,14},{11,... | collective-permute-start | bytes 786440 | tf_op jit(solution)/shard_map/ppermute | solution.py:206
  68.5 10.7 %copy-start.4 = (f32[64,2048]{1,0:T(8,128)S(1)}, f32[64,2048]{1,0:T(8,128)}, u32[]{:S(2)}) copy-start(f32[64,2048]{1,0:T(8,128)} %get-tuple-element.22) | copy-start | bytes 1572868
  68.5 10.7 %copy-start.5 = (f32[64,2048]{1,0:T(8,128)S(1)}, f32[64,2048]{1,0:T(8,128)}, u32[]{:S(2)}) copy-start(f32[64,2048]{1,0:T(8,128)} %get-tuple-element.29) | copy-start | bytes 1572868
  68.5 10.7 %collective-permute-start.27 = (bf16[64,2048]{1,0:T(8,128)(2,1)S(1)}, bf16[64,2048]{1,0:T(8,128)(2,1)}, u32[]{:S(2)}, u32[]{:S(2)}) collective-permute-start(bf16[64,2048]{1,0:T(8,128)(2,1)S(1)} %get-tuple-element.36), channel_id=1, source_target_pairs={{0,4},{1,5},{4,8},{5,9},{8,12},{9,13},{12,14},{13,15},{14,10},{15,... | collective-permute-start | bytes 786440 | tf_op jit(solution)/shard_map/ppermute | solution.py:206
  70.1 12.4 %collective-permute-start = (bf16[65,16,128]{2,1,0:T(8,128)(2,1)S(1)}, bf16[65,16,128]{2,1,0:T(8,128)(2,1)S(1)}, u32[]{:S(2)}, u32[]{:S(2)}) collective-permute-start(bf16[65,16,128]{2,1,0:T(8,128)(2,1)S(1)} %copy-done), channel_id=1, source_target_pairs={{0,1},{1,0},{2,3},{3,2},{4,5},{5,4},{6,7},{7,6},{8,9},{9,8},{10,11... | collective-permute-start | bytes 798728 | tf_op jit(solution)/shard_map/ppermute | solution.py:206
  78.6 11.8 %collective-permute-start.6 = (bf16[128,2048]{1,0:T(8,128)(2,1)}, bf16[128,2048]{1,0:T(8,128)(2,1)S(1)}, u32[]{:S(2)}, u32[]{:S(2)}) collective-permute-start(bf16[128,2048]{1,0:T(8,128)(2,1)} %get-tuple-element.21), channel_id=1, source_target_pairs={{0,1},{1,0},{2,3},{3,2},{4,5},{5,4},{6,7},{7,6},{8,9},{9,8},{10,11... | collective-permute-start | bytes 1572872 | tf_op jit(solution)/shard_map/ppermute | solution.py:206
  80.4 10.1 %collective-permute-start.24 = (bf16[64,2048]{1,0:T(8,128)(2,1)S(1)}, bf16[64,2048]{1,0:T(8,128)(2,1)S(1)}, u32[]{:S(2)}, u32[]{:S(2)}) collective-permute-start(bf16[64,2048]{1,0:T(8,128)(2,1)S(1)} %get-tuple-element.33), channel_id=1, source_target_pairs={{4,0},{5,1},{8,4},{9,5},{12,8},{13,9},{14,12},{15,13},{10,14},{11,... | collective-permute-start | bytes 786440 | tf_op jit(solution)/shard_map/ppermute | solution.py:206
  80.9 9.7 %copy-start.6 = (f32[64,2048]{1,0:T(8,128)S(1)}, f32[64,2048]{1,0:T(8,128)}, u32[]{:S(2)}) copy-start(f32[64,2048]{1,0:T(8,128)} %get-tuple-element.20) | copy-start | bytes 1572868
  80.9 9.7 %copy-start.7 = (f32[64,2048]{1,0:T(8,128)S(1)}, f32[64,2048]{1,0:T(8,128)}, u32[]{:S(2)}) copy-start(f32[64,2048]{1,0:T(8,128)} %get-tuple-element.28) | copy-start | bytes 1572868
  80.9 9.6 %collective-permute-start.28 = (bf16[64,2048]{1,0:T(8,128)(2,1)S(1)}, bf16[64,2048]{1,0:T(8,128)(2,1)S(1)}, u32[]{:S(2)}, u32[]{:S(2)}) collective-permute-start(bf16[64,2048]{1,0:T(8,128)(2,1)S(1)} %get-tuple-element.34), channel_id=1, source_target_pairs={{0,4},{1,5},{4,8},{5,9},{8,12},{9,13},{12,14},{13,15},{14,10},{15,... | collective-permute-start | bytes 786440 | tf_op jit(solution)/shard_map/ppermute | solution.py:206
  82.5 0.7 copy-start.10
  90.4 2.5 %collective-permute-start.1 = (bf16[64,2048]{1,0:T(8,128)(2,1)}, bf16[64,2048]{1,0:T(8,128)(2,1)S(1)}, u32[]{:S(2)}, u32[]{:S(2)}) collective-permute-start(bf16[64,2048]{1,0:T(8,128)(2,1)} %get-tuple-element.19), channel_id=1, source_target_pairs={{0,1},{1,0},{2,3},{3,2},{4,5},{5,4},{6,7},{7,6},{8,9},{9,8},{10,11... | collective-permute-start | bytes 786440 | tf_op jit(solution)/shard_map/ppermute | solution.py:206
  90.8 8.8 %collective-permute-start.25 = (bf16[64,2048]{1,0:T(8,128)(2,1)S(1)}, bf16[64,2048]{1,0:T(8,128)(2,1)S(1)}, u32[]{:S(2)}, u32[]{:S(2)}) collective-permute-start(bf16[64,2048]{1,0:T(8,128)(2,1)S(1)} %get-tuple-element.31), channel_id=1, source_target_pairs={{4,0},{5,1},{8,4},{9,5},{12,8},{13,9},{14,12},{15,13},{10,14},{11,... | collective-permute-start | bytes 786440 | tf_op jit(solution)/shard_map/ppermute | solution.py:206
  91.3 8.4 %collective-permute-start.29 = (bf16[64,2048]{1,0:T(8,128)(2,1)S(1)}, bf16[64,2048]{1,0:T(8,128)(2,1)S(1)}, u32[]{:S(2)}, u32[]{:S(2)}) collective-permute-start(bf16[64,2048]{1,0:T(8,128)(2,1)S(1)} %get-tuple-element.32), channel_id=1, source_target_pairs={{0,4},{1,5},{4,8},{5,9},{8,12},{9,13},{12,14},{13,15},{14,10},{15,... | collective-permute-start | bytes 786440 | tf_op jit(solution)/shard_map/ppermute | solution.py:206

commit v2 on v1

v2 whole, which is shorter than its diff:
```python
import functools

import jax
import jax.numpy as jnp
from jax import lax
from jax.experimental import pallas as pl
from jax.experimental.pallas import tpu as pltpu
from jax.sharding import PartitionSpec as P

LANES = 128
SUBS = 16
THIRD = 3
VMEM = pl.BlockSpec(memory_space=pltpu.VMEM)
SMEM = pl.BlockSpec(memory_space=pltpu.SMEM)
HBM = pl.BlockSpec(memory_space=pltpu.HBM)
VMEM_BYTES = 24 * 1024 * 1024


class Packing:
    def __init__(self, local_tokens, feature, experts):
        self.local_tokens = local_tokens
        self.feature = feature
        self.experts = experts
        self.cols = feature // LANES
        self.groups = local_tokens // SUBS
        self.per_tile = max(1, LANES // (2 * experts))
        self.gate_tiles = pl.cdiv(self.groups, self.per_tile)
        self.token_tiles = self.groups * self.cols
        self.tiles = self.token_tiles + self.gate_tiles


def pack_body(pk, capacity, devices, tokens_ref, ids_ref, gates_ref, spare_ref, out_ref):
    for group in range(pk.groups):
        for col in range(pk.cols):
            out_ref[group * pk.cols + col] = tokens_ref[
                group * SUBS : (group + 1) * SUBS, col * LANES : (col + 1) * LANES
            ]
    rows = pk.local_tokens
    lane = lax.broadcasted_iota(jnp.int32, (1, LANES), 1)
    expert = lax.rem(lane, pk.experts)
    ids = ids_ref[...].T
    gates = gates_ref[...].T
    chosen = jnp.zeros((rows, LANES), jnp.float32)
    gate = jnp.zeros((rows, LANES), jnp.float32)
    for k in range(ids.shape[1]):
        match = ids[:, k : k + 1] == expert
        chosen = jnp.where(match, 1.0, chosen)
        gate = jnp.where(match, gates[:, k : k + 1], gate)
    before = (
        lax.broadcasted_iota(jnp.int32, (rows, rows), 0)
        > lax.broadcasted_iota(jnp.int32, (rows, rows), 1)
    ).astype(jnp.float32).astype(jnp.bfloat16)
    arrival = jnp.dot(before, chosen.astype(jnp.bfloat16), preferred_element_type=jnp.float32)
    named = jnp.zeros((1, LANES), jnp.int32)
    for device in range(devices):
        named = named + (expert == spare_ref[device]).astype(jnp.int32)
    count = jnp.ones((1, LANES), jnp.int32)
    for copy in range(1, devices // THIRD + 1):
        count = count + (named >= THIRD * copy).astype(jnp.int32)
    gate = jnp.where(arrival < (count * capacity).astype(jnp.float32), gate, 0.0)
    high = gate.astype(jnp.bfloat16).astype(jnp.float32)
    low = gate - high
    value = jnp.where(lax.rem(lane // pk.experts, 2) == 0, high, low)
    slot = lane // (2 * pk.experts)
    for index in range(pk.gate_tiles):
        tile = jnp.zeros((SUBS, LANES), jnp.float32)
        for part in range(pk.per_tile):
            group = index * pk.per_tile + part
            if group < pk.groups:
                tile = jnp.where(slot == part, value[group * SUBS : (group + 1) * SUBS], tile)
        out_ref[pk.token_tiles + index] = tile.astype(jnp.bfloat16)


def pack(pk, capacity, devices, tokens, ids, gates, spare):
    return pl.pallas_call(
        functools.partial(pack_body, pk, capacity, devices),
        out_shape=jax.ShapeDtypeStruct((pk.tiles, SUBS, LANES), jnp.bfloat16),
        in_specs=[VMEM, VMEM, VMEM, SMEM],
        out_specs=VMEM,
        compiler_params=pltpu.CompilerParams(vmem_limit_bytes=VMEM_BYTES),
        name="pack",
    )(tokens, ids.T, gates.T, spare)


def gather_rows(pk, buffers, x_ref):
    for index, buffer in enumerate(buffers):
        for group in range(pk.groups):
            row = index * pk.local_tokens + group * SUBS
            for col in range(pk.cols):
                x_ref[row : row + SUBS, col * LANES : (col + 1) * LANES] = buffer[
                    group * pk.cols + col
                ]


def activate(gate, up):
    return (gate / (1.0 + jnp.exp(-gate)) * up).astype(jnp.bfloat16)


def down(hidden, weight):
    return lax.dot_general(
        hidden, weight, (((1,), (1,)), ((), ())), preferred_element_type=jnp.float32
    )


def store_scaled(pk, home_ref, me_ref, buffers, answers, out_refs):
    mine = jnp.int32(0)
    for e in range(pk.experts):
        mine = jnp.where(home_ref[e] == me_ref[0], e, mine)
    lane = lax.broadcasted_iota(jnp.int32, (1, LANES), 1)
    scales = []
    for buffer in buffers:
        for group in range(pk.groups):
            place = (group % pk.per_tile) * 2 * pk.experts + mine
            wanted = (lane == place) | (lane == place + pk.experts)
            table = buffer[pk.token_tiles + group // pk.per_tile].astype(jnp.float32)
            scales.append(jnp.sum(jnp.where(wanted, table, 0.0), axis=1, keepdims=True))
    row = 0
    for out_ref in out_refs:
        for start in range(0, out_ref.shape[0], SUBS):
            scaled = answers[row : row + SUBS, :] * scales[row // SUBS]
            out_ref[start : start + SUBS, :] = scaled.astype(out_ref.dtype)
            row += SUBS


def first_body(pk, width, home_ref, me_ref, own_ref, other_ref, weights_ref, *rest):
    keep_ref, give_ref, kept_ref, x_ref, acc_ref, sems = rest
    block = width // THIRD
    copies = []
    for j in range(THIRD):
        for part in range(THIRD):
            columns = slice(part * width + j * block, part * width + (j + 1) * block)
            copy = pltpu.make_async_copy(
                weights_ref.at[0, :, columns], kept_ref.at[:, columns], sems.at[j, part]
            )
            copy.start()
            copies.append(copy)
    gather_rows(pk, [own_ref, other_ref], x_ref)
    rows = x_ref[...]
    for j in range(THIRD):
        for part in range(THIRD):
            copies[j * THIRD + part].wait()
        gate = jnp.dot(
            rows, kept_ref[:, j * block : (j + 1) * block], preferred_element_type=jnp.float32
        )
        up = jnp.dot(
            rows,
            kept_ref[:, width + j * block : width + (j + 1) * block],
            preferred_element_type=jnp.float32,
        )
        part = down(
            activate(gate, up), kept_ref[:, 2 * width + j * block : 2 * width + (j + 1) * block]
        )
        if j == 0:
            acc_ref[...] = part
        else:
            acc_ref[...] += part
    store_scaled(pk, home_ref, me_ref, [own_ref, other_ref], acc_ref, [keep_ref, give_ref])


def first_chunk(pk, weights, home, me, own, other):
    width = weights.shape[2] // 4
    rows, feature = pk.local_tokens, pk.feature
    return pl.pallas_call(
        functools.partial(first_body, pk, width),
        out_shape=[
            jax.ShapeDtypeStruct((rows, feature), jnp.float32),
            jax.ShapeDtypeStruct((rows, feature), jnp.bfloat16),
            pltpu.VMEM((feature, THIRD * width), jnp.bfloat16),
        ],
        in_specs=[SMEM, SMEM, VMEM, VMEM, HBM],
        out_specs=[VMEM, VMEM, VMEM],
        scratch_shapes=[
            pltpu.VMEM((2 * rows, feature), jnp.bfloat16),
            pltpu.VMEM((2 * rows, feature), jnp.float32),
            pltpu.SemaphoreType.DMA((THIRD, THIRD)),
        ],
        compiler_params=pltpu.CompilerParams(vmem_limit_bytes=VMEM_BYTES),
        cost_estimate=pl.CostEstimate(
            flops=4 * rows * feature * 3 * width,
            transcendentals=2 * rows * width,
            bytes_accessed=2 * feature * 3 * width,
        ),
        name="first_chunk",
    )(home, me, own, other, pltpu.with_memory_space_constraint(weights, pltpu.HBM))


def chunk_body(pk, width, count, *refs):
    home_ref, me_ref = refs[:2]
    buffers = refs[2 : 2 + count]
    weights_ref = refs[2 + count]
    out_refs = refs[3 + count : -1]
    x_ref = refs[-1]
    gather_rows(pk, buffers, x_ref)
    rows = x_ref[...]
    gate = jnp.dot(rows, weights_ref[:, :width], preferred_element_type=jnp.float32)
    up = jnp.dot(rows, weights_ref[:, width : 2 * width], preferred_element_type=jnp.float32)
    answers = down(activate(gate, up), weights_ref[:, 2 * width :])
    store_scaled(pk, home_ref, me_ref, buffers, answers, out_refs)


def chunk(pk, weights, home, me, own, crossed):
    width = weights.shape[1] // THIRD
    rows, feature = pk.local_tokens, pk.feature
    buffers = own + crossed
    total = rows * len(buffers)
    return pl.pallas_call(
        functools.partial(chunk_body, pk, width, len(buffers)),
        out_shape=[jax.ShapeDtypeStruct((rows, feature), jnp.float32) for _ in own]
        + [jax.ShapeDtypeStruct((rows * len(crossed), feature), jnp.bfloat16)],
        in_specs=[SMEM, SMEM] + [VMEM] * (len(buffers) + 1),
        out_specs=[VMEM] * (len(own) + 1),
        scratch_shapes=[pltpu.VMEM((total, feature), jnp.bfloat16)],
        compiler_params=pltpu.CompilerParams(vmem_limit_bytes=VMEM_BYTES),
        cost_estimate=pl.CostEstimate(
            flops=2 * total * feature * 3 * width,
            transcendentals=total * width,
            bytes_accessed=2 * feature * 3 * width,
        ),
        name="chunk",
    )(home, me, *buffers, weights)


def shards(tokens, expert_ids, gate_values, expert_weights, home_slot, spare_expert):
    devices = lax.axis_size("ep")
    local_tokens, feature = tokens.shape
    capacity = local_tokens * expert_ids.shape[1] // devices
    pk = Packing(local_tokens, feature, home_slot.shape[0])
    chips = devices // 2
    far = chips // 2
    ring = list(range(0, chips, 2)) + list(range(chips - 1, 0, -2))

    def near(i, core):
        return 2 * ring[(i + (1 if core == 0 else -1)) % chips]

    seats = [(i, core) for i in range(chips) for core in range(2)]
    straight = [(2 * ring[i] + core, near(i, core) + core) for i, core in seats]
    crossing = [(2 * ring[i] + 1 - core, near(i, core) + core) for i, core in seats]
    straight_back = [(t, s) for s, t in straight]
    crossing_back = [(t, s) for s, t in crossing]
    pair = [(d, d ^ 1) for d in range(devices)]
    wire = jnp.bfloat16 if chips <= 8 else jnp.float32

    def send(x, where):
        return lax.ppermute(x, "ep", where)

    me = lax.axis_index("ep").astype(jnp.int32).reshape(1)
    packed = pack(pk, capacity, devices, tokens, expert_ids, gate_values, spare_expert)

    keep, gave = {}, {}
    a, b = send(packed, straight), send(packed, crossing)
    other = send(packed, pair)
    keep[0], give, weights = first_chunk(
        pk, expert_weights, home_slot, me, packed, other
    )
    gave[0] = send(give, pair)
    for r in range(1, far):
        xa, xb = send(a, pair), send(b, pair)
        keep_a, keep_b, give = chunk(pk, weights, home_slot, me, [a, b], [xa, xb])
        keep[r] = (keep_a, keep_b)
        gave[r] = send(give, pair)
        a = send(a, straight)
        if r + 1 < far:
            b = send(b, straight)
    xa = send(a, pair)
    keep_a, give = chunk(pk, weights, home_slot, me, [a], [xa])
    gave[far] = send(give, pair)

    a = (keep_a + gave[far].astype(jnp.float32)).astype(wire)
    a = send(a, straight_back).astype(jnp.float32)
    b = jnp.zeros((), jnp.float32)
    for r in range(far - 1, 0, -1):
        keep_a, keep_b = keep[r]
        a = (a + keep_a + gave[r][:local_tokens].astype(jnp.float32)).astype(wire)
        b = (b + keep_b + gave[r][local_tokens:].astype(jnp.float32)).astype(wire)
        a = send(a, straight_back).astype(jnp.float32)
        b = send(b, straight_back if r > 1 else crossing_back).astype(jnp.float32)
    total = keep[0] + gave[0].astype(jnp.float32) + a + b
    return total.astype(jnp.bfloat16)


def solution(mesh):
    in_specs = (
        P(("groups", "ep"), None),
        P(("groups", "ep"), None),
        P(("groups", "ep"), None),
        P(("groups", "ep"), None, None),
        P("groups"),
        P("groups"),
    )
    out_specs = P(("groups", "ep"), None)

    return jax.shard_map(shards, mesh=mesh, in_specs=in_specs, out_specs=out_specs, check_vma=False)
```

time: 102 us -> 84.3 us (0.83)
  the two profiles are of different devices: /device:TPU:0 before, /device:TPU:13 now
where the time goes in v2:
time: 84.3 us; the launch traced here: 84 us
  starting transfers between devices  36.1 us (43%)
  waiting for transfers between devices  24 us (28%)
  Pallas kernels  18.7 us (22%)
  local copies, waits for them, and re-layouts  3.65 us (4%)
  other arithmetic  1.45 us (2%)
    ppermute x27, starting transfers between devices, send(): return lax.ppermute(x, 'ep', where)  36.1 us
    ppermute x27, waiting for transfers between devices, send(): return lax.ppermute(x, 'ep', where)  24 us
    pallas_call x4, Pallas kernels, chunk(): pl.pallas_call(functools.partial(chunk_body, pk, width, len(buffers)), ou...  12.4 us
    pallas_call x1, Pallas kernels, first_chunk(): pl.pallas_call(functools.partial(first_body, pk, width), out_shape=[jax.S...  5.31 us
    unnamed x12, local copies, waits for them, and re-layouts  3.65 us
  transfers between devices with their start and end apart: 27, of which 10 were waited for; matrix products, arithmetic and copies ran while one was open for 1% of the time, Pallas kernels for 21%

profile of v2, /device:TPU:13, one launch (start us, length us, event | category | flops | bytes accessed | tf_op | source)
XLA Modules:
  0.0 84.0 jit_solution(2247523184865062680)
XLA Ops:
  0.0 1.0 %copy-done = bf16[64,2048]{1,0:T(8,128)(2,1)S(1)} copy-done((bf16[64,2048]{1,0:T(8,128)(2,1)S(1)}, bf16[64,2048]{1,0:T(8,128)(2,1)}, u32[]{:S(2)}) %copy-start) | copy-done | bytes 262168
  1.0 0.7 copy-done.3
  1.7 0.7 copy-done.4
  2.3 0.7 copy-done.5
  3.0 1.0 %pack.1.own_ref = bf16[65,16,128]{2,1,0:T(8,128)(2,1)S(1)} custom-call(bf16[64,2048]{1,0:T(8,128)(2,1)S(1)} %copy-done, s32[8,64]{1,0:T(8,128)S(1)} %bitcast.3, f32[8,64]{1,0:T(8,128)S(1)} %bitcast.4, s32[16]{0:T(128)S(1)} %copy-done.5), custom_call_target="tpu_custom_call" | custom-call | tf_op jit(solution)/shard_map/pack/pallas_call | solution.py:75
  4.0 1.3 %collective-permute-start.2 = (bf16[65,16,128]{2,1,0:T(8,128)(2,1)S(1)}, bf16[65,16,128]{2,1,0:T(8,128)(2,1)S(1)}, u32[]{:S(2)}, u32[]{:S(2)}) collective-permute-start(bf16[65,16,128]{2,1,0:T(8,128)(2,1)S(1)} %pack.1.own_ref), channel_id=1, source_target_pairs={{0,4},{1,3},{4,8},{5,1},{8,12},{9,5},{12,14},{13,9},{14,10},{15,13... | collective-permute-start | bytes 798728 | tf_op jit(solution)/shard_map/ppermute | solution.py:244
  5.3 4.3 %collective-permute-done.2.refs_2_ = bf16[65,16,128]{2,1,0:T(8,128)(2,1)S(1)} collective-permute-done((bf16[65,16,128]{2,1,0:T(8,128)(2,1)S(1)}, bf16[65,16,128]{2,1,0:T(8,128)(2,1)S(1)}, u32[]{:S(2)}, u32[]{:S(2)}) %collective-permute-start.2) | collective-permute-done | bytes 266272 | tf_op jit(solution)/shard_map/ppermute | solution.py:244
  9.6 1.3 %collective-permute-start.3 = (bf16[65,16,128]{2,1,0:T(8,128)(2,1)S(1)}, bf16[65,16,128]{2,1,0:T(8,128)(2,1)S(1)}, u32[]{:S(2)}, u32[]{:S(2)}) collective-permute-start(bf16[65,16,128]{2,1,0:T(8,128)(2,1)S(1)} %collective-permute-done.2.refs_2_), channel_id=1, source_target_pairs={{0,4},{1,3},{4,8},{5,1},{8,12},{9,5},{12,14},{13,9},{14,10},{15,13... | collective-permute-start | bytes 798728 | tf_op jit(solution)/shard_map/ppermute | solution.py:244
  10.9 0.3 collective-permute-start.9
  11.2 4.9 %collective-permute-done.3.refs_2_ = bf16[65,16,128]{2,1,0:T(8,128)(2,1)S(1)} collective-permute-done((bf16[65,16,128]{2,1,0:T(8,128)(2,1)S(1)}, bf16[65,16,128]{2,1,0:T(8,128)(2,1)S(1)}, u32[]{:S(2)}, u32[]{:S(2)}) %collective-permute-start.3) | collective-permute-done | bytes 266272 | tf_op jit(solution)/shard_map/ppermute | solution.py:244
  16.1 1.4 %collective-permute-start.4 = (bf16[65,16,128]{2,1,0:T(8,128)(2,1)S(1)}, bf16[65,16,128]{2,1,0:T(8,128)(2,1)S(1)}, u32[]{:S(2)}, u32[]{:S(2)}) collective-permute-start(bf16[65,16,128]{2,1,0:T(8,128)(2,1)S(1)} %collective-permute-done.3.refs_2_), channel_id=1, source_target_pairs={{0,4},{1,3},{4,8},{5,1},{8,12},{9,5},{12,14},{13,9},{14,10},{15,13... | collective-permute-start | bytes 798728 | tf_op jit(solution)/shard_map/ppermute | solution.py:244
  17.5 0.5 collective-permute-done.9.refs_3_
  18.0 1.7 %collective-permute-start.10 = (bf16[65,16,128]{2,1,0:T(8,128)(2,1)S(1)}, bf16[65,16,128]{2,1,0:T(8,128)(2,1)S(1)}, u32[]{:S(2)}, u32[]{:S(2)}) collective-permute-start(bf16[65,16,128]{2,1,0:T(8,128)(2,1)S(1)} %collective-permute-done.9.refs_3_), channel_id=1, source_target_pairs={{0,4},{1,3},{4,8},{5,1},{8,12},{9,5},{12,14},{13,9},{14,10},{15,13... | collective-permute-start | bytes 798728 | tf_op jit(solution)/shard_map/ppermute | solution.py:244
  19.7 1.7 %collective-permute-done.4.refs_2_ = bf16[65,16,128]{2,1,0:T(8,128)(2,1)S(1)} collective-permute-done((bf16[65,16,128]{2,1,0:T(8,128)(2,1)S(1)}, bf16[65,16,128]{2,1,0:T(8,128)(2,1)S(1)}, u32[]{:S(2)}, u32[]{:S(2)}) %collective-permute-start.4) | collective-permute-done | bytes 266272 | tf_op jit(solution)/shard_map/ppermute | solution.py:244
  21.4 1.7 %collective-permute-start.5 = (bf16[65,16,128]{2,1,0:T(8,128)(2,1)S(1)}, bf16[65,16,128]{2,1,0:T(8,128)(2,1)S(1)}, u32[]{:S(2)}, u32[]{:S(2)}) collective-permute-start(bf16[65,16,128]{2,1,0:T(8,128)(2,1)S(1)} %collective-permute-done.4.refs_2_), channel_id=1, source_target_pairs={{0,4},{1,3},{4,8},{5,1},{8,12},{9,5},{12,14},{13,9},{14,10},{15,13... | collective-permute-start | bytes 798728 | tf_op jit(solution)/shard_map/ppermute | solution.py:244
  23.1 1.4 %collective-permute-done.10.refs_3_ = bf16[65,16,128]{2,1,0:T(8,128)(2,1)S(1)} collective-permute-done((bf16[65,16,128]{2,1,0:T(8,128)(2,1)S(1)}, bf16[65,16,128]{2,1,0:T(8,128)(2,1)S(1)}, u32[]{:S(2)}, u32[]{:S(2)}) %collective-permute-start.10) | collective-permute-done | bytes 266272 | tf_op jit(solution)/shard_map/ppermute | solution.py:244
  24.5 1.4 %collective-permute-start.11 = (bf16[65,16,128]{2,1,0:T(8,128)(2,1)S(1)}, bf16[65,16,128]{2,1,0:T(8,128)(2,1)S(1)}, u32[]{:S(2)}, u32[]{:S(2)}) collective-permute-start(bf16[65,16,128]{2,1,0:T(8,128)(2,1)S(1)} %collective-permute-done.10.refs_3_), channel_id=1, source_target_pairs={{0,4},{1,3},{4,8},{5,1},{8,12},{9,5},{12,14},{13,9},{14,10},{15,13... | collective-permute-start | bytes 798728 | tf_op jit(solution)/shard_map/ppermute | solution.py:244
  25.9 3.6 %collective-permute-start = (bf16[65,16,128]{2,1,0:T(8,128)(2,1)S(1)}, bf16[65,16,128]{2,1,0:T(8,128)(2,1)S(1)}, u32[]{:S(2)}, u32[]{:S(2)}) collective-permute-start(bf16[65,16,128]{2,1,0:T(8,128)(2,1)S(1)} %pack.1.own_ref), channel_id=1, source_target_pairs={{0,1},{1,0},{2,3},{3,2},{4,5},{5,4},{6,7},{7,6},{8,9},{9,8},{10,11... | collective-permute-start | bytes 798728 | tf_op jit(solution)/shard_map/ppermute | solution.py:244
  29.5 0.0 collective-permute-done.5.refs_2_
  29.5 3.6 %collective-permute-start.6 = (bf16[65,16,128]{2,1,0:T(8,128)(2,1)S(1)}, bf16[65,16,128]{2,1,0:T(8,128)(2,1)S(1)}, u32[]{:S(2)}, u32[]{:S(2)}) collective-permute-start(bf16[65,16,128]{2,1,0:T(8,128)(2,1)S(1)} %collective-permute-done.5.refs_2_), channel_id=1, source_target_pairs={{0,1},{1,0},{2,3},{3,2},{4,5},{5,4},{6,7},{7,6},{8,9},{9,8},{10,11... | collective-permute-start | bytes 798728 | tf_op jit(solution)/shard_map/ppermute | solution.py:244
  33.1 0.0 collective-permute-start.12
  33.1 0.0 collective-permute-done.11.refs_3_
  33.1 2.8 %collective-permute-start.13 = (bf16[65,16,128]{2,1,0:T(8,128)(2,1)S(1)}, bf16[65,16,128]{2,1,0:T(8,128)(2,1)S(1)}, u32[]{:S(2)}, u32[]{:S(2)}) collective-permute-start(bf16[65,16,128]{2,1,0:T(8,128)(2,1)S(1)} %collective-permute-done.11.refs_3_), channel_id=1, source_target_pairs={{0,1},{1,0},{2,3},{3,2},{4,5},{5,4},{6,7},{7,6},{8,9},{9,8},{10,11... | collective-permute-start | bytes 798728 | tf_op jit(solution)/shard_map/ppermute | solution.py:244
  35.9 0.0 collective-permute-done.other_ref
  36.0 0.7 copy-done.1
  36.6 5.3 %first_chunk.1 = (f32[64,2048]{1,0:T(8,128)S(1)}, bf16[64,2048]{1,0:T(8,128)(2,1)S(1)}, bf16[2048,2304]{1,0:T(8,128)(2,1)S(1)}) custom-call(s32[16]{0:T(128)S(1)} %copy-done.1, s32[1]{0:T(128)} %bitcast.me_ref.refs_1_, bf16[65,16,128]{2,1,0:T(8,128)(2,1)S(1)} %pack.1.own_ref, bf16[65,16,128]{2,1,0:T(8,128)(2,1)S(1)} %collective-permute-done.other_ref, ...), custom_call_target="tpu_custom_call" | custom-call | flops 1207959552 | bytes 9437184 | tf_op jit(solution)/shard_map/first_chunk/pallas_call | solution.py:163
  41.9 0.0 collective-permute-done.6.refs_3_
  41.9 2.6 %chunk.4 = (f32[64,2048]{1,0:T(8,128)S(1)}, bf16[64,2048]{1,0:T(8,128)(2,1)S(1)}) custom-call(s32[16]{0:T(128)S(1)} %copy-done.2, s32[1]{0:T(128)} %bitcast.me_ref.refs_1_, bf16[65,16,128]{2,1,0:T(8,128)(2,1)S(1)} %collective-permute-done.5.refs_2_, bf16[65,16,128]{2,1,0:T(8,128)(2,1)S(1)} %collective-permute-done.6.refs_3_, ...), custom_call_target="tpu_custom_call" | custom-call | flops 1207959552 | bytes 9437184 | tf_op jit(solution)/shard_map/chunk/pallas_call | solution.py:206
  44.6 0.1 collective-permute-start.7
  44.6 0.5 collective-permute-start.16
  45.1 0.1 collective-permute-start.17
  45.2 0.0 collective-permute-done.12.refs_4_
  45.2 0.0 collective-permute-done.13.refs_5_
  45.2 3.3 %chunk.5 = (f32[64,2048]{1,0:T(8,128)S(1)}, f32[64,2048]{1,0:T(8,128)S(1)}, bf16[128,2048]{1,0:T(8,128)(2,1)S(1)}) custom-call(s32[16]{0:T(128)S(1)} %copy-done.2, s32[1]{0:T(128)} %bitcast.me_ref.refs_1_, bf16[65,16,128]{2,1,0:T(8,128)(2,1)S(1)} %collective-permute-done.4.refs_2_, bf16[65,16,128]{2,1,0:T(8,128)(2,1)S(1)} %collective-permute-done.11.refs_3_, ...), custom_call_target="tpu_custom_call" | custom-call | flops 2415919104 | bytes 9437184 | tf_op jit(solution)/shard_map/chunk/pallas_call | solution.py:206
  48.5 0.5 collective-permute-start.14
  49.0 0.0 collective-permute-done.7
  49.0 0.1 add_convert_fusion.7
  49.1 0.1 collective-permute-start.8
  49.1 1.6 %collective-permute-start.20 = (bf16[65,16,128]{2,1,0:T(8,128)(2,1)S(1)}, bf16[65,16,128]{2,1,0:T(8,128)(2,1)S(1)}, u32[]{:S(2)}, u32[]{:S(2)}) collective-permute-start(bf16[65,16,128]{2,1,0:T(8,128)(2,1)S(1)} %collective-permute-done.2.refs_2_), channel_id=1, source_target_pairs={{0,1},{1,0},{2,3},{3,2},{4,5},{5,4},{6,7},{7,6},{8,9},{9,8},{10,11... | collective-permute-start | bytes 798728 | tf_op jit(solution)/shard_map/ppermute | solution.py:244
  50.8 0.0 collective-permute-done.16.refs_4_
  50.8 0.0 collective-permute-start.21
  50.8 3.3 %chunk.6 = (f32[64,2048]{1,0:T(8,128)S(1)}, f32[64,2048]{1,0:T(8,128)S(1)}, bf16[128,2048]{1,0:T(8,128)(2,1)S(1)}) custom-call(s32[16]{0:T(128)S(1)} %copy-done.2, s32[1]{0:T(128)} %bitcast.me_ref.refs_1_, bf16[65,16,128]{2,1,0:T(8,128)(2,1)S(1)} %collective-permute-done.3.refs_2_, bf16[65,16,128]{2,1,0:T(8,128)(2,1)S(1)} %collective-permute-done.10.refs_3_, ...), custom_call_target="tpu_custom_call" | custom-call | flops 2415919104 | bytes 9437184 | tf_op jit(solution)/shard_map/chunk/pallas_call | solution.py:206
  54.1 0.6 collective-permute-start.18
  54.6 0.0 collective-permute-done.14
  54.6 0.0 collective-permute-done.8
  54.7 0.2 add_convert_fusion.6
  54.8 0.2 collective-permute-start.15
  55.0 0.2 collective-permute-start.24
  55.3 3.3 %chunk.7 = (f32[64,2048]{1,0:T(8,128)S(1)}, f32[64,2048]{1,0:T(8,128)S(1)}, bf16[128,2048]{1,0:T(8,128)(2,1)S(1)}) custom-call(s32[16]{0:T(128)S(1)} %copy-done.2, s32[1]{0:T(128)} %bitcast.me_ref.refs_1_, bf16[65,16,128]{2,1,0:T(8,128)(2,1)S(1)} %collective-permute-done.2.refs_2_, bf16[65,16,128]{2,1,0:T(8,128)(2,1)S(1)} %collective-permute-done.9.refs_3_, ...), custom_call_target="tpu_custom_call" | custom-call | flops 2415919104 | bytes 9437184 | tf_op jit(solution)/shard_map/chunk/pallas_call | solution.py:206
  58.6 3.7 %collective-permute-start.22 = (bf16[128,2048]{1,0:T(8,128)(2,1)S(1)}, bf16[128,2048]{1,0:T(8,128)(2,1)S(1)}, u32[]{:S(2)}, u32[]{:S(2)}) collective-permute-start(bf16[128,2048]{1,0:T(8,128)(2,1)S(1)} %get-tuple-element.29), channel_id=1, source_target_pairs={{0,1},{1,0},{2,3},{3,2},{4,5},{5,4},{6,7},{7,6},{8,9},{9,8},{10,11... | collective-permute-start | bytes 1572872 | tf_op jit(solution)/shard_map/ppermute | solution.py:244
  62.3 0.9 %collective-permute-done.24 = bf16[64,2048]{1,0:T(8,128)(2,1)S(1)} collective-permute-done((bf16[64,2048]{1,0:T(8,128)(2,1)S(1)}, bf16[64,2048]{1,0:T(8,128)(2,1)S(1)}, u32[]{:S(2)}, u32[]{:S(2)}) %collective-permute-start.24) | collective-permute-done | bytes 262176 | tf_op jit(solution)/shard_map/ppermute | solution.py:244
  63.2 0.2 add_convert_fusion.5
  63.4 0.2 collective-permute-start.19
  63.6 0.1 collective-permute-start.25
  63.7 4.7 %collective-permute-start.1 = (bf16[64,2048]{1,0:T(8,128)(2,1)S(1)}, bf16[64,2048]{1,0:T(8,128)(2,1)S(1)}, u32[]{:S(2)}, u32[]{:S(2)}) collective-permute-start(bf16[64,2048]{1,0:T(8,128)(2,1)S(1)} %get-tuple-element.20), channel_id=1, source_target_pairs={{0,1},{1,0},{2,3},{3,2},{4,5},{5,4},{6,7},{7,6},{8,9},{9,8},{10,11... | collective-permute-start | bytes 786440 | tf_op jit(solution)/shard_map/ppermute | solution.py:244
  68.4 0.0 collective-permute-done.22
  68.4 0.6 collective-permute-done.19
  69.0 2.8 %collective-permute-done.25 = bf16[64,2048]{1,0:T(8,128)(2,1)S(1)} collective-permute-done((bf16[64,2048]{1,0:T(8,128)(2,1)S(1)}, bf16[64,2048]{1,0:T(8,128)(2,1)S(1)}, u32[]{:S(2)}, u32[]{:S(2)}) %collective-permute-start.25) | collective-permute-done | bytes 262176 | tf_op jit(solution)/shard_map/ppermute | solution.py:244
  71.8 0.2 add_convert_fusion.4
  72.0 0.2 collective-permute-start.23
  72.2 4.1 %collective-permute-start.26 = (bf16[64,2048]{1,0:T(8,128)(2,1)S(1)}, bf16[64,2048]{1,0:T(8,128)(2,1)S(1)}, u32[]{:S(2)}, u32[]{:S(2)}) collective-permute-start(bf16[64,2048]{1,0:T(8,128)(2,1)S(1)} %get-tuple-element.34), channel_id=1, source_target_pairs={{4,1},{3,0},{8,5},{1,4},{12,9},{5,8},{14,13},{9,12},{10,15},{13,14... | collective-permute-start | bytes 786440 | tf_op jit(solution)/shard_map/ppermute | solution.py:244
  76.3 1.0 %collective-permute-done.23 = bf16[64,2048]{1,0:T(8,128)(2,1)S(1)} collective-permute-done((bf16[64,2048]{1,0:T(8,128)(2,1)S(1)}, bf16[64,2048]{1,0:T(8,128)(2,1)S(1)}, u32[]{:S(2)}, u32[]{:S(2)}) %collective-permute-start.23) | collective-permute-done | bytes 262176 | tf_op jit(solution)/shard_map/ppermute | solution.py:244
  77.3 5.9 %collective-permute-done.26 = bf16[64,2048]{1,0:T(8,128)(2,1)S(1)} collective-permute-done((bf16[64,2048]{1,0:T(8,128)(2,1)S(1)}, bf16[64,2048]{1,0:T(8,128)(2,1)S(1)}, u32[]{:S(2)}, u32[]{:S(2)}) %collective-permute-start.26) | collective-permute-done | bytes 262176 | tf_op jit(solution)/shard_map/ppermute | solution.py:244
  83.2 0.8 add_convert_fusion
  (13 shorter events, 0.0 us)
Async XLA Ops:
  0.0 41.9 %copy-start.2 = (s32[16]{0:T(128)S(1)}, s32[16]{0:T(128)}, u32[]{:S(2)}) copy-start(s32[16]{0:T(128)} %refs_0_.7) | copy-start | bytes 196
  0.0 1.0 %copy-start = (bf16[64,2048]{1,0:T(8,128)(2,1)S(1)}, bf16[64,2048]{1,0:T(8,128)(2,1)}, u32[]{:S(2)}) copy-start(bf16[64,2048]{1,0:T(8,128)(2,1)} %tokens_ref.1) | copy-start | bytes 786436
  1.0 0.7 copy-start.3
  1.7 0.7 copy-start.4
  2.3 0.7 copy-start.5
  4.0 5.6 %collective-permute-start.2 = (bf16[65,16,128]{2,1,0:T(8,128)(2,1)S(1)}, bf16[65,16,128]{2,1,0:T(8,128)(2,1)S(1)}, u32[]{:S(2)}, u32[]{:S(2)}) collective-permute-start(bf16[65,16,128]{2,1,0:T(8,128)(2,1)S(1)} %pack.1.own_ref), channel_id=1, source_target_pairs={{0,4},{1,3},{4,8},{5,1},{8,12},{9,5},{12,14},{13,9},{14,10},{15,13... | collective-permute-start | bytes 798728 | tf_op jit(solution)/shard_map/ppermute | solution.py:244
  9.6 6.5 %collective-permute-start.3 = (bf16[65,16,128]{2,1,0:T(8,128)(2,1)S(1)}, bf16[65,16,128]{2,1,0:T(8,128)(2,1)S(1)}, u32[]{:S(2)}, u32[]{:S(2)}) collective-permute-start(bf16[65,16,128]{2,1,0:T(8,128)(2,1)S(1)} %collective-permute-done.2.refs_2_), channel_id=1, source_target_pairs={{0,4},{1,3},{4,8},{5,1},{8,12},{9,5},{12,14},{13,9},{14,10},{15,13... | collective-permute-start | bytes 798728 | tf_op jit(solution)/shard_map/ppermute | solution.py:244
  10.9 7.1 %collective-permute-start.9 = (bf16[65,16,128]{2,1,0:T(8,128)(2,1)S(1)}, bf16[65,16,128]{2,1,0:T(8,128)(2,1)S(1)}, u32[]{:S(2)}, u32[]{:S(2)}) collective-permute-start(bf16[65,16,128]{2,1,0:T(8,128)(2,1)S(1)} %pack.1.own_ref), channel_id=1, source_target_pairs={{1,4},{0,3},{5,8},{4,1},{9,12},{8,5},{13,14},{12,9},{15,10},{14,13... | collective-permute-start | bytes 798728 | tf_op jit(solution)/shard_map/ppermute | solution.py:244
  16.1 5.3 %collective-permute-start.4 = (bf16[65,16,128]{2,1,0:T(8,128)(2,1)S(1)}, bf16[65,16,128]{2,1,0:T(8,128)(2,1)S(1)}, u32[]{:S(2)}, u32[]{:S(2)}) collective-permute-start(bf16[65,16,128]{2,1,0:T(8,128)(2,1)S(1)} %collective-permute-done.3.refs_2_), channel_id=1, source_target_pairs={{0,4},{1,3},{4,8},{5,1},{8,12},{9,5},{12,14},{13,9},{14,10},{15,13... | collective-permute-start | bytes 798728 | tf_op jit(solution)/shard_map/ppermute | solution.py:244
  18.0 6.5 %collective-permute-start.10 = (bf16[65,16,128]{2,1,0:T(8,128)(2,1)S(1)}, bf16[65,16,128]{2,1,0:T(8,128)(2,1)S(1)}, u32[]{:S(2)}, u32[]{:S(2)}) collective-permute-start(bf16[65,16,128]{2,1,0:T(8,128)(2,1)S(1)} %collective-permute-done.9.refs_3_), channel_id=1, source_target_pairs={{0,4},{1,3},{4,8},{5,1},{8,12},{9,5},{12,14},{13,9},{14,10},{15,13... | collective-permute-start | bytes 798728 | tf_op jit(solution)/shard_map/ppermute | solution.py:244
  21.4 8.1 %collective-permute-start.5 = (bf16[65,16,128]{2,1,0:T(8,128)(2,1)S(1)}, bf16[65,16,128]{2,1,0:T(8,128)(2,1)S(1)}, u32[]{:S(2)}, u32[]{:S(2)}) collective-permute-start(bf16[65,16,128]{2,1,0:T(8,128)(2,1)S(1)} %collective-permute-done.4.refs_2_), channel_id=1, source_target_pairs={{0,4},{1,3},{4,8},{5,1},{8,12},{9,5},{12,14},{13,9},{14,10},{15,13... | collective-permute-start | bytes 798728 | tf_op jit(solution)/shard_map/ppermute | solution.py:244
  24.5 8.6 %collective-permute-start.11 = (bf16[65,16,128]{2,1,0:T(8,128)(2,1)S(1)}, bf16[65,16,128]{2,1,0:T(8,128)(2,1)S(1)}, u32[]{:S(2)}, u32[]{:S(2)}) collective-permute-start(bf16[65,16,128]{2,1,0:T(8,128)(2,1)S(1)} %collective-permute-done.10.refs_3_), channel_id=1, source_target_pairs={{0,4},{1,3},{4,8},{5,1},{8,12},{9,5},{12,14},{13,9},{14,10},{15,13... | collective-permute-start | bytes 798728 | tf_op jit(solution)/shard_map/ppermute | solution.py:244
  25.9 10.0 %collective-permute-start = (bf16[65,16,128]{2,1,0:T(8,128)(2,1)S(1)}, bf16[65,16,128]{2,1,0:T(8,128)(2,1)S(1)}, u32[]{:S(2)}, u32[]{:S(2)}) collective-permute-start(bf16[65,16,128]{2,1,0:T(8,128)(2,1)S(1)} %pack.1.own_ref), channel_id=1, source_target_pairs={{0,1},{1,0},{2,3},{3,2},{4,5},{5,4},{6,7},{7,6},{8,9},{9,8},{10,11... | collective-permute-start | bytes 798728 | tf_op jit(solution)/shard_map/ppermute | solution.py:244
  29.5 12.4 %collective-permute-start.6 = (bf16[65,16,128]{2,1,0:T(8,128)(2,1)S(1)}, bf16[65,16,128]{2,1,0:T(8,128)(2,1)S(1)}, u32[]{:S(2)}, u32[]{:S(2)}) collective-permute-start(bf16[65,16,128]{2,1,0:T(8,128)(2,1)S(1)} %collective-permute-done.5.refs_2_), channel_id=1, source_target_pairs={{0,1},{1,0},{2,3},{3,2},{4,5},{5,4},{6,7},{7,6},{8,9},{9,8},{10,11... | collective-permute-start | bytes 798728 | tf_op jit(solution)/shard_map/ppermute | solution.py:244
  33.1 12.1 %collective-permute-start.12 = (bf16[65,16,128]{2,1,0:T(8,128)(2,1)S(1)}, bf16[65,16,128]{2,1,0:T(8,128)(2,1)S(1)}, u32[]{:S(2)}, u32[]{:S(2)}) collective-permute-start(bf16[65,16,128]{2,1,0:T(8,128)(2,1)S(1)} %collective-permute-done.4.refs_2_), channel_id=1, source_target_pairs={{0,1},{1,0},{2,3},{3,2},{4,5},{5,4},{6,7},{7,6},{8,9},{9,8},{10,11... | collective-permute-start | bytes 798728 | tf_op jit(solution)/shard_map/ppermute | solution.py:244
  33.1 12.1 %collective-permute-start.13 = (bf16[65,16,128]{2,1,0:T(8,128)(2,1)S(1)}, bf16[65,16,128]{2,1,0:T(8,128)(2,1)S(1)}, u32[]{:S(2)}, u32[]{:S(2)}) collective-permute-start(bf16[65,16,128]{2,1,0:T(8,128)(2,1)S(1)} %collective-permute-done.11.refs_3_), channel_id=1, source_target_pairs={{0,1},{1,0},{2,3},{3,2},{4,5},{5,4},{6,7},{7,6},{8,9},{9,8},{10,11... | collective-permute-start | bytes 798728 | tf_op jit(solution)/shard_map/ppermute | solution.py:244
  35.9 0.7 copy-start.1
  44.6 4.4 %collective-permute-start.7 = (bf16[64,2048]{1,0:T(8,128)(2,1)S(1)}, bf16[64,2048]{1,0:T(8,128)(2,1)S(1)}, u32[]{:S(2)}, u32[]{:S(2)}) collective-permute-start(bf16[64,2048]{1,0:T(8,128)(2,1)S(1)} %get-tuple-element.23), channel_id=1, source_target_pairs={{0,1},{1,0},{2,3},{3,2},{4,5},{5,4},{6,7},{7,6},{8,9},{9,8},{10,11... | collective-permute-start | bytes 786440 | tf_op jit(solution)/shard_map/ppermute | solution.py:244
  44.6 6.1 %collective-permute-start.16 = (bf16[65,16,128]{2,1,0:T(8,128)(2,1)S(1)}, bf16[65,16,128]{2,1,0:T(8,128)(2,1)S(1)}, u32[]{:S(2)}, u32[]{:S(2)}) collective-permute-start(bf16[65,16,128]{2,1,0:T(8,128)(2,1)S(1)} %collective-permute-done.3.refs_2_), channel_id=1, source_target_pairs={{0,1},{1,0},{2,3},{3,2},{4,5},{5,4},{6,7},{7,6},{8,9},{9,8},{10,11... | collective-permute-start | bytes 798728 | tf_op jit(solution)/shard_map/ppermute | solution.py:244
  45.1 5.6 %collective-permute-start.17 = (bf16[65,16,128]{2,1,0:T(8,128)(2,1)S(1)}, bf16[65,16,128]{2,1,0:T(8,128)(2,1)S(1)}, u32[]{:S(2)}, u32[]{:S(2)}) collective-permute-start(bf16[65,16,128]{2,1,0:T(8,128)(2,1)S(1)} %collective-permute-done.10.refs_3_), channel_id=1, source_target_pairs={{0,1},{1,0},{2,3},{3,2},{4,5},{5,4},{6,7},{7,6},{8,9},{9,8},{10,11... | collective-permute-start | bytes 798728 | tf_op jit(solution)/shard_map/ppermute | solution.py:244
  48.5 6.1 %collective-permute-start.14 = (bf16[128,2048]{1,0:T(8,128)(2,1)S(1)}, bf16[128,2048]{1,0:T(8,128)(2,1)S(1)}, u32[]{:S(2)}, u32[]{:S(2)}) collective-permute-start(bf16[128,2048]{1,0:T(8,128)(2,1)S(1)} %get-tuple-element.25), channel_id=1, source_target_pairs={{0,1},{1,0},{2,3},{3,2},{4,5},{5,4},{6,7},{7,6},{8,9},{9,8},{10,11... | collective-permute-start | bytes 1572872 | tf_op jit(solution)/shard_map/ppermute | solution.py:244
  49.1 5.6 %collective-permute-start.8 = (bf16[64,2048]{1,0:T(8,128)(2,1)S(1)}, bf16[64,2048]{1,0:T(8,128)(2,1)S(1)}, u32[]{:S(2)}, u32[]{:S(2)}) collective-permute-start(bf16[64,2048]{1,0:T(8,128)(2,1)S(1)} %add_convert_fusion.7), channel_id=1, source_target_pairs={{4,0},{3,1},{8,4},{1,5},{12,8},{5,9},{14,12},{9,13},{10,14},{13,15... | collective-permute-start | bytes 786440 | tf_op jit(solution)/shard_map/ppermute | solution.py:244
  49.1 6.2 %collective-permute-start.20 = (bf16[65,16,128]{2,1,0:T(8,128)(2,1)S(1)}, bf16[65,16,128]{2,1,0:T(8,128)(2,1)S(1)}, u32[]{:S(2)}, u32[]{:S(2)}) collective-permute-start(bf16[65,16,128]{2,1,0:T(8,128)(2,1)S(1)} %collective-permute-done.2.refs_2_), channel_id=1, source_target_pairs={{0,1},{1,0},{2,3},{3,2},{4,5},{5,4},{6,7},{7,6},{8,9},{9,8},{10,11... | collective-permute-start | bytes 798728 | tf_op jit(solution)/shard_map/ppermute | solution.py:244
  50.8 4.5 %collective-permute-start.21 = (bf16[65,16,128]{2,1,0:T(8,128)(2,1)S(1)}, bf16[65,16,128]{2,1,0:T(8,128)(2,1)S(1)}, u32[]{:S(2)}, u32[]{:S(2)}) collective-permute-start(bf16[65,16,128]{2,1,0:T(8,128)(2,1)S(1)} %collective-permute-done.9.refs_3_), channel_id=1, source_target_pairs={{0,1},{1,0},{2,3},{3,2},{4,5},{5,4},{6,7},{7,6},{8,9},{9,8},{10,11... | collective-permute-start | bytes 798728 | tf_op jit(solution)/shard_map/ppermute | solution.py:244
  54.1 8.2 %collective-permute-start.18 = (bf16[128,2048]{1,0:T(8,128)(2,1)S(1)}, bf16[128,2048]{1,0:T(8,128)(2,1)S(1)}, u32[]{:S(2)}, u32[]{:S(2)}) collective-permute-start(bf16[128,2048]{1,0:T(8,128)(2,1)S(1)} %get-tuple-element.27), channel_id=1, source_target_pairs={{0,1},{1,0},{2,3},{3,2},{4,5},{5,4},{6,7},{7,6},{8,9},{9,8},{10,11... | collective-permute-start | bytes 1572872 | tf_op jit(solution)/shard_map/ppermute | solution.py:244
  54.8 7.5 %collective-permute-start.15 = (bf16[64,2048]{1,0:T(8,128)(2,1)S(1)}, bf16[64,2048]{1,0:T(8,128)(2,1)S(1)}, u32[]{:S(2)}, u32[]{:S(2)}) collective-permute-start(bf16[64,2048]{1,0:T(8,128)(2,1)S(1)} %get-tuple-element.37), channel_id=1, source_target_pairs={{4,0},{3,1},{8,4},{1,5},{12,8},{5,9},{14,12},{9,13},{10,14},{13,15... | collective-permute-start | bytes 786440 | tf_op jit(solution)/shard_map/ppermute | solution.py:244
  55.0 8.2 %collective-permute-start.24 = (bf16[64,2048]{1,0:T(8,128)(2,1)S(1)}, bf16[64,2048]{1,0:T(8,128)(2,1)S(1)}, u32[]{:S(2)}, u32[]{:S(2)}) collective-permute-start(bf16[64,2048]{1,0:T(8,128)(2,1)S(1)} %get-tuple-element.38), channel_id=1, source_target_pairs={{4,0},{3,1},{8,4},{1,5},{12,8},{5,9},{14,12},{9,13},{10,14},{13,15... | collective-permute-start | bytes 786440 | tf_op jit(solution)/shard_map/ppermute | solution.py:244
  58.6 9.8 %collective-permute-start.22 = (bf16[128,2048]{1,0:T(8,128)(2,1)S(1)}, bf16[128,2048]{1,0:T(8,128)(2,1)S(1)}, u32[]{:S(2)}, u32[]{:S(2)}) collective-permute-start(bf16[128,2048]{1,0:T(8,128)(2,1)S(1)} %get-tuple-element.29), channel_id=1, source_target_pairs={{0,1},{1,0},{2,3},{3,2},{4,5},{5,4},{6,7},{7,6},{8,9},{9,8},{10,11... | collective-permute-start | bytes 1572872 | tf_op jit(solution)/shard_map/ppermute | solution.py:244
  63.4 5.6 %collective-permute-start.19 = (bf16[64,2048]{1,0:T(8,128)(2,1)S(1)}, bf16[64,2048]{1,0:T(8,128)(2,1)S(1)}, u32[]{:S(2)}, u32[]{:S(2)}) collective-permute-start(bf16[64,2048]{1,0:T(8,128)(2,1)S(1)} %get-tuple-element.35), channel_id=1, source_target_pairs={{4,0},{3,1},{8,4},{1,5},{12,8},{5,9},{14,12},{9,13},{10,14},{13,15... | collective-permute-start | bytes 786440 | tf_op jit(solution)/shard_map/ppermute | solution.py:244
  63.6 8.2 %collective-permute-start.25 = (bf16[64,2048]{1,0:T(8,128)(2,1)S(1)}, bf16[64,2048]{1,0:T(8,128)(2,1)S(1)}, u32[]{:S(2)}, u32[]{:S(2)}) collective-permute-start(bf16[64,2048]{1,0:T(8,128)(2,1)S(1)} %get-tuple-element.36), channel_id=1, source_target_pairs={{4,0},{3,1},{8,4},{1,5},{12,8},{5,9},{14,12},{9,13},{10,14},{13,15... | collective-permute-start | bytes 786440 | tf_op jit(solution)/shard_map/ppermute | solution.py:244
  63.7 12.6 %collective-permute-start.1 = (bf16[64,2048]{1,0:T(8,128)(2,1)S(1)}, bf16[64,2048]{1,0:T(8,128)(2,1)S(1)}, u32[]{:S(2)}, u32[]{:S(2)}) collective-permute-start(bf16[64,2048]{1,0:T(8,128)(2,1)S(1)} %get-tuple-element.20), channel_id=1, source_target_pairs={{0,1},{1,0},{2,3},{3,2},{4,5},{5,4},{6,7},{7,6},{8,9},{9,8},{10,11... | collective-permute-start | bytes 786440 | tf_op jit(solution)/shard_map/ppermute | solution.py:244
  72.0 5.3 %collective-permute-start.23 = (bf16[64,2048]{1,0:T(8,128)(2,1)S(1)}, bf16[64,2048]{1,0:T(8,128)(2,1)S(1)}, u32[]{:S(2)}, u32[]{:S(2)}) collective-permute-start(bf16[64,2048]{1,0:T(8,128)(2,1)S(1)} %get-tuple-element.33), channel_id=1, source_target_pairs={{4,0},{3,1},{8,4},{1,5},{12,8},{5,9},{14,12},{9,13},{10,14},{13,15... | collective-permute-start | bytes 786440 | tf_op jit(solution)/shard_map/ppermute | solution.py:244
  72.2 10.9 %collective-permute-start.26 = (bf16[64,2048]{1,0:T(8,128)(2,1)S(1)}, bf16[64,2048]{1,0:T(8,128)(2,1)S(1)}, u32[]{:S(2)}, u32[]{:S(2)}) collective-permute-start(bf16[64,2048]{1,0:T(8,128)(2,1)S(1)} %get-tuple-element.34), channel_id=1, source_target_pairs={{4,1},{3,0},{8,5},{1,4},{12,9},{5,8},{14,13},{9,12},{10,15},{13,14... | collective-permute-start | bytes 786440 | tf_op jit(solution)/shard_map/ppermute | solution.py:244

commit v3 on v2

--- a/solution.py
+++ b/solution.py
@@ -13,7 +13,7 @@
 VMEM = pl.BlockSpec(memory_space=pltpu.VMEM)
 SMEM = pl.BlockSpec(memory_space=pltpu.SMEM)
 HBM = pl.BlockSpec(memory_space=pltpu.HBM)
-VMEM_BYTES = 24 * 1024 * 1024
+VMEM_BYTES = 20 * 1024 * 1024
 
 
 class Packing:
@@ -29,7 +29,17 @@
         self.tiles = self.token_tiles + self.gate_tiles
 
 
-def pack_body(pk, capacity, devices, tokens_ref, ids_ref, gates_ref, spare_ref, out_ref):
+def pack_body(pk, capacity, devices, me_ref, *refs):
+    sources, (out_ref, mine_ref), scratch, sems = refs[:5], refs[5:7], refs[7:12], refs[12]
+    copies = [
+        pltpu.make_async_copy(source, target, sems.at[index])
+        for index, (source, target) in enumerate(zip(sources, scratch))
+    ]
+    for copy in copies:
+        copy.start()
+    for copy in copies:
+        copy.wait()
+    tokens_ref, ids_ref, gates_ref, home_ref, spare_ref = scratch
     for group in range(pk.groups):
         for col in range(pk.cols):
             out_ref[group * pk.cols + col] = tokens_ref[
@@ -52,8 +62,11 @@
     ).astype(jnp.float32).astype(jnp.bfloat16)
     arrival = jnp.dot(before, chosen.astype(jnp.bfloat16), preferred_element_type=jnp.float32)
     named = jnp.zeros((1, LANES), jnp.int32)
-    for device in range(devices):
-        named = named + (expert == spare_ref[device]).astype(jnp.int32)
+    mine = jnp.int32(0)
+    for index in range(devices):
+        named = named + (expert == spare_ref[index]).astype(jnp.int32)
+        mine = jnp.where(home_ref[index] == me_ref[0], index, mine)
+    mine_ref[...] = jnp.full(mine_ref.shape, mine, jnp.int32)
     count = jnp.ones((1, LANES), jnp.int32)
     for copy in range(1, devices // THIRD + 1):
         count = count + (named >= THIRD * copy).astype(jnp.int32)
@@ -71,15 +84,22 @@
         out_ref[pk.token_tiles + index] = tile.astype(jnp.bfloat16)
 
 
-def pack(pk, capacity, devices, tokens, ids, gates, spare):
+def pack(pk, capacity, devices, me, tokens, ids, gates, home, spare):
+    sources = [tokens, ids.T, gates.T, home, spare]
+    spaces = [pltpu.VMEM, pltpu.VMEM, pltpu.VMEM, pltpu.SMEM, pltpu.SMEM]
     return pl.pallas_call(
         functools.partial(pack_body, pk, capacity, devices),
-        out_shape=jax.ShapeDtypeStruct((pk.tiles, SUBS, LANES), jnp.bfloat16),
-        in_specs=[VMEM, VMEM, VMEM, SMEM],
-        out_specs=VMEM,
+        out_shape=[
+            jax.ShapeDtypeStruct((pk.tiles, SUBS, LANES), jnp.bfloat16),
+            pltpu.VMEM((SUBS, LANES), jnp.int32),
+        ],
+        in_specs=[SMEM] + [HBM] * len(sources),
+        out_specs=[VMEM, VMEM],
+        scratch_shapes=[space(x.shape, x.dtype) for space, x in zip(spaces, sources)]
+        + [pltpu.SemaphoreType.DMA((len(sources),))],
         compiler_params=pltpu.CompilerParams(vmem_limit_bytes=VMEM_BYTES),
         name="pack",
-    )(tokens, ids.T, gates.T, spare)
+    )(me, *[pltpu.with_memory_space_constraint(x, pltpu.HBM) for x in sources])
 
 
 def gather_rows(pk, buffers, x_ref):
@@ -102,15 +122,12 @@
     )
 
 
-def store_scaled(pk, home_ref, me_ref, buffers, answers, out_refs):
-    mine = jnp.int32(0)
-    for e in range(pk.experts):
-        mine = jnp.where(home_ref[e] == me_ref[0], e, mine)
-    lane = lax.broadcasted_iota(jnp.int32, (1, LANES), 1)
+def store_scaled(pk, mine_ref, buffers, answers, out_refs):
+    lane = lax.broadcasted_iota(jnp.int32, (SUBS, LANES), 1)
     scales = []
     for buffer in buffers:
         for group in range(pk.groups):
-            place = (group % pk.per_tile) * 2 * pk.experts + mine
+            place = (group % pk.per_tile) * 2 * pk.experts + mine_ref[...]
             wanted = (lane == place) | (lane == place + pk.experts)
             table = buffer[pk.token_tiles + group // pk.per_tile].astype(jnp.float32)
             scales.append(jnp.sum(jnp.where(wanted, table, 0.0), axis=1, keepdims=True))
@@ -122,8 +139,8 @@
             row += SUBS
 
 
-def first_body(pk, width, home_ref, me_ref, own_ref, other_ref, weights_ref, *rest):
-    keep_ref, give_ref, kept_ref, x_ref, acc_ref, sems = rest
+def first_body(pk, width, mine_ref, own_ref, weights_ref, *rest):
+    keep_ref, kept_ref, x_ref, acc_ref, sems = rest
     block = width // THIRD
     copies = []
     for j in range(THIRD):
@@ -134,7 +151,7 @@
             )
             copy.start()
             copies.append(copy)
-    gather_rows(pk, [own_ref, other_ref], x_ref)
+    gather_rows(pk, [own_ref], x_ref)
     rows = x_ref[...]
     for j in range(THIRD):
         for part in range(THIRD):
@@ -154,51 +171,50 @@
             acc_ref[...] = part
         else:
             acc_ref[...] += part
-    store_scaled(pk, home_ref, me_ref, [own_ref, other_ref], acc_ref, [keep_ref, give_ref])
-
-
-def first_chunk(pk, weights, home, me, own, other):
+    store_scaled(pk, mine_ref, [own_ref], acc_ref, [keep_ref])
+
+
+def first_chunk(pk, weights, mine, own):
     width = weights.shape[2] // 4
     rows, feature = pk.local_tokens, pk.feature
     return pl.pallas_call(
         functools.partial(first_body, pk, width),
         out_shape=[
-            jax.ShapeDtypeStruct((rows, feature), jnp.float32),
-            jax.ShapeDtypeStruct((rows, feature), jnp.bfloat16),
+            pltpu.VMEM((rows, feature), jnp.float32),
             pltpu.VMEM((feature, THIRD * width), jnp.bfloat16),
         ],
-        in_specs=[SMEM, SMEM, VMEM, VMEM, HBM],
-        out_specs=[VMEM, VMEM, VMEM],
+        in_specs=[VMEM, VMEM, HBM],
+        out_specs=[VMEM, VMEM],
         scratch_shapes=[
-            pltpu.VMEM((2 * rows, feature), jnp.bfloat16),
-            pltpu.VMEM((2 * rows, feature), jnp.float32),
+            pltpu.VMEM((rows, feature), jnp.bfloat16),
+            pltpu.VMEM((rows, feature), jnp.float32),
             pltpu.SemaphoreType.DMA((THIRD, THIRD)),
         ],
         compiler_params=pltpu.CompilerParams(vmem_limit_bytes=VMEM_BYTES),
         cost_estimate=pl.CostEstimate(
-            flops=4 * rows * feature * 3 * width,
-            transcendentals=2 * rows * width,
+            flops=2 * rows * feature * 3 * width,
+            transcendentals=rows * width,
             bytes_accessed=2 * feature * 3 * width,
         ),
         name="first_chunk",
-    )(home, me, own, other, pltpu.with_memory_space_constraint(weights, pltpu.HBM))
+    )(mine, own, pltpu.with_memory_space_constraint(weights, pltpu.HBM))
 
 
 def chunk_body(pk, width, count, *refs):
-    home_ref, me_ref = refs[:2]
-    buffers = refs[2 : 2 + count]
-    weights_ref = refs[2 + count]
-    out_refs = refs[3 + count : -1]
+    mine_ref = refs[0]
+    buffers = refs[1 : 1 + count]
+    weights_ref = refs[1 + count]
+    out_refs = refs[2 + count : -1]
     x_ref = refs[-1]
     gather_rows(pk, buffers, x_ref)
     rows = x_ref[...]
     gate = jnp.dot(rows, weights_ref[:, :width], preferred_element_type=jnp.float32)
     up = jnp.dot(rows, weights_ref[:, width : 2 * width], preferred_element_type=jnp.float32)
     answers = down(activate(gate, up), weights_ref[:, 2 * width :])
-    store_scaled(pk, home_ref, me_ref, buffers, answers, out_refs)
-
-
-def chunk(pk, weights, home, me, own, crossed):
+    store_scaled(pk, mine_ref, buffers, answers, out_refs)
+
+
+def chunk(pk, weights, mine, own, crossed):
     width = weights.shape[1] // THIRD
     rows, feature = pk.local_tokens, pk.feature
     buffers = own + crossed
@@ -207,7 +223,7 @@
         functools.partial(chunk_body, pk, width, len(buffers)),
         out_shape=[jax.ShapeDtypeStruct((rows, feature), jnp.float32) for _ in own]
         + [jax.ShapeDtypeStruct((rows * len(crossed), feature), jnp.bfloat16)],
-        in_specs=[SMEM, SMEM] + [VMEM] * (len(buffers) + 1),
+        in_specs=[VMEM] * (len(buffers) + 2),
         out_specs=[VMEM] * (len(own) + 1),
         scratch_shapes=[pltpu.VMEM((total, feature), jnp.bfloat16)],
         compiler_params=pltpu.CompilerParams(vmem_limit_bytes=VMEM_BYTES),
@@ -217,7 +233,28 @@
             bytes_accessed=2 * feature * 3 * width,
         ),
         name="chunk",
-    )(home, me, *buffers, weights)
+    )(mine, *buffers, weights)
+
+
+def add_body(starts, *refs):
+    out_ref = refs[-1]
+    rows = out_ref.shape[0]
+    total = refs[0][starts[0] : starts[0] + rows, :].astype(jnp.float32)
+    for ref, start in zip(refs[1:-1], starts[1:]):
+        total = total + ref[start : start + rows, :].astype(jnp.float32)
+    out_ref[...] = total.astype(out_ref.dtype)
+
+
+def add(rows, dtype, terms):
+    arrays = [array for array, _ in terms]
+    return pl.pallas_call(
+        functools.partial(add_body, [start for _, start in terms]),
+        out_shape=jax.ShapeDtypeStruct((rows, arrays[0].shape[1]), dtype),
+        in_specs=[VMEM] * len(arrays),
+        out_specs=VMEM,
+        compiler_params=pltpu.CompilerParams(vmem_limit_bytes=VMEM_BYTES),
+        name="add",
+    )(*arrays)
 
 
 def shards(tokens, expert_ids, gate_values, expert_weights, home_slot, spare_expert):
@@ -244,38 +281,38 @@
         return lax.ppermute(x, "ep", where)
 
     me = lax.axis_index("ep").astype(jnp.int32).reshape(1)
-    packed = pack(pk, capacity, devices, tokens, expert_ids, gate_values, spare_expert)
+    packed, mine = pack(
+        pk, capacity, devices, me, tokens, expert_ids, gate_values, home_slot, spare_expert
+    )
 
     keep, gave = {}, {}
     a, b = send(packed, straight), send(packed, crossing)
-    other = send(packed, pair)
-    keep[0], give, weights = first_chunk(
-        pk, expert_weights, home_slot, me, packed, other
-    )
-    gave[0] = send(give, pair)
+    keep_own, weights = first_chunk(pk, expert_weights, mine, packed)
+    other = [send(packed, pair)]
     for r in range(1, far):
         xa, xb = send(a, pair), send(b, pair)
-        keep_a, keep_b, give = chunk(pk, weights, home_slot, me, [a, b], [xa, xb])
+        keep_a, keep_b, give = chunk(pk, weights, mine, [a, b], [xa, xb] + other)
+        other = []
         keep[r] = (keep_a, keep_b)
         gave[r] = send(give, pair)
         a = send(a, straight)
         if r + 1 < far:
             b = send(b, straight)
     xa = send(a, pair)
-    keep_a, give = chunk(pk, weights, home_slot, me, [a], [xa])
+    keep_a, give = chunk(pk, weights, mine, [a], [xa])
     gave[far] = send(give, pair)
 
-    a = (keep_a + gave[far].astype(jnp.float32)).astype(wire)
-    a = send(a, straight_back).astype(jnp.float32)
-    b = jnp.zeros((), jnp.float32)
+    half = local_tokens
+    a = add(half, wire, [(keep_a, 0), (gave[far], 0)])
+    a, b = [(send(a, straight_back), 0)], []
     for r in range(far - 1, 0, -1):
         keep_a, keep_b = keep[r]
-        a = (a + keep_a + gave[r][:local_tokens].astype(jnp.float32)).astype(wire)
-        b = (b + keep_b + gave[r][local_tokens:].astype(jnp.float32)).astype(wire)
-        a = send(a, straight_back).astype(jnp.float32)
-        b = send(b, straight_back if r > 1 else crossing_back).astype(jnp.float32)
-    total = keep[0] + gave[0].astype(jnp.float32) + a + b
-    return total.astype(jnp.bfloat16)
+        b = add(half, wire, [(keep_b, 0), (gave[r], half)] + b)
+        b = [(send(b, straight_back if r > 1 else crossing_back), 0)]
+        a = add(half, wire, [(keep_a, 0), (gave[r], 0)] + a)
+        a = [(send(a, straight_back), 0)]
+    terms = [(keep_own, 0), (gave[1], 2 * half)] + b + a
+    return add(half, jnp.bfloat16, terms)
 
 
 def solution(mesh):

time: 84.3 us -> 75.9 us (0.900)
  the two profiles are of different devices: /device:TPU:13 before, /device:TPU:0 now
where the time goes in v3:
time: 75.9 us; the launch traced here: 75.8 us
  waiting for transfers between devices  31.3 us (41%)
  starting transfers between devices  26 us (34%)
  Pallas kernels  18.4 us (24%)
    ppermute x26, waiting for transfers between devices, send(): return lax.ppermute(x, 'ep', where)  31.3 us
    ppermute x26, starting transfers between devices, send(): return lax.ppermute(x, 'ep', where)  26 us
    pallas_call x4, Pallas kernels, chunk(): pl.pallas_call(functools.partial(chunk_body, pk, width, len(buffers)), ou...  10.8 us
    pallas_call x1, Pallas kernels, first_chunk(): pl.pallas_call(functools.partial(first_body, pk, width), out_shape=[pltpu...  4.77 us
  transfers between devices with their start and end apart: 26, of which 13 were waited for; matrix products, arithmetic and copies ran while one was open for 0% of the time, Pallas kernels for 21%

profile of v3, /device:TPU:0, one launch (start us, length us, event | category | flops | bytes accessed | tf_op | source)
XLA Modules:
  0.0 75.8 jit_solution(2971687564265951737)
XLA Ops:
  0.0 1.4 %pack.1 = (bf16[65,16,128]{2,1,0:T(8,128)(2,1)S(1)}, s32[16,128]{1,0:T(8,128)S(1)}) custom-call(s32[1]{0:T(128)} %bitcast.me_ref, bf16[64,2048]{1,0:T(8,128)(2,1)} %refs_0_.1, s32[8,64]{1,0:T(8,128)} %bitcast.3, f32[8,64]{1,0:T(8,128)} %bitcast.4, s32[16]{0:T(128)} %refs_3_.1, s32[16]{0:T(128)} %refs_4_.1), custom_call_target="tpu_custom_call" | custom-call | tf_op jit(solution)/shard_map/pack/pallas_call | solution.py:90
  1.4 3.1 %collective-permute-start = (bf16[65,16,128]{2,1,0:T(8,128)(2,1)S(1)}, bf16[65,16,128]{2,1,0:T(8,128)(2,1)S(1)}, u32[]{:S(2)}, u32[]{:S(2)}) collective-permute-start(bf16[65,16,128]{2,1,0:T(8,128)(2,1)S(1)} %get-tuple-element.21.own_ref), channel_id=1, source_target_pairs={{0,4},{1,3},{4,8},{5,1},{8,12},{9,5},{12,14},{13,9},{14,10},{15,13... | collective-permute-start | bytes 798728 | tf_op jit(solution)/shard_map/ppermute | solution.py:281
  4.6 0.7 collective-permute-start.1
  5.2 5.1 %collective-permute-done.refs_1_ = bf16[65,16,128]{2,1,0:T(8,128)(2,1)S(1)} collective-permute-done((bf16[65,16,128]{2,1,0:T(8,128)(2,1)S(1)}, bf16[65,16,128]{2,1,0:T(8,128)(2,1)S(1)}, u32[]{:S(2)}, u32[]{:S(2)}) %collective-permute-start) | collective-permute-done | bytes 266272 | tf_op jit(solution)/shard_map/ppermute | solution.py:281
  10.3 2.5 %collective-permute-start.6 = (bf16[65,16,128]{2,1,0:T(8,128)(2,1)S(1)}, bf16[65,16,128]{2,1,0:T(8,128)(2,1)S(1)}, u32[]{:S(2)}, u32[]{:S(2)}) collective-permute-start(bf16[65,16,128]{2,1,0:T(8,128)(2,1)S(1)} %collective-permute-done.refs_1_), channel_id=1, source_target_pairs={{0,4},{1,3},{4,8},{5,1},{8,12},{9,5},{12,14},{13,9},{14,10},{15,13... | collective-permute-start | bytes 798728 | tf_op jit(solution)/shard_map/ppermute | solution.py:281
  12.8 0.0 collective-permute-done.1.refs_2_
  12.8 1.6 %collective-permute-start.7 = (bf16[65,16,128]{2,1,0:T(8,128)(2,1)S(1)}, bf16[65,16,128]{2,1,0:T(8,128)(2,1)S(1)}, u32[]{:S(2)}, u32[]{:S(2)}) collective-permute-start(bf16[65,16,128]{2,1,0:T(8,128)(2,1)S(1)} %collective-permute-done.1.refs_2_), channel_id=1, source_target_pairs={{0,4},{1,3},{4,8},{5,1},{8,12},{9,5},{12,14},{13,9},{14,10},{15,13... | collective-permute-start | bytes 798728 | tf_op jit(solution)/shard_map/ppermute | solution.py:281
  14.4 3.8 %collective-permute-done.6.refs_1_ = bf16[65,16,128]{2,1,0:T(8,128)(2,1)S(1)} collective-permute-done((bf16[65,16,128]{2,1,0:T(8,128)(2,1)S(1)}, bf16[65,16,128]{2,1,0:T(8,128)(2,1)S(1)}, u32[]{:S(2)}, u32[]{:S(2)}) %collective-permute-start.6) | collective-permute-done | bytes 266272 | tf_op jit(solution)/shard_map/ppermute | solution.py:281
  18.2 1.1 %collective-permute-start.11 = (bf16[65,16,128]{2,1,0:T(8,128)(2,1)S(1)}, bf16[65,16,128]{2,1,0:T(8,128)(2,1)S(1)}, u32[]{:S(2)}, u32[]{:S(2)}) collective-permute-start(bf16[65,16,128]{2,1,0:T(8,128)(2,1)S(1)} %collective-permute-done.6.refs_1_), channel_id=1, source_target_pairs={{0,4},{1,3},{4,8},{5,1},{8,12},{9,5},{12,14},{13,9},{14,10},{15,13... | collective-permute-start | bytes 798728 | tf_op jit(solution)/shard_map/ppermute | solution.py:281
  19.2 1.8 %collective-permute-done.7.refs_2_ = bf16[65,16,128]{2,1,0:T(8,128)(2,1)S(1)} collective-permute-done((bf16[65,16,128]{2,1,0:T(8,128)(2,1)S(1)}, bf16[65,16,128]{2,1,0:T(8,128)(2,1)S(1)}, u32[]{:S(2)}, u32[]{:S(2)}) %collective-permute-start.7) | collective-permute-done | bytes 266272 | tf_op jit(solution)/shard_map/ppermute | solution.py:281
  21.0 1.1 %collective-permute-start.12 = (bf16[65,16,128]{2,1,0:T(8,128)(2,1)S(1)}, bf16[65,16,128]{2,1,0:T(8,128)(2,1)S(1)}, u32[]{:S(2)}, u32[]{:S(2)}) collective-permute-start(bf16[65,16,128]{2,1,0:T(8,128)(2,1)S(1)} %collective-permute-done.7.refs_2_), channel_id=1, source_target_pairs={{0,4},{1,3},{4,8},{5,1},{8,12},{9,5},{12,14},{13,9},{14,10},{15,13... | collective-permute-start | bytes 798728 | tf_op jit(solution)/shard_map/ppermute | solution.py:281
  22.1 2.5 %collective-permute-done.11.refs_1_ = bf16[65,16,128]{2,1,0:T(8,128)(2,1)S(1)} collective-permute-done((bf16[65,16,128]{2,1,0:T(8,128)(2,1)S(1)}, bf16[65,16,128]{2,1,0:T(8,128)(2,1)S(1)}, u32[]{:S(2)}, u32[]{:S(2)}) %collective-permute-start.11) | collective-permute-done | bytes 266272 | tf_op jit(solution)/shard_map/ppermute | solution.py:281
  24.6 1.1 %collective-permute-start.19 = (bf16[65,16,128]{2,1,0:T(8,128)(2,1)S(1)}, bf16[65,16,128]{2,1,0:T(8,128)(2,1)S(1)}, u32[]{:S(2)}, u32[]{:S(2)}) collective-permute-start(bf16[65,16,128]{2,1,0:T(8,128)(2,1)S(1)} %collective-permute-done.11.refs_1_), channel_id=1, source_target_pairs={{0,4},{1,3},{4,8},{5,1},{8,12},{9,5},{12,14},{13,9},{14,10},{15,13... | collective-permute-start | bytes 798728 | tf_op jit(solution)/shard_map/ppermute | solution.py:281
  25.7 0.0 collective-permute-start.13
  25.7 1.8 %collective-permute-done.12.refs_2_ = bf16[65,16,128]{2,1,0:T(8,128)(2,1)S(1)} collective-permute-done((bf16[65,16,128]{2,1,0:T(8,128)(2,1)S(1)}, bf16[65,16,128]{2,1,0:T(8,128)(2,1)S(1)}, u32[]{:S(2)}, u32[]{:S(2)}) %collective-permute-start.12) | collective-permute-done | bytes 266272 | tf_op jit(solution)/shard_map/ppermute | solution.py:281
  27.4 0.0 collective-permute-start.14
  27.4 0.5 collective-permute-start.4
  27.9 3.1 %collective-permute-done.19.refs_1_ = bf16[65,16,128]{2,1,0:T(8,128)(2,1)S(1)} collective-permute-done((bf16[65,16,128]{2,1,0:T(8,128)(2,1)S(1)}, bf16[65,16,128]{2,1,0:T(8,128)(2,1)S(1)}, u32[]{:S(2)}, u32[]{:S(2)}) %collective-permute-start.19) | collective-permute-done | bytes 266272 | tf_op jit(solution)/shard_map/ppermute | solution.py:281
  31.0 0.0 collective-permute-start.20
  31.0 4.8 %first_chunk.1 = (f32[64,2048]{1,0:T(8,128)S(1)}, bf16[2048,2304]{1,0:T(8,128)(2,1)S(1)}) custom-call(s32[16,128]{1,0:T(8,128)S(1)} %get-tuple-element.20.mine_ref.refs_0_, bf16[65,16,128]{2,1,0:T(8,128)(2,1)S(1)} %get-tuple-element.21.own_ref, bf16[1,2048,3072]{2,1,0:T(8,128)(2,1)} %weights_ref.1), custom_call_target="tpu_custom_call" | custom-call | flops 603979776 | bytes 9437184 | tf_op jit(solution)/shard_map/first_chunk/pallas_call | solution.py:180
  35.8 0.6 collective-permute-start.2
  36.4 0.0 collective-permute-done.13.refs_3_
  36.4 0.1 collective-permute-start.3
  36.4 0.0 collective-permute-done.14.refs_4_
  36.4 0.4 collective-permute-start.8
  36.9 2.7 %chunk.6 = (f32[64,2048]{1,0:T(8,128)S(1)}, f32[64,2048]{1,0:T(8,128)S(1)}, bf16[128,2048]{1,0:T(8,128)(2,1)S(1)}) custom-call(s32[16,128]{1,0:T(8,128)S(1)} %get-tuple-element.20.mine_ref.refs_0_, bf16[65,16,128]{2,1,0:T(8,128)(2,1)S(1)} %collective-permute-done.11.refs_1_, bf16[65,16,128]{2,1,0:T(8,128)(2,1)S(1)} %collective-permute-done.12.refs_2_, ...), custom_call_target="tpu_custom_call" | custom-call | flops 2415919104 | bytes 9437184 | tf_op jit(solution)/shard_map/chunk/pallas_call | solution.py:222
  39.6 0.0 collective-permute-done.20.refs_2_
  39.6 0.1 collective-permute-start.9
  39.7 2.0 %chunk.7 = (f32[64,2048]{1,0:T(8,128)S(1)}, bf16[64,2048]{1,0:T(8,128)(2,1)S(1)}) custom-call(s32[16,128]{1,0:T(8,128)S(1)} %get-tuple-element.20.mine_ref.refs_0_, bf16[65,16,128]{2,1,0:T(8,128)(2,1)S(1)} %collective-permute-done.19.refs_1_, bf16[65,16,128]{2,1,0:T(8,128)(2,1)S(1)} %collective-permute-done.20.refs_2_, ...), custom_call_target="tpu_custom_call" | custom-call | flops 1207959552 | bytes 9437184 | tf_op jit(solution)/shard_map/chunk/pallas_call | solution.py:222
  41.8 0.0 collective-permute-done.4.refs_5_
  41.8 0.5 collective-permute-start.15
  42.3 0.0 collective-permute-done.2.refs_3_
  42.3 0.1 collective-permute-start.21
  42.4 0.0 collective-permute-done.3.refs_4_
  42.4 3.3 %chunk.4 = (f32[64,2048]{1,0:T(8,128)S(1)}, f32[64,2048]{1,0:T(8,128)S(1)}, bf16[192,2048]{1,0:T(8,128)(2,1)S(1)}) custom-call(s32[16,128]{1,0:T(8,128)S(1)} %get-tuple-element.20.mine_ref.refs_0_, bf16[65,16,128]{2,1,0:T(8,128)(2,1)S(1)} %collective-permute-done.refs_1_, bf16[65,16,128]{2,1,0:T(8,128)(2,1)S(1)} %collective-permute-done.1.refs_2_, ...), custom_call_target="tpu_custom_call" | custom-call | flops 3019898880 | bytes 9437184 | tf_op jit(solution)/shard_map/chunk/pallas_call | solution.py:222
  45.7 0.0 collective-permute-done.8.refs_3_
  45.7 0.0 collective-permute-done.9.refs_4_
  45.7 2.7 %chunk.5 = (f32[64,2048]{1,0:T(8,128)S(1)}, f32[64,2048]{1,0:T(8,128)S(1)}, bf16[128,2048]{1,0:T(8,128)(2,1)S(1)}) custom-call(s32[16,128]{1,0:T(8,128)S(1)} %get-tuple-element.20.mine_ref.refs_0_, bf16[65,16,128]{2,1,0:T(8,128)(2,1)S(1)} %collective-permute-done.6.refs_1_, bf16[65,16,128]{2,1,0:T(8,128)(2,1)S(1)} %collective-permute-done.7.refs_2_, ...), custom_call_target="tpu_custom_call" | custom-call | flops 2415919104 | bytes 9437184 | tf_op jit(solution)/shard_map/chunk/pallas_call | solution.py:222
  48.5 0.5 collective-permute-start.10
  49.0 0.0 collective-permute-done.21.refs_1_
  49.0 2.1 %collective-permute-start.22 = (bf16[64,2048]{1,0:T(8,128)(2,1)S(1)}, bf16[64,2048]{1,0:T(8,128)(2,1)S(1)}, u32[]{:S(2)}, u32[]{:S(2)}) collective-permute-start(bf16[64,2048]{1,0:T(8,128)(2,1)S(1)} %add.11), channel_id=1, source_target_pairs={{4,0},{3,1},{8,4},{1,5},{12,8},{5,9},{14,12},{9,13},{10,14},{13,15... | collective-permute-start | bytes 786440 | tf_op jit(solution)/shard_map/ppermute | solution.py:281
  51.1 0.0 collective-permute-start.5
  51.1 0.0 collective-permute-done.15.refs_1_
  51.1 1.6 %collective-permute-start.16 = (bf16[64,2048]{1,0:T(8,128)(2,1)S(1)}, bf16[64,2048]{1,0:T(8,128)(2,1)S(1)}, u32[]{:S(2)}, u32[]{:S(2)}) collective-permute-start(bf16[64,2048]{1,0:T(8,128)(2,1)S(1)} %add.8), channel_id=1, source_target_pairs={{4,0},{3,1},{8,4},{1,5},{12,8},{5,9},{14,12},{9,13},{10,14},{13,15... | collective-permute-start | bytes 786440 | tf_op jit(solution)/shard_map/ppermute | solution.py:281
  52.8 2.7 %collective-permute-done.22.refs_2_ = bf16[64,2048]{1,0:T(8,128)(2,1)S(1)} collective-permute-done((bf16[64,2048]{1,0:T(8,128)(2,1)S(1)}, bf16[64,2048]{1,0:T(8,128)(2,1)S(1)}, u32[]{:S(2)}, u32[]{:S(2)}) %collective-permute-start.22) | collective-permute-done | bytes 262176 | tf_op jit(solution)/shard_map/ppermute | solution.py:281
  55.4 0.1 add.12
  55.5 2.1 %collective-permute-start.23 = (bf16[64,2048]{1,0:T(8,128)(2,1)S(1)}, bf16[64,2048]{1,0:T(8,128)(2,1)S(1)}, u32[]{:S(2)}, u32[]{:S(2)}) collective-permute-start(bf16[64,2048]{1,0:T(8,128)(2,1)S(1)} %add.12), channel_id=1, source_target_pairs={{4,0},{3,1},{8,4},{1,5},{12,8},{5,9},{14,12},{9,13},{10,14},{13,15... | collective-permute-start | bytes 786440 | tf_op jit(solution)/shard_map/ppermute | solution.py:281
  57.6 0.0 collective-permute-done.10.refs_1_
  57.6 0.6 collective-permute-done.16.refs_2_
  58.2 0.1 add.9
  58.3 2.1 %collective-permute-start.17 = (bf16[64,2048]{1,0:T(8,128)(2,1)S(1)}, bf16[64,2048]{1,0:T(8,128)(2,1)S(1)}, u32[]{:S(2)}, u32[]{:S(2)}) collective-permute-start(bf16[64,2048]{1,0:T(8,128)(2,1)S(1)} %add.9), channel_id=1, source_target_pairs={{4,0},{3,1},{8,4},{1,5},{12,8},{5,9},{14,12},{9,13},{10,14},{13,15... | collective-permute-start | bytes 786440 | tf_op jit(solution)/shard_map/ppermute | solution.py:281
  60.4 1.5 %collective-permute-done.23.refs_2_ = bf16[64,2048]{1,0:T(8,128)(2,1)S(1)} collective-permute-done((bf16[64,2048]{1,0:T(8,128)(2,1)S(1)}, bf16[64,2048]{1,0:T(8,128)(2,1)S(1)}, u32[]{:S(2)}, u32[]{:S(2)}) %collective-permute-start.23) | collective-permute-done | bytes 262176 | tf_op jit(solution)/shard_map/ppermute | solution.py:281
  61.9 0.1 add.13
  62.0 2.1 %collective-permute-start.24 = (bf16[64,2048]{1,0:T(8,128)(2,1)S(1)}, bf16[64,2048]{1,0:T(8,128)(2,1)S(1)}, u32[]{:S(2)}, u32[]{:S(2)}) collective-permute-start(bf16[64,2048]{1,0:T(8,128)(2,1)S(1)} %add.13), channel_id=1, source_target_pairs={{4,0},{3,1},{8,4},{1,5},{12,8},{5,9},{14,12},{9,13},{10,14},{13,15... | collective-permute-start | bytes 786440 | tf_op jit(solution)/shard_map/ppermute | solution.py:281
  64.1 0.0 collective-permute-done.5.refs_1_
  64.1 0.6 collective-permute-done.17.refs_2_
  64.8 0.1 add.10
  64.9 0.1 collective-permute-start.18
  64.9 3.5 %collective-permute-done.24.refs_2_ = bf16[64,2048]{1,0:T(8,128)(2,1)S(1)} collective-permute-done((bf16[64,2048]{1,0:T(8,128)(2,1)S(1)}, bf16[64,2048]{1,0:T(8,128)(2,1)S(1)}, u32[]{:S(2)}, u32[]{:S(2)}) %collective-permute-start.24) | collective-permute-done | bytes 262176 | tf_op jit(solution)/shard_map/ppermute | solution.py:281
  68.5 0.1 add.14
  68.6 2.1 %collective-permute-start.25 = (bf16[64,2048]{1,0:T(8,128)(2,1)S(1)}, bf16[64,2048]{1,0:T(8,128)(2,1)S(1)}, u32[]{:S(2)}, u32[]{:S(2)}) collective-permute-start(bf16[64,2048]{1,0:T(8,128)(2,1)S(1)} %add.14), channel_id=1, source_target_pairs={{4,0},{3,1},{8,4},{1,5},{12,8},{5,9},{14,12},{9,13},{10,14},{13,15... | collective-permute-start | bytes 786440 | tf_op jit(solution)/shard_map/ppermute | solution.py:281
  70.6 0.2 collective-permute-done.18.refs_2_
  70.8 4.2 %collective-permute-done.25.refs_3_ = bf16[64,2048]{1,0:T(8,128)(2,1)S(1)} collective-permute-done((bf16[64,2048]{1,0:T(8,128)(2,1)S(1)}, bf16[64,2048]{1,0:T(8,128)(2,1)S(1)}, u32[]{:S(2)}, u32[]{:S(2)}) %collective-permute-start.25) | collective-permute-done | bytes 262176 | tf_op jit(solution)/shard_map/ppermute | solution.py:281
  75.0 0.8 %add.15 = bf16[64,2048]{1,0:T(8,128)(2,1)} custom-call(f32[64,2048]{1,0:T(8,128)S(1)} %get-tuple-element.22.refs_0_, bf16[192,2048]{1,0:T(8,128)(2,1)S(1)} %collective-permute-done.5.refs_1_, bf16[64,2048]{1,0:T(8,128)(2,1)S(1)} %collective-permute-done.18.refs_2_, bf16[64,2048]{1,0:T(8,128)(2,1)S(1)} %collective-permute-done.25.refs_3_), custom_call_target="tpu_custom_call" | custom-call | tf_op jit(solution)/shard_map/add/pallas_call | solution.py:250
  (2 shorter events, 0.1 us)
Async XLA Ops:
  1.4 8.9 %collective-permute-start = (bf16[65,16,128]{2,1,0:T(8,128)(2,1)S(1)}, bf16[65,16,128]{2,1,0:T(8,128)(2,1)S(1)}, u32[]{:S(2)}, u32[]{:S(2)}) collective-permute-start(bf16[65,16,128]{2,1,0:T(8,128)(2,1)S(1)} %get-tuple-element.21.own_ref), channel_id=1, source_target_pairs={{0,4},{1,3},{4,8},{5,1},{8,12},{9,5},{12,14},{13,9},{14,10},{15,13... | collective-permute-start | bytes 798728 | tf_op jit(solution)/shard_map/ppermute | solution.py:281
  4.6 8.3 %collective-permute-start.1 = (bf16[65,16,128]{2,1,0:T(8,128)(2,1)S(1)}, bf16[65,16,128]{2,1,0:T(8,128)(2,1)S(1)}, u32[]{:S(2)}, u32[]{:S(2)}) collective-permute-start(bf16[65,16,128]{2,1,0:T(8,128)(2,1)S(1)} %get-tuple-element.21.own_ref), channel_id=1, source_target_pairs={{1,4},{0,3},{5,8},{4,1},{9,12},{8,5},{13,14},{12,9},{15,10},{14,13... | collective-permute-start | bytes 798728 | tf_op jit(solution)/shard_map/ppermute | solution.py:281
  10.3 7.8 %collective-permute-start.6 = (bf16[65,16,128]{2,1,0:T(8,128)(2,1)S(1)}, bf16[65,16,128]{2,1,0:T(8,128)(2,1)S(1)}, u32[]{:S(2)}, u32[]{:S(2)}) collective-permute-start(bf16[65,16,128]{2,1,0:T(8,128)(2,1)S(1)} %collective-permute-done.refs_1_), channel_id=1, source_target_pairs={{0,4},{1,3},{4,8},{5,1},{8,12},{9,5},{12,14},{13,9},{14,10},{15,13... | collective-permute-start | bytes 798728 | tf_op jit(solution)/shard_map/ppermute | solution.py:281
  12.8 8.2 %collective-permute-start.7 = (bf16[65,16,128]{2,1,0:T(8,128)(2,1)S(1)}, bf16[65,16,128]{2,1,0:T(8,128)(2,1)S(1)}, u32[]{:S(2)}, u32[]{:S(2)}) collective-permute-start(bf16[65,16,128]{2,1,0:T(8,128)(2,1)S(1)} %collective-permute-done.1.refs_2_), channel_id=1, source_target_pairs={{0,4},{1,3},{4,8},{5,1},{8,12},{9,5},{12,14},{13,9},{14,10},{15,13... | collective-permute-start | bytes 798728 | tf_op jit(solution)/shard_map/ppermute | solution.py:281
  18.2 6.4 %collective-permute-start.11 = (bf16[65,16,128]{2,1,0:T(8,128)(2,1)S(1)}, bf16[65,16,128]{2,1,0:T(8,128)(2,1)S(1)}, u32[]{:S(2)}, u32[]{:S(2)}) collective-permute-start(bf16[65,16,128]{2,1,0:T(8,128)(2,1)S(1)} %collective-permute-done.6.refs_1_), channel_id=1, source_target_pairs={{0,4},{1,3},{4,8},{5,1},{8,12},{9,5},{12,14},{13,9},{14,10},{15,13... | collective-permute-start | bytes 798728 | tf_op jit(solution)/shard_map/ppermute | solution.py:281
  21.0 6.4 %collective-permute-start.12 = (bf16[65,16,128]{2,1,0:T(8,128)(2,1)S(1)}, bf16[65,16,128]{2,1,0:T(8,128)(2,1)S(1)}, u32[]{:S(2)}, u32[]{:S(2)}) collective-permute-start(bf16[65,16,128]{2,1,0:T(8,128)(2,1)S(1)} %collective-permute-done.7.refs_2_), channel_id=1, source_target_pairs={{0,4},{1,3},{4,8},{5,1},{8,12},{9,5},{12,14},{13,9},{14,10},{15,13... | collective-permute-start | bytes 798728 | tf_op jit(solution)/shard_map/ppermute | solution.py:281
  24.6 6.4 %collective-permute-start.19 = (bf16[65,16,128]{2,1,0:T(8,128)(2,1)S(1)}, bf16[65,16,128]{2,1,0:T(8,128)(2,1)S(1)}, u32[]{:S(2)}, u32[]{:S(2)}) collective-permute-start(bf16[65,16,128]{2,1,0:T(8,128)(2,1)S(1)} %collective-permute-done.11.refs_1_), channel_id=1, source_target_pairs={{0,4},{1,3},{4,8},{5,1},{8,12},{9,5},{12,14},{13,9},{14,10},{15,13... | collective-permute-start | bytes 798728 | tf_op jit(solution)/shard_map/ppermute | solution.py:281
  25.7 10.7 %collective-permute-start.13 = (bf16[65,16,128]{2,1,0:T(8,128)(2,1)S(1)}, bf16[65,16,128]{2,1,0:T(8,128)(2,1)S(1)}, u32[]{:S(2)}, u32[]{:S(2)}) collective-permute-start(bf16[65,16,128]{2,1,0:T(8,128)(2,1)S(1)} %collective-permute-done.11.refs_1_), channel_id=1, source_target_pairs={{0,1},{1,0},{2,3},{3,2},{4,5},{5,4},{6,7},{7,6},{8,9},{9,8},{10,11... | collective-permute-start | bytes 798728 | tf_op jit(solution)/shard_map/ppermute | solution.py:281
  27.4 9.0 %collective-permute-start.14 = (bf16[65,16,128]{2,1,0:T(8,128)(2,1)S(1)}, bf16[65,16,128]{2,1,0:T(8,128)(2,1)S(1)}, u32[]{:S(2)}, u32[]{:S(2)}) collective-permute-start(bf16[65,16,128]{2,1,0:T(8,128)(2,1)S(1)} %collective-permute-done.12.refs_2_), channel_id=1, source_target_pairs={{0,1},{1,0},{2,3},{3,2},{4,5},{5,4},{6,7},{7,6},{8,9},{9,8},{10,11... | collective-permute-start | bytes 798728 | tf_op jit(solution)/shard_map/ppermute | solution.py:281
  27.4 14.4 %collective-permute-start.4 = (bf16[65,16,128]{2,1,0:T(8,128)(2,1)S(1)}, bf16[65,16,128]{2,1,0:T(8,128)(2,1)S(1)}, u32[]{:S(2)}, u32[]{:S(2)}) collective-permute-start(bf16[65,16,128]{2,1,0:T(8,128)(2,1)S(1)} %get-tuple-element.21.own_ref), channel_id=1, source_target_pairs={{0,1},{1,0},{2,3},{3,2},{4,5},{5,4},{6,7},{7,6},{8,9},{9,8},{10,11... | collective-permute-start | bytes 798728 | tf_op jit(solution)/shard_map/ppermute | solution.py:281
  31.0 8.6 %collective-permute-start.20 = (bf16[65,16,128]{2,1,0:T(8,128)(2,1)S(1)}, bf16[65,16,128]{2,1,0:T(8,128)(2,1)S(1)}, u32[]{:S(2)}, u32[]{:S(2)}) collective-permute-start(bf16[65,16,128]{2,1,0:T(8,128)(2,1)S(1)} %collective-permute-done.19.refs_1_), channel_id=1, source_target_pairs={{0,1},{1,0},{2,3},{3,2},{4,5},{5,4},{6,7},{7,6},{8,9},{9,8},{10,11... | collective-permute-start | bytes 798728 | tf_op jit(solution)/shard_map/ppermute | solution.py:281
  35.8 6.5 %collective-permute-start.2 = (bf16[65,16,128]{2,1,0:T(8,128)(2,1)S(1)}, bf16[65,16,128]{2,1,0:T(8,128)(2,1)S(1)}, u32[]{:S(2)}, u32[]{:S(2)}) collective-permute-start(bf16[65,16,128]{2,1,0:T(8,128)(2,1)S(1)} %collective-permute-done.refs_1_), channel_id=1, source_target_pairs={{0,1},{1,0},{2,3},{3,2},{4,5},{5,4},{6,7},{7,6},{8,9},{9,8},{10,11... | collective-permute-start | bytes 798728 | tf_op jit(solution)/shard_map/ppermute | solution.py:281
  36.4 6.0 %collective-permute-start.3 = (bf16[65,16,128]{2,1,0:T(8,128)(2,1)S(1)}, bf16[65,16,128]{2,1,0:T(8,128)(2,1)S(1)}, u32[]{:S(2)}, u32[]{:S(2)}) collective-permute-start(bf16[65,16,128]{2,1,0:T(8,128)(2,1)S(1)} %collective-permute-done.1.refs_2_), channel_id=1, source_target_pairs={{0,1},{1,0},{2,3},{3,2},{4,5},{5,4},{6,7},{7,6},{8,9},{9,8},{10,11... | collective-permute-start | bytes 798728 | tf_op jit(solution)/shard_map/ppermute | solution.py:281
  36.4 9.3 %collective-permute-start.8 = (bf16[65,16,128]{2,1,0:T(8,128)(2,1)S(1)}, bf16[65,16,128]{2,1,0:T(8,128)(2,1)S(1)}, u32[]{:S(2)}, u32[]{:S(2)}) collective-permute-start(bf16[65,16,128]{2,1,0:T(8,128)(2,1)S(1)} %collective-permute-done.6.refs_1_), channel_id=1, source_target_pairs={{0,1},{1,0},{2,3},{3,2},{4,5},{5,4},{6,7},{7,6},{8,9},{9,8},{10,11... | collective-permute-start | bytes 798728 | tf_op jit(solution)/shard_map/ppermute | solution.py:281
  39.6 6.1 %collective-permute-start.9 = (bf16[65,16,128]{2,1,0:T(8,128)(2,1)S(1)}, bf16[65,16,128]{2,1,0:T(8,128)(2,1)S(1)}, u32[]{:S(2)}, u32[]{:S(2)}) collective-permute-start(bf16[65,16,128]{2,1,0:T(8,128)(2,1)S(1)} %collective-permute-done.7.refs_2_), channel_id=1, source_target_pairs={{0,1},{1,0},{2,3},{3,2},{4,5},{5,4},{6,7},{7,6},{8,9},{9,8},{10,11... | collective-permute-start | bytes 798728 | tf_op jit(solution)/shard_map/ppermute | solution.py:281
  41.8 9.3 %collective-permute-start.15 = (bf16[128,2048]{1,0:T(8,128)(2,1)S(1)}, bf16[128,2048]{1,0:T(8,128)(2,1)S(1)}, u32[]{:S(2)}, u32[]{:S(2)}) collective-permute-start(bf16[128,2048]{1,0:T(8,128)(2,1)S(1)} %get-tuple-element.29), channel_id=1, source_target_pairs={{0,1},{1,0},{2,3},{3,2},{4,5},{5,4},{6,7},{7,6},{8,9},{9,8},{10,11... | collective-permute-start | bytes 1572872 | tf_op jit(solution)/shard_map/ppermute | solution.py:281
  42.3 6.7 %collective-permute-start.21 = (bf16[64,2048]{1,0:T(8,128)(2,1)S(1)}, bf16[64,2048]{1,0:T(8,128)(2,1)S(1)}, u32[]{:S(2)}, u32[]{:S(2)}) collective-permute-start(bf16[64,2048]{1,0:T(8,128)(2,1)S(1)} %get-tuple-element.34), channel_id=1, source_target_pairs={{0,1},{1,0},{2,3},{3,2},{4,5},{5,4},{6,7},{7,6},{8,9},{9,8},{10,11... | collective-permute-start | bytes 786440 | tf_op jit(solution)/shard_map/ppermute | solution.py:281
  48.5 9.1 %collective-permute-start.10 = (bf16[128,2048]{1,0:T(8,128)(2,1)S(1)}, bf16[128,2048]{1,0:T(8,128)(2,1)S(1)}, u32[]{:S(2)}, u32[]{:S(2)}) collective-permute-start(bf16[128,2048]{1,0:T(8,128)(2,1)S(1)} %get-tuple-element.27), channel_id=1, source_target_pairs={{0,1},{1,0},{2,3},{3,2},{4,5},{5,4},{6,7},{7,6},{8,9},{9,8},{10,11... | collective-permute-start | bytes 1572872 | tf_op jit(solution)/shard_map/ppermute | solution.py:281
  49.0 6.4 %collective-permute-start.22 = (bf16[64,2048]{1,0:T(8,128)(2,1)S(1)}, bf16[64,2048]{1,0:T(8,128)(2,1)S(1)}, u32[]{:S(2)}, u32[]{:S(2)}) collective-permute-start(bf16[64,2048]{1,0:T(8,128)(2,1)S(1)} %add.11), channel_id=1, source_target_pairs={{4,0},{3,1},{8,4},{1,5},{12,8},{5,9},{14,12},{9,13},{10,14},{13,15... | collective-permute-start | bytes 786440 | tf_op jit(solution)/shard_map/ppermute | solution.py:281
  51.1 13.0 %collective-permute-start.5 = (bf16[192,2048]{1,0:T(8,128)(2,1)S(1)}, bf16[192,2048]{1,0:T(8,128)(2,1)S(1)}, u32[]{:S(2)}, u32[]{:S(2)}) collective-permute-start(bf16[192,2048]{1,0:T(8,128)(2,1)S(1)} %get-tuple-element.24), channel_id=1, source_target_pairs={{0,1},{1,0},{2,3},{3,2},{4,5},{5,4},{6,7},{7,6},{8,9},{9,8},{10,11... | collective-permute-start | bytes 2359304 | tf_op jit(solution)/shard_map/ppermute | solution.py:281
  51.1 7.1 %collective-permute-start.16 = (bf16[64,2048]{1,0:T(8,128)(2,1)S(1)}, bf16[64,2048]{1,0:T(8,128)(2,1)S(1)}, u32[]{:S(2)}, u32[]{:S(2)}) collective-permute-start(bf16[64,2048]{1,0:T(8,128)(2,1)S(1)} %add.8), channel_id=1, source_target_pairs={{4,0},{3,1},{8,4},{1,5},{12,8},{5,9},{14,12},{9,13},{10,14},{13,15... | collective-permute-start | bytes 786440 | tf_op jit(solution)/shard_map/ppermute | solution.py:281
  55.5 6.4 %collective-permute-start.23 = (bf16[64,2048]{1,0:T(8,128)(2,1)S(1)}, bf16[64,2048]{1,0:T(8,128)(2,1)S(1)}, u32[]{:S(2)}, u32[]{:S(2)}) collective-permute-start(bf16[64,2048]{1,0:T(8,128)(2,1)S(1)} %add.12), channel_id=1, source_target_pairs={{4,0},{3,1},{8,4},{1,5},{12,8},{5,9},{14,12},{9,13},{10,14},{13,15... | collective-permute-start | bytes 786440 | tf_op jit(solution)/shard_map/ppermute | solution.py:281
  58.3 6.4 %collective-permute-start.17 = (bf16[64,2048]{1,0:T(8,128)(2,1)S(1)}, bf16[64,2048]{1,0:T(8,128)(2,1)S(1)}, u32[]{:S(2)}, u32[]{:S(2)}) collective-permute-start(bf16[64,2048]{1,0:T(8,128)(2,1)S(1)} %add.9), channel_id=1, source_target_pairs={{4,0},{3,1},{8,4},{1,5},{12,8},{5,9},{14,12},{9,13},{10,14},{13,15... | collective-permute-start | bytes 786440 | tf_op jit(solution)/shard_map/ppermute | solution.py:281
  62.0 6.4 %collective-permute-start.24 = (bf16[64,2048]{1,0:T(8,128)(2,1)S(1)}, bf16[64,2048]{1,0:T(8,128)(2,1)S(1)}, u32[]{:S(2)}, u32[]{:S(2)}) collective-permute-start(bf16[64,2048]{1,0:T(8,128)(2,1)S(1)} %add.13), channel_id=1, source_target_pairs={{4,0},{3,1},{8,4},{1,5},{12,8},{5,9},{14,12},{9,13},{10,14},{13,15... | collective-permute-start | bytes 786440 | tf_op jit(solution)/shard_map/ppermute | solution.py:281
  64.9 6.0 %collective-permute-start.18 = (bf16[64,2048]{1,0:T(8,128)(2,1)S(1)}, bf16[64,2048]{1,0:T(8,128)(2,1)S(1)}, u32[]{:S(2)}, u32[]{:S(2)}) collective-permute-start(bf16[64,2048]{1,0:T(8,128)(2,1)S(1)} %add.10), channel_id=1, source_target_pairs={{4,1},{3,0},{8,5},{1,4},{12,9},{5,8},{14,13},{9,12},{10,15},{13,14... | collective-permute-start | bytes 786440 | tf_op jit(solution)/shard_map/ppermute | solution.py:281
  68.6 6.4 %collective-permute-start.25 = (bf16[64,2048]{1,0:T(8,128)(2,1)S(1)}, bf16[64,2048]{1,0:T(8,128)(2,1)S(1)}, u32[]{:S(2)}, u32[]{:S(2)}) collective-permute-start(bf16[64,2048]{1,0:T(8,128)(2,1)S(1)} %add.14), channel_id=1, source_target_pairs={{4,0},{3,1},{8,4},{1,5},{12,8},{5,9},{14,12},{9,13},{10,14},{13,15... | collective-permute-start | bytes 786440 | tf_op jit(solution)/shard_map/ppermute | solution.py:281

commit v4 on v3

--- a/solution.py
+++ b/solution.py
@@ -25,8 +25,32 @@
         self.groups = local_tokens // SUBS
         self.per_tile = max(1, LANES // (2 * experts))
         self.gate_tiles = pl.cdiv(self.groups, self.per_tile)
-        self.token_tiles = self.groups * self.cols
-        self.tiles = self.token_tiles + self.gate_tiles
+        self.half = self.groups // 2
+        self.split = self.half * self.cols
+        self.tiles = self.groups * self.cols + self.gate_tiles
+
+    def tile(self, group):
+        return group * self.cols + (self.gate_tiles if group >= self.half else 0)
+
+    def cut(self, packed, part):
+        if part == "first":
+            return packed[: self.split + self.gate_tiles]
+        return packed[self.split :]
+
+    def pieces(self, part):
+        picked = range(self.groups)
+        shift = 0
+        if part == "first":
+            picked = range(self.half)
+        elif part == "second":
+            picked, shift = range(self.half, self.groups), self.split
+        return [
+            (self.tile(g) - shift, self.split - shift + g // self.per_tile, g % self.per_tile)
+            for g in picked
+        ]
+
+    def rows(self, part):
+        return SUBS * len(self.pieces(part))
 
 
 def pack_body(pk, capacity, devices, me_ref, *refs):
@@ -42,7 +66,7 @@
     tokens_ref, ids_ref, gates_ref, home_ref, spare_ref = scratch
     for group in range(pk.groups):
         for col in range(pk.cols):
-            out_ref[group * pk.cols + col] = tokens_ref[
+            out_ref[pk.tile(group) + col] = tokens_ref[
                 group * SUBS : (group + 1) * SUBS, col * LANES : (col + 1) * LANES
             ]
     rows = pk.local_tokens
@@ -81,7 +105,7 @@
             group = index * pk.per_tile + part
             if group < pk.groups:
                 tile = jnp.where(slot == part, value[group * SUBS : (group + 1) * SUBS], tile)
-        out_ref[pk.token_tiles + index] = tile.astype(jnp.bfloat16)
+        out_ref[pk.split + index] = tile.astype(jnp.bfloat16)
 
 
 def pack(pk, capacity, devices, me, tokens, ids, gates, home, spare):
@@ -102,14 +126,13 @@
     )(me, *[pltpu.with_memory_space_constraint(x, pltpu.HBM) for x in sources])
 
 
-def gather_rows(pk, buffers, x_ref):
-    for index, buffer in enumerate(buffers):
-        for group in range(pk.groups):
-            row = index * pk.local_tokens + group * SUBS
+def gather_rows(pk, buffers, parts, x_ref):
+    row = 0
+    for buffer, part in zip(buffers, parts):
+        for first, _, _ in pk.pieces(part):
             for col in range(pk.cols):
-                x_ref[row : row + SUBS, col * LANES : (col + 1) * LANES] = buffer[
-                    group * pk.cols + col
-                ]
+                x_ref[row : row + SUBS, col * LANES : (col + 1) * LANES] = buffer[first + col]
+            row += SUBS
 
 
 def activate(gate, up):
@@ -122,14 +145,14 @@
     )
 
 
-def store_scaled(pk, mine_ref, buffers, answers, out_refs):
+def store_scaled(pk, mine_ref, buffers, parts, answers, out_refs):
     lane = lax.broadcasted_iota(jnp.int32, (SUBS, LANES), 1)
     scales = []
-    for buffer in buffers:
-        for group in range(pk.groups):
-            place = (group % pk.per_tile) * 2 * pk.experts + mine_ref[...]
+    for buffer, part in zip(buffers, parts):
+        for _, gate_tile, slot in pk.pieces(part):
+            place = slot * 2 * pk.experts + mine_ref[...]
             wanted = (lane == place) | (lane == place + pk.experts)
-            table = buffer[pk.token_tiles + group // pk.per_tile].astype(jnp.float32)
+            table = buffer[gate_tile].astype(jnp.float32)
             scales.append(jnp.sum(jnp.where(wanted, table, 0.0), axis=1, keepdims=True))
     row = 0
     for out_ref in out_refs:
@@ -151,7 +174,7 @@
             )
             copy.start()
             copies.append(copy)
-    gather_rows(pk, [own_ref], x_ref)
+    gather_rows(pk, [own_ref], ["all"], x_ref)
     rows = x_ref[...]
     for j in range(THIRD):
         for part in range(THIRD):
@@ -171,7 +194,7 @@
             acc_ref[...] = part
         else:
             acc_ref[...] += part
-    store_scaled(pk, mine_ref, [own_ref], acc_ref, [keep_ref])
+    store_scaled(pk, mine_ref, [own_ref], ["all"], acc_ref, [keep_ref])
 
 
 def first_chunk(pk, weights, mine, own):
@@ -200,29 +223,32 @@
     )(mine, own, pltpu.with_memory_space_constraint(weights, pltpu.HBM))
 
 
-def chunk_body(pk, width, count, *refs):
+def chunk_body(pk, width, parts, *refs):
     mine_ref = refs[0]
+    count = len(parts)
     buffers = refs[1 : 1 + count]
     weights_ref = refs[1 + count]
     out_refs = refs[2 + count : -1]
     x_ref = refs[-1]
-    gather_rows(pk, buffers, x_ref)
+    gather_rows(pk, buffers, parts, x_ref)
     rows = x_ref[...]
     gate = jnp.dot(rows, weights_ref[:, :width], preferred_element_type=jnp.float32)
     up = jnp.dot(rows, weights_ref[:, width : 2 * width], preferred_element_type=jnp.float32)
     answers = down(activate(gate, up), weights_ref[:, 2 * width :])
-    store_scaled(pk, mine_ref, buffers, answers, out_refs)
+    store_scaled(pk, mine_ref, buffers, parts, answers, out_refs)
 
 
 def chunk(pk, weights, mine, own, crossed):
     width = weights.shape[1] // THIRD
-    rows, feature = pk.local_tokens, pk.feature
-    buffers = own + crossed
-    total = rows * len(buffers)
+    feature = pk.feature
+    buffers = [buffer for buffer, _ in own + crossed]
+    parts = [part for _, part in own + crossed]
+    given = sum(pk.rows(part) for _, part in crossed)
+    total = sum(pk.rows(part) for part in parts)
     return pl.pallas_call(
-        functools.partial(chunk_body, pk, width, len(buffers)),
-        out_shape=[jax.ShapeDtypeStruct((rows, feature), jnp.float32) for _ in own]
-        + [jax.ShapeDtypeStruct((rows * len(crossed), feature), jnp.bfloat16)],
+        functools.partial(chunk_body, pk, width, parts),
+        out_shape=[jax.ShapeDtypeStruct((pk.rows(part), feature), jnp.float32) for _, part in own]
+        + [jax.ShapeDtypeStruct((given, feature), jnp.bfloat16)],
         in_specs=[VMEM] * (len(buffers) + 2),
         out_specs=[VMEM] * (len(own) + 1),
         scratch_shapes=[pltpu.VMEM((total, feature), jnp.bfloat16)],
@@ -236,19 +262,27 @@
     )(mine, *buffers, weights)
 
 
-def add_body(starts, *refs):
+def add_body(places, *refs):
     out_ref = refs[-1]
     rows = out_ref.shape[0]
-    total = refs[0][starts[0] : starts[0] + rows, :].astype(jnp.float32)
-    for ref, start in zip(refs[1:-1], starts[1:]):
-        total = total + ref[start : start + rows, :].astype(jnp.float32)
-    out_ref[...] = total.astype(out_ref.dtype)
+    cuts = {0, rows}
+    for ref, (there, here) in zip(refs, places):
+        cuts |= {here, min(rows, here + ref.shape[0] - there)}
+    cuts = sorted(cuts)
+    for low, high in zip(cuts, cuts[1:]):
+        total = None
+        for ref, (there, here) in zip(refs, places):
+            if here <= low and high - here + there <= ref.shape[0]:
+                start = there + low - here
+                term = ref[start : start + high - low, :].astype(jnp.float32)
+                total = term if total is None else total + term
+        out_ref[low:high, :] = total.astype(out_ref.dtype)
 
 
 def add(rows, dtype, terms):
-    arrays = [array for array, _ in terms]
+    arrays = [array for array, _, _ in terms]
     return pl.pallas_call(
-        functools.partial(add_body, [start for _, start in terms]),
+        functools.partial(add_body, [(there, here) for _, there, here in terms]),
         out_shape=jax.ShapeDtypeStruct((rows, arrays[0].shape[1]), dtype),
         in_specs=[VMEM] * len(arrays),
         out_specs=VMEM,
@@ -288,31 +322,38 @@
     keep, gave = {}, {}
     a, b = send(packed, straight), send(packed, crossing)
     keep_own, weights = first_chunk(pk, expert_weights, mine, packed)
-    other = [send(packed, pair)]
+    other = [(send(packed, pair), "all")]
     for r in range(1, far):
         xa, xb = send(a, pair), send(b, pair)
-        keep_a, keep_b, give = chunk(pk, weights, mine, [a, b], [xa, xb] + other)
+        keep_a, keep_b, give = chunk(
+            pk, weights, mine, [(a, "all"), (b, "all")], [(xa, "all"), (xb, "all")] + other
+        )
         other = []
         keep[r] = (keep_a, keep_b)
         gave[r] = send(give, pair)
-        a = send(a, straight)
-        if r + 1 < far:
-            b = send(b, straight)
-    xa = send(a, pair)
-    keep_a, give = chunk(pk, weights, mine, [a], [xa])
+        if r + 1 == far:
+            a, b = pk.cut(a, "first"), pk.cut(b, "second")
+        a, b = send(a, straight), send(b, straight)
+    xa, xb = send(a, pair), send(b, pair)
+    keep_a, keep_b, give = chunk(
+        pk, weights, mine, [(a, "first"), (b, "second")], [(xa, "first"), (xb, "second")]
+    )
     gave[far] = send(give, pair)
 
-    half = local_tokens
-    a = add(half, wire, [(keep_a, 0), (gave[far], 0)])
-    a, b = [(send(a, straight_back), 0)], []
+    rows = local_tokens
+    first, second = pk.rows("first"), pk.rows("second")
+    a = add(first, wire, [(keep_a, 0, 0), (gave[far], 0, 0)])
+    a = [(send(a, straight_back), 0, 0)]
+    b = add(second, wire, [(keep_b, 0, 0), (gave[far], first, 0)])
+    b = [(send(b, straight_back), 0, first)]
     for r in range(far - 1, 0, -1):
         keep_a, keep_b = keep[r]
-        b = add(half, wire, [(keep_b, 0), (gave[r], half)] + b)
-        b = [(send(b, straight_back if r > 1 else crossing_back), 0)]
-        a = add(half, wire, [(keep_a, 0), (gave[r], 0)] + a)
-        a = [(send(a, straight_back), 0)]
-    terms = [(keep_own, 0), (gave[1], 2 * half)] + b + a
-    return add(half, jnp.bfloat16, terms)
+        a = add(rows, wire, [(keep_a, 0, 0), (gave[r], 0, 0)] + a)
+        a = [(send(a, straight_back), 0, 0)]
+        b = add(rows, wire, [(keep_b, 0, 0), (gave[r], rows, 0)] + b)
+        b = [(send(b, straight_back if r > 1 else crossing_back), 0, 0)]
+    terms = [(keep_own, 0, 0), (gave[1], 2 * rows, 0)] + a + b
+    return add(rows, jnp.bfloat16, terms)
 
 
 def solution(mesh):

time: 75.9 us -> 77.1 us (1.016)
  the two profiles are of different devices: /device:TPU:0 before, /device:TPU:13 now
where the time goes in v4:
time: 77.1 us; the launch traced here: 75.7 us
  waiting for transfers between devices  30.9 us (40%)
  starting transfers between devices  26.3 us (34%)
  Pallas kernels  18.3 us (24%)
    ppermute x29, waiting for transfers between devices, send(): return lax.ppermute(x, 'ep', where)  30.9 us
    ppermute x29, starting transfers between devices, send(): return lax.ppermute(x, 'ep', where)  26.3 us
    pallas_call x4, Pallas kernels, chunk(): pl.pallas_call(functools.partial(chunk_body, pk, width, parts), out_shape...  10.8 us
    pallas_call x1, Pallas kernels, first_chunk(): pl.pallas_call(functools.partial(first_body, pk, width), out_shape=[pltpu...  4.78 us
  transfers between devices with their start and end apart: 29, of which 12 were waited for; matrix products, arithmetic and copies ran while one was open for 0% of the time, Pallas kernels for 21%

profile of v4, /device:TPU:13, one launch (start us, length us, event | category | flops | bytes accessed | tf_op | source)
XLA Modules:
  0.0 75.7 jit_solution(4364332774317601391)
XLA Ops:
  0.0 1.4 %pack.1 = (bf16[65,16,128]{2,1,0:T(8,128)(2,1)S(1)}, s32[16,128]{1,0:T(8,128)S(1)}) custom-call(s32[1]{0:T(128)} %bitcast.me_ref, bf16[64,2048]{1,0:T(8,128)(2,1)} %refs_0_.1, s32[8,64]{1,0:T(8,128)} %bitcast.3, f32[8,64]{1,0:T(8,128)} %bitcast.4, s32[16]{0:T(128)} %refs_3_.1, s32[16]{0:T(128)} %refs_4_.1), custom_call_target="tpu_custom_call" | custom-call | tf_op jit(solution)/shard_map/pack/pallas_call | solution.py:114
  1.4 1.3 %collective-permute-start = (bf16[65,16,128]{2,1,0:T(8,128)(2,1)S(1)}, bf16[65,16,128]{2,1,0:T(8,128)(2,1)S(1)}, u32[]{:S(2)}, u32[]{:S(2)}) collective-permute-start(bf16[65,16,128]{2,1,0:T(8,128)(2,1)S(1)} %get-tuple-element.22.own_ref), channel_id=1, source_target_pairs={{0,4},{1,3},{4,8},{5,1},{8,12},{9,5},{12,14},{13,9},{14,10},{15,13... | collective-permute-start | bytes 798728 | tf_op jit(solution)/shard_map/ppermute | solution.py:315
  2.8 0.0 collective-permute-start.1
  2.8 5.2 %collective-permute-done.refs_1_ = bf16[65,16,128]{2,1,0:T(8,128)(2,1)S(1)} collective-permute-done((bf16[65,16,128]{2,1,0:T(8,128)(2,1)S(1)}, bf16[65,16,128]{2,1,0:T(8,128)(2,1)S(1)}, u32[]{:S(2)}, u32[]{:S(2)}) %collective-permute-start) | collective-permute-done | bytes 266272 | tf_op jit(solution)/shard_map/ppermute | solution.py:315
  8.0 1.5 %collective-permute-start.6 = (bf16[65,16,128]{2,1,0:T(8,128)(2,1)S(1)}, bf16[65,16,128]{2,1,0:T(8,128)(2,1)S(1)}, u32[]{:S(2)}, u32[]{:S(2)}) collective-permute-start(bf16[65,16,128]{2,1,0:T(8,128)(2,1)S(1)} %collective-permute-done.refs_1_), channel_id=1, source_target_pairs={{0,4},{1,3},{4,8},{5,1},{8,12},{9,5},{12,14},{13,9},{14,10},{15,13... | collective-permute-start | bytes 798728 | tf_op jit(solution)/shard_map/ppermute | solution.py:315
  9.5 0.4 collective-permute-done.1.refs_2_
  9.9 1.8 %collective-permute-start.7 = (bf16[65,16,128]{2,1,0:T(8,128)(2,1)S(1)}, bf16[65,16,128]{2,1,0:T(8,128)(2,1)S(1)}, u32[]{:S(2)}, u32[]{:S(2)}) collective-permute-start(bf16[65,16,128]{2,1,0:T(8,128)(2,1)S(1)} %collective-permute-done.1.refs_2_), channel_id=1, source_target_pairs={{0,4},{1,3},{4,8},{5,1},{8,12},{9,5},{12,14},{13,9},{14,10},{15,13... | collective-permute-start | bytes 798728 | tf_op jit(solution)/shard_map/ppermute | solution.py:315
  11.7 1.6 %collective-permute-done.6.refs_1_ = bf16[65,16,128]{2,1,0:T(8,128)(2,1)S(1)} collective-permute-done((bf16[65,16,128]{2,1,0:T(8,128)(2,1)S(1)}, bf16[65,16,128]{2,1,0:T(8,128)(2,1)S(1)}, u32[]{:S(2)}, u32[]{:S(2)}) %collective-permute-start.6) | collective-permute-done | bytes 266272 | tf_op jit(solution)/shard_map/ppermute | solution.py:315
  13.3 1.8 %collective-permute-start.11 = (bf16[65,16,128]{2,1,0:T(8,128)(2,1)S(1)}, bf16[65,16,128]{2,1,0:T(8,128)(2,1)S(1)}, u32[]{:S(2)}, u32[]{:S(2)}) collective-permute-start(bf16[65,16,128]{2,1,0:T(8,128)(2,1)S(1)} %collective-permute-done.6.refs_1_), channel_id=1, source_target_pairs={{0,4},{1,3},{4,8},{5,1},{8,12},{9,5},{12,14},{13,9},{14,10},{15,13... | collective-permute-start | bytes 798728 | tf_op jit(solution)/shard_map/ppermute | solution.py:315
  15.1 1.4 %collective-permute-done.7.refs_2_ = bf16[65,16,128]{2,1,0:T(8,128)(2,1)S(1)} collective-permute-done((bf16[65,16,128]{2,1,0:T(8,128)(2,1)S(1)}, bf16[65,16,128]{2,1,0:T(8,128)(2,1)S(1)}, u32[]{:S(2)}, u32[]{:S(2)}) %collective-permute-start.7) | collective-permute-done | bytes 266272 | tf_op jit(solution)/shard_map/ppermute | solution.py:315
  16.5 1.5 %collective-permute-start.12 = (bf16[65,16,128]{2,1,0:T(8,128)(2,1)S(1)}, bf16[65,16,128]{2,1,0:T(8,128)(2,1)S(1)}, u32[]{:S(2)}, u32[]{:S(2)}) collective-permute-start(bf16[65,16,128]{2,1,0:T(8,128)(2,1)S(1)} %collective-permute-done.7.refs_2_), channel_id=1, source_target_pairs={{0,4},{1,3},{4,8},{5,1},{8,12},{9,5},{12,14},{13,9},{14,10},{15,13... | collective-permute-start | bytes 798728 | tf_op jit(solution)/shard_map/ppermute | solution.py:315
  17.9 3.2 %collective-permute-start.8 = (bf16[65,16,128]{2,1,0:T(8,128)(2,1)S(1)}, bf16[65,16,128]{2,1,0:T(8,128)(2,1)S(1)}, u32[]{:S(2)}, u32[]{:S(2)}) collective-permute-start(bf16[65,16,128]{2,1,0:T(8,128)(2,1)S(1)} %collective-permute-done.6.refs_1_), channel_id=1, source_target_pairs={{0,1},{1,0},{2,3},{3,2},{4,5},{5,4},{6,7},{7,6},{8,9},{9,8},{10,11... | collective-permute-start | bytes 798728 | tf_op jit(solution)/shard_map/ppermute | solution.py:315
  21.2 0.0 collective-permute-start.9
  21.2 0.5 collective-permute-start.4
  21.7 0.0 collective-permute-done.11.refs_1_
  21.7 2.6 %collective-permute-start.13 = (bf16[65,16,128]{2,1,0:T(8,128)(2,1)S(1)}, bf16[65,16,128]{2,1,0:T(8,128)(2,1)S(1)}, u32[]{:S(2)}, u32[]{:S(2)}) collective-permute-start(bf16[65,16,128]{2,1,0:T(8,128)(2,1)S(1)} %collective-permute-done.11.refs_1_), channel_id=1, source_target_pairs={{0,1},{1,0},{2,3},{3,2},{4,5},{5,4},{6,7},{7,6},{8,9},{9,8},{10,11... | collective-permute-start | bytes 798728 | tf_op jit(solution)/shard_map/ppermute | solution.py:315
  24.3 0.0 collective-permute-done.12.refs_2_
  24.3 2.8 %collective-permute-start.14 = (bf16[65,16,128]{2,1,0:T(8,128)(2,1)S(1)}, bf16[65,16,128]{2,1,0:T(8,128)(2,1)S(1)}, u32[]{:S(2)}, u32[]{:S(2)}) collective-permute-start(bf16[65,16,128]{2,1,0:T(8,128)(2,1)S(1)} %collective-permute-done.12.refs_2_), channel_id=1, source_target_pairs={{0,1},{1,0},{2,3},{3,2},{4,5},{5,4},{6,7},{7,6},{8,9},{9,8},{10,11... | collective-permute-start | bytes 798728 | tf_op jit(solution)/shard_map/ppermute | solution.py:315
  27.1 4.8 %first_chunk.1 = (f32[64,2048]{1,0:T(8,128)S(1)}, bf16[2048,2304]{1,0:T(8,128)(2,1)S(1)}) custom-call(s32[16,128]{1,0:T(8,128)S(1)} %get-tuple-element.21.mine_ref.refs_0_, bf16[65,16,128]{2,1,0:T(8,128)(2,1)S(1)} %get-tuple-element.22.own_ref, bf16[1,2048,3072]{2,1,0:T(8,128)(2,1)} %weights_ref.1), custom_call_target="tpu_custom_call" | custom-call | flops 603979776 | bytes 9437184 | tf_op jit(solution)/shard_map/first_chunk/pallas_call | solution.py:203
  32.0 0.0 collective-permute-done.8.refs_3_
  32.0 1.2 %collective-permute-start.16 = (bf16[33,16,128]{2,1,0:T(8,128)(2,1)S(1)}, bf16[33,16,128]{2,1,0:T(8,128)(2,1)S(1)}, u32[]{:S(2)}, u32[]{:S(2)}) collective-permute-start(bf16[33,16,128]{2,1,0:T(8,128)(2,1)S(1)} %slice.8), channel_id=1, source_target_pairs={{0,4},{1,3},{4,8},{5,1},{8,12},{9,5},{12,14},{13,9},{14,10},{15,13... | collective-permute-start | bytes 405512 | tf_op jit(solution)/shard_map/ppermute | solution.py:315
  33.2 1.3 %collective-permute-start.17 = (bf16[33,16,128]{2,1,0:T(8,128)(2,1)S(1)}, bf16[33,16,128]{2,1,0:T(8,128)(2,1)S(1)}, u32[]{:S(2)}, u32[]{:S(2)}) collective-permute-start(bf16[33,16,128]{2,1,0:T(8,128)(2,1)S(1)} %slice.9), channel_id=1, source_target_pairs={{0,4},{1,3},{4,8},{5,1},{8,12},{9,5},{12,14},{13,9},{14,10},{15,13... | collective-permute-start | bytes 405512 | tf_op jit(solution)/shard_map/ppermute | solution.py:315
  34.5 2.7 %chunk.5 = (f32[64,2048]{1,0:T(8,128)S(1)}, f32[64,2048]{1,0:T(8,128)S(1)}, bf16[128,2048]{1,0:T(8,128)(2,1)S(1)}) custom-call(s32[16,128]{1,0:T(8,128)S(1)} %get-tuple-element.21.mine_ref.refs_0_, bf16[65,16,128]{2,1,0:T(8,128)(2,1)S(1)} %collective-permute-done.6.refs_1_, bf16[65,16,128]{2,1,0:T(8,128)(2,1)S(1)} %collective-permute-done.7.refs_2_, ...), custom_call_target="tpu_custom_call" | custom-call | flops 2415919104 | bytes 9437184 | tf_op jit(solution)/shard_map/chunk/pallas_call | solution.py:248
  37.2 0.1 collective-permute-start.2
  37.3 0.3 collective-permute-done.17.refs_2_
  37.6 0.9 %collective-permute-start.3 = (bf16[65,16,128]{2,1,0:T(8,128)(2,1)S(1)}, bf16[65,16,128]{2,1,0:T(8,128)(2,1)S(1)}, u32[]{:S(2)}, u32[]{:S(2)}) collective-permute-start(bf16[65,16,128]{2,1,0:T(8,128)(2,1)S(1)} %collective-permute-done.1.refs_2_), channel_id=1, source_target_pairs={{0,1},{1,0},{2,3},{3,2},{4,5},{5,4},{6,7},{7,6},{8,9},{9,8},{10,11... | collective-permute-start | bytes 798728 | tf_op jit(solution)/shard_map/ppermute | solution.py:315
  38.5 0.0 collective-permute-done.13.refs_3_
  38.5 0.0 collective-permute-start.18
  38.5 0.5 collective-permute-start.19
  39.0 2.7 %chunk.6 = (f32[64,2048]{1,0:T(8,128)S(1)}, f32[64,2048]{1,0:T(8,128)S(1)}, bf16[128,2048]{1,0:T(8,128)(2,1)S(1)}) custom-call(s32[16,128]{1,0:T(8,128)S(1)} %get-tuple-element.21.mine_ref.refs_0_, bf16[65,16,128]{2,1,0:T(8,128)(2,1)S(1)} %collective-permute-done.11.refs_1_, bf16[65,16,128]{2,1,0:T(8,128)(2,1)S(1)} %collective-permute-done.12.refs_2_, ...), custom_call_target="tpu_custom_call" | custom-call | flops 2415919104 | bytes 9437184 | tf_op jit(solution)/shard_map/chunk/pallas_call | solution.py:248
  41.7 0.0 collective-permute-done.18.refs_3_
  41.7 0.1 collective-permute-start.10
  41.9 0.0 collective-permute-done.19.refs_4_
  41.9 0.4 collective-permute-start.15
  42.3 2.0 %chunk.7 = (f32[32,2048]{1,0:T(8,128)S(1)}, f32[32,2048]{1,0:T(8,128)S(1)}, bf16[64,2048]{1,0:T(8,128)(2,1)S(1)}) custom-call(s32[16,128]{1,0:T(8,128)S(1)} %get-tuple-element.21.mine_ref.refs_0_, bf16[33,16,128]{2,1,0:T(8,128)(2,1)S(1)} %collective-permute-done.16.refs_1_, bf16[33,16,128]{2,1,0:T(8,128)(2,1)S(1)} %collective-permute-done.17.refs_2_, ...), custom_call_target="tpu_custom_call" | custom-call | flops 1207959552 | bytes 9437184 | tf_op jit(solution)/shard_map/chunk/pallas_call | solution.py:248
  44.3 0.0 collective-permute-done.4.refs_5_
  44.3 0.2 collective-permute-start.20
  44.5 0.0 collective-permute-done.3.refs_4_
  44.5 3.3 %chunk.4 = (f32[64,2048]{1,0:T(8,128)S(1)}, f32[64,2048]{1,0:T(8,128)S(1)}, bf16[192,2048]{1,0:T(8,128)(2,1)S(1)}) custom-call(s32[16,128]{1,0:T(8,128)S(1)} %get-tuple-element.21.mine_ref.refs_0_, bf16[65,16,128]{2,1,0:T(8,128)(2,1)S(1)} %collective-permute-done.refs_1_, bf16[65,16,128]{2,1,0:T(8,128)(2,1)S(1)} %collective-permute-done.1.refs_2_, ...), custom_call_target="tpu_custom_call" | custom-call | flops 3019898880 | bytes 9437184 | tf_op jit(solution)/shard_map/chunk/pallas_call | solution.py:248
  47.9 0.5 collective-permute-start.5
  48.4 0.2 collective-permute-start.25
  48.6 0.1 collective-permute-start.21
  48.7 3.8 %collective-permute-done.25.refs_2_ = bf16[32,2048]{1,0:T(8,128)(2,1)S(1)} collective-permute-done((bf16[32,2048]{1,0:T(8,128)(2,1)S(1)}, bf16[32,2048]{1,0:T(8,128)(2,1)S(1)}, u32[]{:S(2)}, u32[]{:S(2)}) %collective-permute-start.25) | collective-permute-done | bytes 131104 | tf_op jit(solution)/shard_map/ppermute | solution.py:315
  52.5 0.1 add.14
  52.6 0.2 collective-permute-start.26
  52.8 1.1 %collective-permute-done.21.refs_2_ = bf16[32,2048]{1,0:T(8,128)(2,1)S(1)} collective-permute-done((bf16[32,2048]{1,0:T(8,128)(2,1)S(1)}, bf16[32,2048]{1,0:T(8,128)(2,1)S(1)}, u32[]{:S(2)}, u32[]{:S(2)}) %collective-permute-start.21) | collective-permute-done | bytes 131104 | tf_op jit(solution)/shard_map/ppermute | solution.py:315
  53.9 0.1 add.10
  54.0 0.2 collective-permute-start.22
  54.2 0.0 collective-permute-done.10.refs_1_
  54.2 3.9 %collective-permute-done.26.refs_2_ = bf16[64,2048]{1,0:T(8,128)(2,1)S(1)} collective-permute-done((bf16[64,2048]{1,0:T(8,128)(2,1)S(1)}, bf16[64,2048]{1,0:T(8,128)(2,1)S(1)}, u32[]{:S(2)}, u32[]{:S(2)}) %collective-permute-start.26) | collective-permute-done | bytes 262176 | tf_op jit(solution)/shard_map/ppermute | solution.py:315
  58.2 0.1 add.15
  58.3 0.2 collective-permute-start.27
  58.5 2.5 %collective-permute-done.22.refs_2_ = bf16[64,2048]{1,0:T(8,128)(2,1)S(1)} collective-permute-done((bf16[64,2048]{1,0:T(8,128)(2,1)S(1)}, bf16[64,2048]{1,0:T(8,128)(2,1)S(1)}, u32[]{:S(2)}, u32[]{:S(2)}) %collective-permute-start.22) | collective-permute-done | bytes 262176 | tf_op jit(solution)/shard_map/ppermute | solution.py:315
  61.0 0.1 add.11
  61.1 0.2 collective-permute-start.23
  61.3 0.0 collective-permute-done.5.refs_1_
  61.3 2.5 %collective-permute-done.27.refs_2_ = bf16[64,2048]{1,0:T(8,128)(2,1)S(1)} collective-permute-done((bf16[64,2048]{1,0:T(8,128)(2,1)S(1)}, bf16[64,2048]{1,0:T(8,128)(2,1)S(1)}, u32[]{:S(2)}, u32[]{:S(2)}) %collective-permute-start.27) | collective-permute-done | bytes 262176 | tf_op jit(solution)/shard_map/ppermute | solution.py:315
  63.8 0.1 add.16
  63.9 2.8 %collective-permute-start.28 = (bf16[64,2048]{1,0:T(8,128)(2,1)S(1)}, bf16[64,2048]{1,0:T(8,128)(2,1)S(1)}, u32[]{:S(2)}, u32[]{:S(2)}) collective-permute-start(bf16[64,2048]{1,0:T(8,128)(2,1)S(1)} %add.16), channel_id=1, source_target_pairs={{4,1},{3,0},{8,5},{1,4},{12,9},{5,8},{14,13},{9,12},{10,15},{13,14... | collective-permute-start | bytes 786440 | tf_op jit(solution)/shard_map/ppermute | solution.py:315
  66.7 0.1 add.12
  66.8 0.1 collective-permute-start.24
  67.0 4.8 %collective-permute-done.28.refs_3_ = bf16[64,2048]{1,0:T(8,128)(2,1)S(1)} collective-permute-done((bf16[64,2048]{1,0:T(8,128)(2,1)S(1)}, bf16[64,2048]{1,0:T(8,128)(2,1)S(1)}, u32[]{:S(2)}, u32[]{:S(2)}) %collective-permute-start.28) | collective-permute-done | bytes 262176 | tf_op jit(solution)/shard_map/ppermute | solution.py:315
  71.7 3.1 %collective-permute-done.24.refs_2_ = bf16[64,2048]{1,0:T(8,128)(2,1)S(1)} collective-permute-done((bf16[64,2048]{1,0:T(8,128)(2,1)S(1)}, bf16[64,2048]{1,0:T(8,128)(2,1)S(1)}, u32[]{:S(2)}, u32[]{:S(2)}) %collective-permute-start.24) | collective-permute-done | bytes 262176 | tf_op jit(solution)/shard_map/ppermute | solution.py:315
  74.9 0.8 %add.17 = bf16[64,2048]{1,0:T(8,128)(2,1)} custom-call(f32[64,2048]{1,0:T(8,128)S(1)} %get-tuple-element.23.refs_0_, bf16[192,2048]{1,0:T(8,128)(2,1)S(1)} %collective-permute-done.5.refs_1_, bf16[64,2048]{1,0:T(8,128)(2,1)S(1)} %collective-permute-done.24.refs_2_, bf16[64,2048]{1,0:T(8,128)(2,1)S(1)} %collective-permute-done.28.refs_3_), custom_call_target="tpu_custom_call" | custom-call | tf_op jit(solution)/shard_map/add/pallas_call | solution.py:284
  (11 shorter events, 0.1 us)
Async XLA Ops:
  1.4 6.6 %collective-permute-start = (bf16[65,16,128]{2,1,0:T(8,128)(2,1)S(1)}, bf16[65,16,128]{2,1,0:T(8,128)(2,1)S(1)}, u32[]{:S(2)}, u32[]{:S(2)}) collective-permute-start(bf16[65,16,128]{2,1,0:T(8,128)(2,1)S(1)} %get-tuple-element.22.own_ref), channel_id=1, source_target_pairs={{0,4},{1,3},{4,8},{5,1},{8,12},{9,5},{12,14},{13,9},{14,10},{15,13... | collective-permute-start | bytes 798728 | tf_op jit(solution)/shard_map/ppermute | solution.py:315
  2.8 7.1 %collective-permute-start.1 = (bf16[65,16,128]{2,1,0:T(8,128)(2,1)S(1)}, bf16[65,16,128]{2,1,0:T(8,128)(2,1)S(1)}, u32[]{:S(2)}, u32[]{:S(2)}) collective-permute-start(bf16[65,16,128]{2,1,0:T(8,128)(2,1)S(1)} %get-tuple-element.22.own_ref), channel_id=1, source_target_pairs={{1,4},{0,3},{5,8},{4,1},{9,12},{8,5},{13,14},{12,9},{15,10},{14,13... | collective-permute-start | bytes 798728 | tf_op jit(solution)/shard_map/ppermute | solution.py:315
  8.0 5.3 %collective-permute-start.6 = (bf16[65,16,128]{2,1,0:T(8,128)(2,1)S(1)}, bf16[65,16,128]{2,1,0:T(8,128)(2,1)S(1)}, u32[]{:S(2)}, u32[]{:S(2)}) collective-permute-start(bf16[65,16,128]{2,1,0:T(8,128)(2,1)S(1)} %collective-permute-done.refs_1_), channel_id=1, source_target_pairs={{0,4},{1,3},{4,8},{5,1},{8,12},{9,5},{12,14},{13,9},{14,10},{15,13... | collective-permute-start | bytes 798728 | tf_op jit(solution)/shard_map/ppermute | solution.py:315
  9.9 6.5 %collective-permute-start.7 = (bf16[65,16,128]{2,1,0:T(8,128)(2,1)S(1)}, bf16[65,16,128]{2,1,0:T(8,128)(2,1)S(1)}, u32[]{:S(2)}, u32[]{:S(2)}) collective-permute-start(bf16[65,16,128]{2,1,0:T(8,128)(2,1)S(1)} %collective-permute-done.1.refs_2_), channel_id=1, source_target_pairs={{0,4},{1,3},{4,8},{5,1},{8,12},{9,5},{12,14},{13,9},{14,10},{15,13... | collective-permute-start | bytes 798728 | tf_op jit(solution)/shard_map/ppermute | solution.py:315
  13.3 8.4 %collective-permute-start.11 = (bf16[65,16,128]{2,1,0:T(8,128)(2,1)S(1)}, bf16[65,16,128]{2,1,0:T(8,128)(2,1)S(1)}, u32[]{:S(2)}, u32[]{:S(2)}) collective-permute-start(bf16[65,16,128]{2,1,0:T(8,128)(2,1)S(1)} %collective-permute-done.6.refs_1_), channel_id=1, source_target_pairs={{0,4},{1,3},{4,8},{5,1},{8,12},{9,5},{12,14},{13,9},{14,10},{15,13... | collective-permute-start | bytes 798728 | tf_op jit(solution)/shard_map/ppermute | solution.py:315
  16.5 7.8 %collective-permute-start.12 = (bf16[65,16,128]{2,1,0:T(8,128)(2,1)S(1)}, bf16[65,16,128]{2,1,0:T(8,128)(2,1)S(1)}, u32[]{:S(2)}, u32[]{:S(2)}) collective-permute-start(bf16[65,16,128]{2,1,0:T(8,128)(2,1)S(1)} %collective-permute-done.7.refs_2_), channel_id=1, source_target_pairs={{0,4},{1,3},{4,8},{5,1},{8,12},{9,5},{12,14},{13,9},{14,10},{15,13... | collective-permute-start | bytes 798728 | tf_op jit(solution)/shard_map/ppermute | solution.py:315
  17.9 14.0 %collective-permute-start.8 = (bf16[65,16,128]{2,1,0:T(8,128)(2,1)S(1)}, bf16[65,16,128]{2,1,0:T(8,128)(2,1)S(1)}, u32[]{:S(2)}, u32[]{:S(2)}) collective-permute-start(bf16[65,16,128]{2,1,0:T(8,128)(2,1)S(1)} %collective-permute-done.6.refs_1_), channel_id=1, source_target_pairs={{0,1},{1,0},{2,3},{3,2},{4,5},{5,4},{6,7},{7,6},{8,9},{9,8},{10,11... | collective-permute-start | bytes 798728 | tf_op jit(solution)/shard_map/ppermute | solution.py:315
  21.2 12.0 %collective-permute-start.9 = (bf16[65,16,128]{2,1,0:T(8,128)(2,1)S(1)}, bf16[65,16,128]{2,1,0:T(8,128)(2,1)S(1)}, u32[]{:S(2)}, u32[]{:S(2)}) collective-permute-start(bf16[65,16,128]{2,1,0:T(8,128)(2,1)S(1)} %collective-permute-done.7.refs_2_), channel_id=1, source_target_pairs={{0,1},{1,0},{2,3},{3,2},{4,5},{5,4},{6,7},{7,6},{8,9},{9,8},{10,11... | collective-permute-start | bytes 798728 | tf_op jit(solution)/shard_map/ppermute | solution.py:315
  21.2 23.2 %collective-permute-start.4 = (bf16[65,16,128]{2,1,0:T(8,128)(2,1)S(1)}, bf16[65,16,128]{2,1,0:T(8,128)(2,1)S(1)}, u32[]{:S(2)}, u32[]{:S(2)}) collective-permute-start(bf16[65,16,128]{2,1,0:T(8,128)(2,1)S(1)} %get-tuple-element.22.own_ref), channel_id=1, source_target_pairs={{0,1},{1,0},{2,3},{3,2},{4,5},{5,4},{6,7},{7,6},{8,9},{9,8},{10,11... | collective-permute-start | bytes 798728 | tf_op jit(solution)/shard_map/ppermute | solution.py:315
  21.7 16.8 %collective-permute-start.13 = (bf16[65,16,128]{2,1,0:T(8,128)(2,1)S(1)}, bf16[65,16,128]{2,1,0:T(8,128)(2,1)S(1)}, u32[]{:S(2)}, u32[]{:S(2)}) collective-permute-start(bf16[65,16,128]{2,1,0:T(8,128)(2,1)S(1)} %collective-permute-done.11.refs_1_), channel_id=1, source_target_pairs={{0,1},{1,0},{2,3},{3,2},{4,5},{5,4},{6,7},{7,6},{8,9},{9,8},{10,11... | collective-permute-start | bytes 798728 | tf_op jit(solution)/shard_map/ppermute | solution.py:315
  24.3 14.2 %collective-permute-start.14 = (bf16[65,16,128]{2,1,0:T(8,128)(2,1)S(1)}, bf16[65,16,128]{2,1,0:T(8,128)(2,1)S(1)}, u32[]{:S(2)}, u32[]{:S(2)}) collective-permute-start(bf16[65,16,128]{2,1,0:T(8,128)(2,1)S(1)} %collective-permute-done.12.refs_2_), channel_id=1, source_target_pairs={{0,1},{1,0},{2,3},{3,2},{4,5},{5,4},{6,7},{7,6},{8,9},{9,8},{10,11... | collective-permute-start | bytes 798728 | tf_op jit(solution)/shard_map/ppermute | solution.py:315
  32.0 5.2 %collective-permute-start.16 = (bf16[33,16,128]{2,1,0:T(8,128)(2,1)S(1)}, bf16[33,16,128]{2,1,0:T(8,128)(2,1)S(1)}, u32[]{:S(2)}, u32[]{:S(2)}) collective-permute-start(bf16[33,16,128]{2,1,0:T(8,128)(2,1)S(1)} %slice.8), channel_id=1, source_target_pairs={{0,4},{1,3},{4,8},{5,1},{8,12},{9,5},{12,14},{13,9},{14,10},{15,13... | collective-permute-start | bytes 405512 | tf_op jit(solution)/shard_map/ppermute | solution.py:315
  33.2 4.4 %collective-permute-start.17 = (bf16[33,16,128]{2,1,0:T(8,128)(2,1)S(1)}, bf16[33,16,128]{2,1,0:T(8,128)(2,1)S(1)}, u32[]{:S(2)}, u32[]{:S(2)}) collective-permute-start(bf16[33,16,128]{2,1,0:T(8,128)(2,1)S(1)} %slice.9), channel_id=1, source_target_pairs={{0,4},{1,3},{4,8},{5,1},{8,12},{9,5},{12,14},{13,9},{14,10},{15,13... | collective-permute-start | bytes 405512 | tf_op jit(solution)/shard_map/ppermute | solution.py:315
  37.2 7.3 %collective-permute-start.2 = (bf16[65,16,128]{2,1,0:T(8,128)(2,1)S(1)}, bf16[65,16,128]{2,1,0:T(8,128)(2,1)S(1)}, u32[]{:S(2)}, u32[]{:S(2)}) collective-permute-start(bf16[65,16,128]{2,1,0:T(8,128)(2,1)S(1)} %collective-permute-done.refs_1_), channel_id=1, source_target_pairs={{0,1},{1,0},{2,3},{3,2},{4,5},{5,4},{6,7},{7,6},{8,9},{9,8},{10,11... | collective-permute-start | bytes 798728 | tf_op jit(solution)/shard_map/ppermute | solution.py:315
  37.6 6.9 %collective-permute-start.3 = (bf16[65,16,128]{2,1,0:T(8,128)(2,1)S(1)}, bf16[65,16,128]{2,1,0:T(8,128)(2,1)S(1)}, u32[]{:S(2)}, u32[]{:S(2)}) collective-permute-start(bf16[65,16,128]{2,1,0:T(8,128)(2,1)S(1)} %collective-permute-done.1.refs_2_), channel_id=1, source_target_pairs={{0,1},{1,0},{2,3},{3,2},{4,5},{5,4},{6,7},{7,6},{8,9},{9,8},{10,11... | collective-permute-start | bytes 798728 | tf_op jit(solution)/shard_map/ppermute | solution.py:315
  38.5 3.2 %collective-permute-start.18 = (bf16[33,16,128]{2,1,0:T(8,128)(2,1)S(1)}, bf16[33,16,128]{2,1,0:T(8,128)(2,1)S(1)}, u32[]{:S(2)}, u32[]{:S(2)}) collective-permute-start(bf16[33,16,128]{2,1,0:T(8,128)(2,1)S(1)} %collective-permute-done.16.refs_1_), channel_id=1, source_target_pairs={{0,1},{1,0},{2,3},{3,2},{4,5},{5,4},{6,7},{7,6},{8,9},{9,8},{10,11... | collective-permute-start | bytes 405512 | tf_op jit(solution)/shard_map/ppermute | solution.py:315
  38.5 3.4 %collective-permute-start.19 = (bf16[33,16,128]{2,1,0:T(8,128)(2,1)S(1)}, bf16[33,16,128]{2,1,0:T(8,128)(2,1)S(1)}, u32[]{:S(2)}, u32[]{:S(2)}) collective-permute-start(bf16[33,16,128]{2,1,0:T(8,128)(2,1)S(1)} %collective-permute-done.17.refs_2_), channel_id=1, source_target_pairs={{0,1},{1,0},{2,3},{3,2},{4,5},{5,4},{6,7},{7,6},{8,9},{9,8},{10,11... | collective-permute-start | bytes 405512 | tf_op jit(solution)/shard_map/ppermute | solution.py:315
  41.7 12.5 %collective-permute-start.10 = (bf16[128,2048]{1,0:T(8,128)(2,1)S(1)}, bf16[128,2048]{1,0:T(8,128)(2,1)S(1)}, u32[]{:S(2)}, u32[]{:S(2)}) collective-permute-start(bf16[128,2048]{1,0:T(8,128)(2,1)S(1)} %get-tuple-element.28), channel_id=1, source_target_pairs={{0,1},{1,0},{2,3},{3,2},{4,5},{5,4},{6,7},{7,6},{8,9},{9,8},{10,11... | collective-permute-start | bytes 1572872 | tf_op jit(solution)/shard_map/ppermute | solution.py:315
  41.9 10.7 %collective-permute-start.15 = (bf16[128,2048]{1,0:T(8,128)(2,1)S(1)}, bf16[128,2048]{1,0:T(8,128)(2,1)S(1)}, u32[]{:S(2)}, u32[]{:S(2)}) collective-permute-start(bf16[128,2048]{1,0:T(8,128)(2,1)S(1)} %get-tuple-element.30), channel_id=1, source_target_pairs={{0,1},{1,0},{2,3},{3,2},{4,5},{5,4},{6,7},{7,6},{8,9},{9,8},{10,11... | collective-permute-start | bytes 1572872 | tf_op jit(solution)/shard_map/ppermute | solution.py:315
  44.3 4.0 %collective-permute-start.20 = (bf16[64,2048]{1,0:T(8,128)(2,1)S(1)}, bf16[64,2048]{1,0:T(8,128)(2,1)S(1)}, u32[]{:S(2)}, u32[]{:S(2)}) collective-permute-start(bf16[64,2048]{1,0:T(8,128)(2,1)S(1)} %get-tuple-element.32), channel_id=1, source_target_pairs={{0,1},{1,0},{2,3},{3,2},{4,5},{5,4},{6,7},{7,6},{8,9},{9,8},{10,11... | collective-permute-start | bytes 786440 | tf_op jit(solution)/shard_map/ppermute | solution.py:315
  47.9 13.4 %collective-permute-start.5 = (bf16[192,2048]{1,0:T(8,128)(2,1)S(1)}, bf16[192,2048]{1,0:T(8,128)(2,1)S(1)}, u32[]{:S(2)}, u32[]{:S(2)}) collective-permute-start(bf16[192,2048]{1,0:T(8,128)(2,1)S(1)} %get-tuple-element.25), channel_id=1, source_target_pairs={{0,1},{1,0},{2,3},{3,2},{4,5},{5,4},{6,7},{7,6},{8,9},{9,8},{10,11... | collective-permute-start | bytes 2359304 | tf_op jit(solution)/shard_map/ppermute | solution.py:315
  48.4 4.2 %collective-permute-start.25 = (bf16[32,2048]{1,0:T(8,128)(2,1)S(1)}, bf16[32,2048]{1,0:T(8,128)(2,1)S(1)}, u32[]{:S(2)}, u32[]{:S(2)}) collective-permute-start(bf16[32,2048]{1,0:T(8,128)(2,1)S(1)} %add.13), channel_id=1, source_target_pairs={{4,0},{3,1},{8,4},{1,5},{12,8},{5,9},{14,12},{9,13},{10,14},{13,15... | collective-permute-start | bytes 393224 | tf_op jit(solution)/shard_map/ppermute | solution.py:315
  48.6 5.3 %collective-permute-start.21 = (bf16[32,2048]{1,0:T(8,128)(2,1)S(1)}, bf16[32,2048]{1,0:T(8,128)(2,1)S(1)}, u32[]{:S(2)}, u32[]{:S(2)}) collective-permute-start(bf16[32,2048]{1,0:T(8,128)(2,1)S(1)} %add.9), channel_id=1, source_target_pairs={{4,0},{3,1},{8,4},{1,5},{12,8},{5,9},{14,12},{9,13},{10,14},{13,15... | collective-permute-start | bytes 393224 | tf_op jit(solution)/shard_map/ppermute | solution.py:315
  52.6 5.6 %collective-permute-start.26 = (bf16[64,2048]{1,0:T(8,128)(2,1)S(1)}, bf16[64,2048]{1,0:T(8,128)(2,1)S(1)}, u32[]{:S(2)}, u32[]{:S(2)}) collective-permute-start(bf16[64,2048]{1,0:T(8,128)(2,1)S(1)} %add.14), channel_id=1, source_target_pairs={{4,0},{3,1},{8,4},{1,5},{12,8},{5,9},{14,12},{9,13},{10,14},{13,15... | collective-permute-start | bytes 786440 | tf_op jit(solution)/shard_map/ppermute | solution.py:315
  54.0 7.0 %collective-permute-start.22 = (bf16[64,2048]{1,0:T(8,128)(2,1)S(1)}, bf16[64,2048]{1,0:T(8,128)(2,1)S(1)}, u32[]{:S(2)}, u32[]{:S(2)}) collective-permute-start(bf16[64,2048]{1,0:T(8,128)(2,1)S(1)} %add.10), channel_id=1, source_target_pairs={{4,0},{3,1},{8,4},{1,5},{12,8},{5,9},{14,12},{9,13},{10,14},{13,15... | collective-permute-start | bytes 786440 | tf_op jit(solution)/shard_map/ppermute | solution.py:315
  58.3 5.6 %collective-permute-start.27 = (bf16[64,2048]{1,0:T(8,128)(2,1)S(1)}, bf16[64,2048]{1,0:T(8,128)(2,1)S(1)}, u32[]{:S(2)}, u32[]{:S(2)}) collective-permute-start(bf16[64,2048]{1,0:T(8,128)(2,1)S(1)} %add.15), channel_id=1, source_target_pairs={{4,0},{3,1},{8,4},{1,5},{12,8},{5,9},{14,12},{9,13},{10,14},{13,15... | collective-permute-start | bytes 786440 | tf_op jit(solution)/shard_map/ppermute | solution.py:315
  61.1 5.6 %collective-permute-start.23 = (bf16[64,2048]{1,0:T(8,128)(2,1)S(1)}, bf16[64,2048]{1,0:T(8,128)(2,1)S(1)}, u32[]{:S(2)}, u32[]{:S(2)}) collective-permute-start(bf16[64,2048]{1,0:T(8,128)(2,1)S(1)} %add.11), channel_id=1, source_target_pairs={{4,0},{3,1},{8,4},{1,5},{12,8},{5,9},{14,12},{9,13},{10,14},{13,15... | collective-permute-start | bytes 786440 | tf_op jit(solution)/shard_map/ppermute | solution.py:315
  63.9 7.8 %collective-permute-start.28 = (bf16[64,2048]{1,0:T(8,128)(2,1)S(1)}, bf16[64,2048]{1,0:T(8,128)(2,1)S(1)}, u32[]{:S(2)}, u32[]{:S(2)}) collective-permute-start(bf16[64,2048]{1,0:T(8,128)(2,1)S(1)} %add.16), channel_id=1, source_target_pairs={{4,1},{3,0},{8,5},{1,4},{12,9},{5,8},{14,13},{9,12},{10,15},{13,14... | collective-permute-start | bytes 786440 | tf_op jit(solution)/shard_map/ppermute | solution.py:315
  66.8 8.1 %collective-permute-start.24 = (bf16[64,2048]{1,0:T(8,128)(2,1)S(1)}, bf16[64,2048]{1,0:T(8,128)(2,1)S(1)}, u32[]{:S(2)}, u32[]{:S(2)}) collective-permute-start(bf16[64,2048]{1,0:T(8,128)(2,1)S(1)} %add.12), channel_id=1, source_target_pairs={{4,0},{3,1},{8,4},{1,5},{12,8},{5,9},{14,12},{9,13},{10,14},{13,15... | collective-permute-start | bytes 786440 | tf_op jit(solution)/shard_map/ppermute | solution.py:315

commit v5 on v4

--- a/solution.py
+++ b/solution.py
@@ -10,6 +10,7 @@
 LANES = 128
 SUBS = 16
 THIRD = 3
+COPIES = 8
 VMEM = pl.BlockSpec(memory_space=pltpu.VMEM)
 SMEM = pl.BlockSpec(memory_space=pltpu.SMEM)
 HBM = pl.BlockSpec(memory_space=pltpu.HBM)
@@ -162,94 +163,73 @@
             row += SUBS
 
 
-def first_body(pk, width, mine_ref, own_ref, weights_ref, *rest):
-    keep_ref, kept_ref, x_ref, acc_ref, sems = rest
-    block = width // THIRD
+def copy_rows(source_ref, columns, target_ref, sems):
+    blocks = sems.shape[0]
+    rows = target_ref.shape[0] // blocks
     copies = []
-    for j in range(THIRD):
-        for part in range(THIRD):
-            columns = slice(part * width + j * block, part * width + (j + 1) * block)
-            copy = pltpu.make_async_copy(
-                weights_ref.at[0, :, columns], kept_ref.at[:, columns], sems.at[j, part]
-            )
-            copy.start()
-            copies.append(copy)
-    gather_rows(pk, [own_ref], ["all"], x_ref)
-    rows = x_ref[...]
-    for j in range(THIRD):
-        for part in range(THIRD):
-            copies[j * THIRD + part].wait()
-        gate = jnp.dot(
-            rows, kept_ref[:, j * block : (j + 1) * block], preferred_element_type=jnp.float32
+    for index in range(blocks):
+        span = slice(index * rows, (index + 1) * rows)
+        copy = pltpu.make_async_copy(
+            source_ref.at[0, span, columns], target_ref.at[span, :], sems.at[index]
         )
-        up = jnp.dot(
-            rows,
-            kept_ref[:, width + j * block : width + (j + 1) * block],
-            preferred_element_type=jnp.float32,
-        )
-        part = down(
-            activate(gate, up), kept_ref[:, 2 * width + j * block : 2 * width + (j + 1) * block]
-        )
-        if j == 0:
-            acc_ref[...] = part
-        else:
-            acc_ref[...] += part
-    store_scaled(pk, mine_ref, [own_ref], ["all"], acc_ref, [keep_ref])
-
-
-def first_chunk(pk, weights, mine, own):
-    width = weights.shape[2] // 4
-    rows, feature = pk.local_tokens, pk.feature
+        copy.start()
+        copies.append(copy)
+    return copies
+
+
+def fetch_body(columns, weights_ref, kept_ref, sems):
+    for copy in copy_rows(weights_ref, columns, kept_ref, sems):
+        copy.wait()
+
+
+def fetch(weights, columns):
+    count = columns.stop - columns.start
     return pl.pallas_call(
-        functools.partial(first_body, pk, width),
-        out_shape=[
-            pltpu.VMEM((rows, feature), jnp.float32),
-            pltpu.VMEM((feature, THIRD * width), jnp.bfloat16),
-        ],
-        in_specs=[VMEM, VMEM, HBM],
-        out_specs=[VMEM, VMEM],
-        scratch_shapes=[
-            pltpu.VMEM((rows, feature), jnp.bfloat16),
-            pltpu.VMEM((rows, feature), jnp.float32),
-            pltpu.SemaphoreType.DMA((THIRD, THIRD)),
-        ],
+        functools.partial(fetch_body, columns),
+        out_shape=pltpu.VMEM((weights.shape[1], count), weights.dtype),
+        in_specs=[HBM],
+        out_specs=VMEM,
+        scratch_shapes=[pltpu.SemaphoreType.DMA((COPIES,))],
         compiler_params=pltpu.CompilerParams(vmem_limit_bytes=VMEM_BYTES),
         cost_estimate=pl.CostEstimate(
-            flops=2 * rows * feature * 3 * width,
-            transcendentals=rows * width,
-            bytes_accessed=2 * feature * 3 * width,
+            flops=0, transcendentals=0, bytes_accessed=2 * weights.shape[1] * count
         ),
-        name="first_chunk",
-    )(mine, own, pltpu.with_memory_space_constraint(weights, pltpu.HBM))
-
-
-def chunk_body(pk, width, parts, *refs):
+        name="fetch",
+    )(pltpu.with_memory_space_constraint(weights, pltpu.HBM))
+
+
+def expert(rows, gate_up_ref, down_ref):
+    width = down_ref.shape[1]
+    gate = jnp.dot(rows, gate_up_ref[:, :width], preferred_element_type=jnp.float32)
+    up = jnp.dot(rows, gate_up_ref[:, width:], preferred_element_type=jnp.float32)
+    return down(activate(gate, up), down_ref[...])
+
+
+def chunk_body(pk, parts, *refs):
     mine_ref = refs[0]
     count = len(parts)
     buffers = refs[1 : 1 + count]
-    weights_ref = refs[1 + count]
-    out_refs = refs[2 + count : -1]
+    gate_up_ref, down_ref = refs[1 + count : 3 + count]
+    out_refs = refs[3 + count : -1]
     x_ref = refs[-1]
     gather_rows(pk, buffers, parts, x_ref)
-    rows = x_ref[...]
-    gate = jnp.dot(rows, weights_ref[:, :width], preferred_element_type=jnp.float32)
-    up = jnp.dot(rows, weights_ref[:, width : 2 * width], preferred_element_type=jnp.float32)
-    answers = down(activate(gate, up), weights_ref[:, 2 * width :])
+    answers = expert(x_ref[...], gate_up_ref, down_ref)
     store_scaled(pk, mine_ref, buffers, parts, answers, out_refs)
 
 
 def chunk(pk, weights, mine, own, crossed):
-    width = weights.shape[1] // THIRD
+    gate_up, down_weights = weights
+    width = down_weights.shape[1]
     feature = pk.feature
     buffers = [buffer for buffer, _ in own + crossed]
     parts = [part for _, part in own + crossed]
     given = sum(pk.rows(part) for _, part in crossed)
     total = sum(pk.rows(part) for part in parts)
     return pl.pallas_call(
-        functools.partial(chunk_body, pk, width, parts),
+        functools.partial(chunk_body, pk, parts),
         out_shape=[jax.ShapeDtypeStruct((pk.rows(part), feature), jnp.float32) for _, part in own]
         + [jax.ShapeDtypeStruct((given, feature), jnp.bfloat16)],
-        in_specs=[VMEM] * (len(buffers) + 2),
+        in_specs=[VMEM] * (len(buffers) + 3),
         out_specs=[VMEM] * (len(own) + 1),
         scratch_shapes=[pltpu.VMEM((total, feature), jnp.bfloat16)],
         compiler_params=pltpu.CompilerParams(vmem_limit_bytes=VMEM_BYTES),
@@ -259,7 +239,7 @@
             bytes_accessed=2 * feature * 3 * width,
         ),
         name="chunk",
-    )(mine, *buffers, weights)
+    )(mine, *buffers, gate_up, down_weights)
 
 
 def add_body(places, *refs):
@@ -304,9 +284,9 @@
         return 2 * ring[(i + (1 if core == 0 else -1)) % chips]
 
     seats = [(i, core) for i in range(chips) for core in range(2)]
-    straight = [(2 * ring[i] + core, near(i, core) + core) for i, core in seats]
+    along = [(2 * ring[i] + core, near(i, core) + core) for i, core in seats]
+    against = [(t, s) for s, t in along]
     crossing = [(2 * ring[i] + 1 - core, near(i, core) + core) for i, core in seats]
-    straight_back = [(t, s) for s, t in straight]
     crossing_back = [(t, s) for s, t in crossing]
     pair = [(d, d ^ 1) for d in range(devices)]
     wire = jnp.bfloat16 if chips <= 8 else jnp.float32
@@ -320,39 +300,37 @@
     )
 
     keep, gave = {}, {}
-    a, b = send(packed, straight), send(packed, crossing)
-    keep_own, weights = first_chunk(pk, expert_weights, mine, packed)
-    other = [(send(packed, pair), "all")]
+    width = expert_weights.shape[2] // 4
+    gate_up = fetch(expert_weights, slice(0, 2 * width))
+    weights = (gate_up, fetch(expert_weights, slice(2 * width, 3 * width)))
+    a, b = send(packed, along), send(packed, crossing)
+    other = send(packed, pair)
+    keep_own, give = chunk(pk, weights, mine, [(packed, "all")], [(other, "all")])
+    gave[0] = send(give, pair)
     for r in range(1, far):
         xa, xb = send(a, pair), send(b, pair)
         keep_a, keep_b, give = chunk(
-            pk, weights, mine, [(a, "all"), (b, "all")], [(xa, "all"), (xb, "all")] + other
+            pk, weights, mine, [(a, "all"), (b, "all")], [(xa, "all"), (xb, "all")]
         )
-        other = []
         keep[r] = (keep_a, keep_b)
         gave[r] = send(give, pair)
-        if r + 1 == far:
-            a, b = pk.cut(a, "first"), pk.cut(b, "second")
-        a, b = send(a, straight), send(b, straight)
-    xa, xb = send(a, pair), send(b, pair)
-    keep_a, keep_b, give = chunk(
-        pk, weights, mine, [(a, "first"), (b, "second")], [(xa, "first"), (xb, "second")]
-    )
+        a = send(a, along)
+        if r + 1 < far:
+            b = send(b, along)
+    xa = send(a, pair)
+    keep_a, give = chunk(pk, weights, mine, [(a, "all")], [(xa, "all")])
     gave[far] = send(give, pair)
 
     rows = local_tokens
-    first, second = pk.rows("first"), pk.rows("second")
-    a = add(first, wire, [(keep_a, 0, 0), (gave[far], 0, 0)])
-    a = [(send(a, straight_back), 0, 0)]
-    b = add(second, wire, [(keep_b, 0, 0), (gave[far], first, 0)])
-    b = [(send(b, straight_back), 0, first)]
+    a = add(rows, wire, [(keep_a, 0, 0), (gave[far], 0, 0)])
+    a, b = [(send(a, against), 0, 0)], []
     for r in range(far - 1, 0, -1):
         keep_a, keep_b = keep[r]
         a = add(rows, wire, [(keep_a, 0, 0), (gave[r], 0, 0)] + a)
-        a = [(send(a, straight_back), 0, 0)]
+        a = [(send(a, against), 0, 0)]
         b = add(rows, wire, [(keep_b, 0, 0), (gave[r], rows, 0)] + b)
-        b = [(send(b, straight_back if r > 1 else crossing_back), 0, 0)]
-    terms = [(keep_own, 0, 0), (gave[1], 2 * rows, 0)] + a + b
+        b = [(send(b, against if r > 1 else crossing_back), 0, 0)]
+    terms = [(keep_own, 0, 0), (gave[0], 0, 0)] + a + b
     return add(rows, jnp.bfloat16, terms)
 
 

time: 77.1 us -> 73.8 us (0.957)
  the two profiles are of different devices: /device:TPU:13 before, /device:TPU:0 now
where the time goes in v5:
time: 73.8 us; the launch traced here: 73.6 us
  waiting for transfers between devices  28.3 us (38%)
  starting transfers between devices  25.7 us (35%)
  Pallas kernels  19.5 us (26%)
    ppermute x27, waiting for transfers between devices, send(): return lax.ppermute(x, 'ep', where)  28.3 us
    ppermute x27, starting transfers between devices, send(): return lax.ppermute(x, 'ep', where)  25.7 us
    pallas_call x5, Pallas kernels, chunk(): pl.pallas_call(functools.partial(chunk_body, pk, parts), out_shape=[jax.S...  11.9 us
    pallas_call x2, Pallas kernels, fetch(): pl.pallas_call(functools.partial(fetch_body, columns), out_shape=pltpu.VM...  4.77 us
  transfers between devices with their start and end apart: 27, of which 11 were waited for; matrix products, arithmetic and copies ran while one was open for 0% of the time, Pallas kernels for 23%

profile of v5, /device:TPU:0, one launch (start us, length us, event | category | flops | bytes accessed | tf_op | source)
XLA Modules:
  0.0 73.6 jit_solution(7211212480904099115)
XLA Ops:
  0.0 1.4 %pack.1 = (bf16[65,16,128]{2,1,0:T(8,128)(2,1)S(1)}, s32[16,128]{1,0:T(8,128)S(1)}) custom-call(s32[1]{0:T(128)} %bitcast.me_ref, bf16[64,2048]{1,0:T(8,128)(2,1)} %refs_0_.1, s32[8,64]{1,0:T(8,128)} %bitcast.3, f32[8,64]{1,0:T(8,128)} %bitcast.4, s32[16]{0:T(128)} %refs_3_.1, s32[16]{0:T(128)} %refs_4_.1), custom_call_target="tpu_custom_call" | custom-call | tf_op jit(solution)/shard_map/pack/pallas_call | solution.py:115
  1.4 3.1 %collective-permute-start.2 = (bf16[65,16,128]{2,1,0:T(8,128)(2,1)S(1)}, bf16[65,16,128]{2,1,0:T(8,128)(2,1)S(1)}, u32[]{:S(2)}, u32[]{:S(2)}) collective-permute-start(bf16[65,16,128]{2,1,0:T(8,128)(2,1)S(1)} %get-tuple-element.21.refs_1_), channel_id=1, source_target_pairs={{0,4},{1,3},{4,8},{5,1},{8,12},{9,5},{12,14},{13,9},{14,10},{15,13... | collective-permute-start | bytes 798728 | tf_op jit(solution)/shard_map/ppermute | solution.py:295
  4.6 0.7 collective-permute-start.3
  5.2 5.1 %collective-permute-done.2.refs_1_ = bf16[65,16,128]{2,1,0:T(8,128)(2,1)S(1)} collective-permute-done((bf16[65,16,128]{2,1,0:T(8,128)(2,1)S(1)}, bf16[65,16,128]{2,1,0:T(8,128)(2,1)S(1)}, u32[]{:S(2)}, u32[]{:S(2)}) %collective-permute-start.2) | collective-permute-done | bytes 266272 | tf_op jit(solution)/shard_map/ppermute | solution.py:295
  10.3 2.5 %collective-permute-start.7 = (bf16[65,16,128]{2,1,0:T(8,128)(2,1)S(1)}, bf16[65,16,128]{2,1,0:T(8,128)(2,1)S(1)}, u32[]{:S(2)}, u32[]{:S(2)}) collective-permute-start(bf16[65,16,128]{2,1,0:T(8,128)(2,1)S(1)} %collective-permute-done.2.refs_1_), channel_id=1, source_target_pairs={{0,4},{1,3},{4,8},{5,1},{8,12},{9,5},{12,14},{13,9},{14,10},{15,13... | collective-permute-start | bytes 798728 | tf_op jit(solution)/shard_map/ppermute | solution.py:295
  12.8 1.6 %collective-permute-start.8 = (bf16[65,16,128]{2,1,0:T(8,128)(2,1)S(1)}, bf16[65,16,128]{2,1,0:T(8,128)(2,1)S(1)}, u32[]{:S(2)}, u32[]{:S(2)}) collective-permute-start(bf16[65,16,128]{2,1,0:T(8,128)(2,1)S(1)} %collective-permute-done.3.refs_2_), channel_id=1, source_target_pairs={{0,4},{1,3},{4,8},{5,1},{8,12},{9,5},{12,14},{13,9},{14,10},{15,13... | collective-permute-start | bytes 798728 | tf_op jit(solution)/shard_map/ppermute | solution.py:295
  14.4 3.8 %collective-permute-done.7.refs_1_ = bf16[65,16,128]{2,1,0:T(8,128)(2,1)S(1)} collective-permute-done((bf16[65,16,128]{2,1,0:T(8,128)(2,1)S(1)}, bf16[65,16,128]{2,1,0:T(8,128)(2,1)S(1)}, u32[]{:S(2)}, u32[]{:S(2)}) %collective-permute-start.7) | collective-permute-done | bytes 266272 | tf_op jit(solution)/shard_map/ppermute | solution.py:295
  18.2 1.1 %collective-permute-start.12 = (bf16[65,16,128]{2,1,0:T(8,128)(2,1)S(1)}, bf16[65,16,128]{2,1,0:T(8,128)(2,1)S(1)}, u32[]{:S(2)}, u32[]{:S(2)}) collective-permute-start(bf16[65,16,128]{2,1,0:T(8,128)(2,1)S(1)} %collective-permute-done.7.refs_1_), channel_id=1, source_target_pairs={{0,4},{1,3},{4,8},{5,1},{8,12},{9,5},{12,14},{13,9},{14,10},{15,13... | collective-permute-start | bytes 798728 | tf_op jit(solution)/shard_map/ppermute | solution.py:295
  19.2 1.8 %collective-permute-done.8.refs_2_ = bf16[65,16,128]{2,1,0:T(8,128)(2,1)S(1)} collective-permute-done((bf16[65,16,128]{2,1,0:T(8,128)(2,1)S(1)}, bf16[65,16,128]{2,1,0:T(8,128)(2,1)S(1)}, u32[]{:S(2)}, u32[]{:S(2)}) %collective-permute-start.8) | collective-permute-done | bytes 266272 | tf_op jit(solution)/shard_map/ppermute | solution.py:295
  21.0 1.1 %collective-permute-start.13 = (bf16[65,16,128]{2,1,0:T(8,128)(2,1)S(1)}, bf16[65,16,128]{2,1,0:T(8,128)(2,1)S(1)}, u32[]{:S(2)}, u32[]{:S(2)}) collective-permute-start(bf16[65,16,128]{2,1,0:T(8,128)(2,1)S(1)} %collective-permute-done.8.refs_2_), channel_id=1, source_target_pairs={{0,4},{1,3},{4,8},{5,1},{8,12},{9,5},{12,14},{13,9},{14,10},{15,13... | collective-permute-start | bytes 798728 | tf_op jit(solution)/shard_map/ppermute | solution.py:295
  22.1 2.5 %collective-permute-done.12.refs_1_ = bf16[65,16,128]{2,1,0:T(8,128)(2,1)S(1)} collective-permute-done((bf16[65,16,128]{2,1,0:T(8,128)(2,1)S(1)}, bf16[65,16,128]{2,1,0:T(8,128)(2,1)S(1)}, u32[]{:S(2)}, u32[]{:S(2)}) %collective-permute-start.12) | collective-permute-done | bytes 266272 | tf_op jit(solution)/shard_map/ppermute | solution.py:295
  24.6 1.1 %collective-permute-start.17 = (bf16[65,16,128]{2,1,0:T(8,128)(2,1)S(1)}, bf16[65,16,128]{2,1,0:T(8,128)(2,1)S(1)}, u32[]{:S(2)}, u32[]{:S(2)}) collective-permute-start(bf16[65,16,128]{2,1,0:T(8,128)(2,1)S(1)} %collective-permute-done.12.refs_1_), channel_id=1, source_target_pairs={{0,4},{1,3},{4,8},{5,1},{8,12},{9,5},{12,14},{13,9},{14,10},{15,13... | collective-permute-start | bytes 798728 | tf_op jit(solution)/shard_map/ppermute | solution.py:295
  25.7 0.0 collective-permute-start.14
  25.7 1.8 %collective-permute-done.13.refs_2_ = bf16[65,16,128]{2,1,0:T(8,128)(2,1)S(1)} collective-permute-done((bf16[65,16,128]{2,1,0:T(8,128)(2,1)S(1)}, bf16[65,16,128]{2,1,0:T(8,128)(2,1)S(1)}, u32[]{:S(2)}, u32[]{:S(2)}) %collective-permute-start.13) | collective-permute-done | bytes 266272 | tf_op jit(solution)/shard_map/ppermute | solution.py:295
  27.4 0.0 collective-permute-start.15
  27.4 3.6 %collective-permute-done.17.refs_1_ = bf16[65,16,128]{2,1,0:T(8,128)(2,1)S(1)} collective-permute-done((bf16[65,16,128]{2,1,0:T(8,128)(2,1)S(1)}, bf16[65,16,128]{2,1,0:T(8,128)(2,1)S(1)}, u32[]{:S(2)}, u32[]{:S(2)}) %collective-permute-start.17) | collective-permute-done | bytes 266272 | tf_op jit(solution)/shard_map/ppermute | solution.py:295
  31.0 2.9 %fetch.2.refs_3_.refs_5_ = bf16[2048,1536]{1,0:T(8,128)(2,1)S(1)} custom-call(bf16[1,2048,3072]{2,1,0:T(8,128)(2,1)} %weights_ref.3), custom_call_target="tpu_custom_call" | custom-call | bytes 6291456 | tf_op jit(solution)/shard_map/fetch/pallas_call | solution.py:187
  33.9 1.9 %fetch.3.refs_4_.refs_6_ = bf16[2048,768]{1,0:T(8,128)(2,1)S(1)} custom-call(bf16[1,2048,3072]{2,1,0:T(8,128)(2,1)} %weights_ref.3), custom_call_target="tpu_custom_call" | custom-call | bytes 3145728 | tf_op jit(solution)/shard_map/fetch/pallas_call | solution.py:187
  35.8 0.6 collective-permute-start.10
  36.3 0.1 collective-permute-start.9
  36.4 0.0 collective-permute-done.14.refs_3_
  36.4 0.0 collective-permute-done.15.refs_4_
  36.4 2.7 %chunk.8 = (f32[64,2048]{1,0:T(8,128)S(1)}, f32[64,2048]{1,0:T(8,128)S(1)}, bf16[128,2048]{1,0:T(8,128)(2,1)S(1)}) custom-call(s32[16,128]{1,0:T(8,128)S(1)} %get-tuple-element.20.refs_0_, bf16[65,16,128]{2,1,0:T(8,128)(2,1)S(1)} %collective-permute-done.12.refs_1_, bf16[65,16,128]{2,1,0:T(8,128)(2,1)S(1)} %collective-permute-done.13.refs_2_, ...), custom_call_target="tpu_custom_call" | custom-call | flops 2415919104 | bytes 9437184 | tf_op jit(solution)/shard_map/chunk/pallas_call | solution.py:228
  39.1 0.5 collective-permute-start.16
  39.6 0.0 collective-permute-done.18.refs_2_
  39.6 2.0 %chunk.9 = (f32[64,2048]{1,0:T(8,128)S(1)}, bf16[64,2048]{1,0:T(8,128)(2,1)S(1)}) custom-call(s32[16,128]{1,0:T(8,128)S(1)} %get-tuple-element.20.refs_0_, bf16[65,16,128]{2,1,0:T(8,128)(2,1)S(1)} %collective-permute-done.17.refs_1_, bf16[65,16,128]{2,1,0:T(8,128)(2,1)S(1)} %collective-permute-done.18.refs_2_, bf16[2048,1536]{1,0:T(8,128)(2,1)S(1)} %fetch.2.refs_3_.refs_5_, ...), custom_call_target="tpu_custom_call" | custom-call | flops 1207959552 | bytes 9437184 | tf_op jit(solution)/shard_map/chunk/pallas_call | solution.py:228
  41.6 0.2 collective-permute-start.19
  41.7 0.4 collective-permute-start.4
  42.2 0.0 collective-permute-done.10.refs_4_
  42.2 0.1 collective-permute-start.5
  42.3 0.0 collective-permute-done.9.refs_3_
  42.3 2.6 %chunk.7 = (f32[64,2048]{1,0:T(8,128)S(1)}, f32[64,2048]{1,0:T(8,128)S(1)}, bf16[128,2048]{1,0:T(8,128)(2,1)S(1)}) custom-call(s32[16,128]{1,0:T(8,128)S(1)} %get-tuple-element.20.refs_0_, bf16[65,16,128]{2,1,0:T(8,128)(2,1)S(1)} %collective-permute-done.7.refs_1_, bf16[65,16,128]{2,1,0:T(8,128)(2,1)S(1)} %collective-permute-done.8.refs_2_, ...), custom_call_target="tpu_custom_call" | custom-call | flops 2415919104 | bytes 9437184 | tf_op jit(solution)/shard_map/chunk/pallas_call | solution.py:228
  44.9 0.5 collective-permute-start.11
  45.4 0.0 collective-permute-done.19.refs_1_
  45.4 2.1 %collective-permute-start.20 = (bf16[64,2048]{1,0:T(8,128)(2,1)S(1)}, bf16[64,2048]{1,0:T(8,128)(2,1)S(1)}, u32[]{:S(2)}, u32[]{:S(2)}) collective-permute-start(bf16[64,2048]{1,0:T(8,128)(2,1)S(1)} %add.8), channel_id=1, source_target_pairs={{4,0},{3,1},{8,4},{1,5},{12,8},{5,9},{14,12},{9,13},{10,14},{13,15... | collective-permute-start | bytes 786440 | tf_op jit(solution)/shard_map/ppermute | solution.py:295
  47.5 0.0 collective-permute-done.4.refs_3_
  47.5 0.0 collective-permute-done.5.refs_4_
  47.5 2.6 %chunk.6 = (f32[64,2048]{1,0:T(8,128)S(1)}, f32[64,2048]{1,0:T(8,128)S(1)}, bf16[128,2048]{1,0:T(8,128)(2,1)S(1)}) custom-call(s32[16,128]{1,0:T(8,128)S(1)} %get-tuple-element.20.refs_0_, bf16[65,16,128]{2,1,0:T(8,128)(2,1)S(1)} %collective-permute-done.2.refs_1_, bf16[65,16,128]{2,1,0:T(8,128)(2,1)S(1)} %collective-permute-done.3.refs_2_, ...), custom_call_target="tpu_custom_call" | custom-call | flops 2415919104 | bytes 9437184 | tf_op jit(solution)/shard_map/chunk/pallas_call | solution.py:228
  50.2 0.1 collective-permute-start.6
  50.2 0.0 collective-permute-done.16.refs_1_
  50.3 1.6 %collective-permute-start.24 = (bf16[64,2048]{1,0:T(8,128)(2,1)S(1)}, bf16[64,2048]{1,0:T(8,128)(2,1)S(1)}, u32[]{:S(2)}, u32[]{:S(2)}) collective-permute-start(bf16[64,2048]{1,0:T(8,128)(2,1)S(1)} %add.12), channel_id=1, source_target_pairs={{4,0},{3,1},{8,4},{1,5},{12,8},{5,9},{14,12},{9,13},{10,14},{13,15... | collective-permute-start | bytes 786440 | tf_op jit(solution)/shard_map/ppermute | solution.py:295
  51.9 0.0 collective-permute-done.20.refs_2_
  51.9 0.1 add.9
  52.0 2.0 %collective-permute-start.21 = (bf16[64,2048]{1,0:T(8,128)(2,1)S(1)}, bf16[64,2048]{1,0:T(8,128)(2,1)S(1)}, u32[]{:S(2)}, u32[]{:S(2)}) collective-permute-start(bf16[64,2048]{1,0:T(8,128)(2,1)S(1)} %add.9), channel_id=1, source_target_pairs={{4,0},{3,1},{8,4},{1,5},{12,8},{5,9},{14,12},{9,13},{10,14},{13,15... | collective-permute-start | bytes 786440 | tf_op jit(solution)/shard_map/ppermute | solution.py:295
  54.0 0.0 collective-permute-start
  54.0 0.0 collective-permute-done.11.refs_1_
  54.0 2.7 %collective-permute-done.24.refs_2_ = bf16[64,2048]{1,0:T(8,128)(2,1)S(1)} collective-permute-done((bf16[64,2048]{1,0:T(8,128)(2,1)S(1)}, bf16[64,2048]{1,0:T(8,128)(2,1)S(1)}, u32[]{:S(2)}, u32[]{:S(2)}) %collective-permute-start.24) | collective-permute-done | bytes 262176 | tf_op jit(solution)/shard_map/ppermute | solution.py:295
  56.7 0.1 add.13
  56.8 1.6 %collective-permute-start.25 = (bf16[64,2048]{1,0:T(8,128)(2,1)S(1)}, bf16[64,2048]{1,0:T(8,128)(2,1)S(1)}, u32[]{:S(2)}, u32[]{:S(2)}) collective-permute-start(bf16[64,2048]{1,0:T(8,128)(2,1)S(1)} %add.13), channel_id=1, source_target_pairs={{4,0},{3,1},{8,4},{1,5},{12,8},{5,9},{14,12},{9,13},{10,14},{13,15... | collective-permute-start | bytes 786440 | tf_op jit(solution)/shard_map/ppermute | solution.py:295
  58.5 1.1 %collective-permute-done.21.refs_2_ = bf16[64,2048]{1,0:T(8,128)(2,1)S(1)} collective-permute-done((bf16[64,2048]{1,0:T(8,128)(2,1)S(1)}, bf16[64,2048]{1,0:T(8,128)(2,1)S(1)}, u32[]{:S(2)}, u32[]{:S(2)}) %collective-permute-start.21) | collective-permute-done | bytes 262176 | tf_op jit(solution)/shard_map/ppermute | solution.py:295
  59.5 0.1 add.10
  59.6 1.6 %collective-permute-start.22 = (bf16[64,2048]{1,0:T(8,128)(2,1)S(1)}, bf16[64,2048]{1,0:T(8,128)(2,1)S(1)}, u32[]{:S(2)}, u32[]{:S(2)}) collective-permute-start(bf16[64,2048]{1,0:T(8,128)(2,1)S(1)} %add.10), channel_id=1, source_target_pairs={{4,0},{3,1},{8,4},{1,5},{12,8},{5,9},{14,12},{9,13},{10,14},{13,15... | collective-permute-start | bytes 786440 | tf_op jit(solution)/shard_map/ppermute | solution.py:295
  61.3 0.0 collective-permute-done.refs_2_
  61.3 2.0 %chunk.5 = (f32[64,2048]{1,0:T(8,128)S(1)}, bf16[64,2048]{1,0:T(8,128)(2,1)S(1)}) custom-call(s32[16,128]{1,0:T(8,128)S(1)} %get-tuple-element.20.refs_0_, bf16[65,16,128]{2,1,0:T(8,128)(2,1)S(1)} %get-tuple-element.21.refs_1_, bf16[65,16,128]{2,1,0:T(8,128)(2,1)S(1)} %collective-permute-done.refs_2_, bf16[2048,1536]{1,0:T(8,128)(2,1)S(1)} %fetch.2.refs_3_.refs_5_, ...), custom_call_target="tpu_custom_call" | custom-call | flops 1207959552 | bytes 9437184 | tf_op jit(solution)/shard_map/chunk/pallas_call | solution.py:228
  63.3 0.1 collective-permute-start.1
  63.4 0.0 collective-permute-done.25.refs_2_
  63.4 0.1 add.14
  63.5 1.6 %collective-permute-start.26 = (bf16[64,2048]{1,0:T(8,128)(2,1)S(1)}, bf16[64,2048]{1,0:T(8,128)(2,1)S(1)}, u32[]{:S(2)}, u32[]{:S(2)}) collective-permute-start(bf16[64,2048]{1,0:T(8,128)(2,1)S(1)} %add.14), channel_id=1, source_target_pairs={{4,1},{3,0},{8,5},{1,4},{12,9},{5,8},{14,13},{9,12},{10,15},{13,14... | collective-permute-start | bytes 786440 | tf_op jit(solution)/shard_map/ppermute | solution.py:295
  65.1 1.0 %collective-permute-done.22.refs_2_ = bf16[64,2048]{1,0:T(8,128)(2,1)S(1)} collective-permute-done((bf16[64,2048]{1,0:T(8,128)(2,1)S(1)}, bf16[64,2048]{1,0:T(8,128)(2,1)S(1)}, u32[]{:S(2)}, u32[]{:S(2)}) %collective-permute-start.22) | collective-permute-done | bytes 262176 | tf_op jit(solution)/shard_map/ppermute | solution.py:295
  66.1 0.1 add.11
  66.2 1.6 %collective-permute-start.23 = (bf16[64,2048]{1,0:T(8,128)(2,1)S(1)}, bf16[64,2048]{1,0:T(8,128)(2,1)S(1)}, u32[]{:S(2)}, u32[]{:S(2)}) collective-permute-start(bf16[64,2048]{1,0:T(8,128)(2,1)S(1)} %add.11), channel_id=1, source_target_pairs={{4,0},{3,1},{8,4},{1,5},{12,8},{5,9},{14,12},{9,13},{10,14},{13,15... | collective-permute-start | bytes 786440 | tf_op jit(solution)/shard_map/ppermute | solution.py:295
  67.8 1.5 %collective-permute-done.26.refs_3_ = bf16[64,2048]{1,0:T(8,128)(2,1)S(1)} collective-permute-done((bf16[64,2048]{1,0:T(8,128)(2,1)S(1)}, bf16[64,2048]{1,0:T(8,128)(2,1)S(1)}, u32[]{:S(2)}, u32[]{:S(2)}) %collective-permute-start.26) | collective-permute-done | bytes 262176 | tf_op jit(solution)/shard_map/ppermute | solution.py:295
  69.3 3.5 %collective-permute-done.23.refs_2_ = bf16[64,2048]{1,0:T(8,128)(2,1)S(1)} collective-permute-done((bf16[64,2048]{1,0:T(8,128)(2,1)S(1)}, bf16[64,2048]{1,0:T(8,128)(2,1)S(1)}, u32[]{:S(2)}, u32[]{:S(2)}) %collective-permute-start.23) | collective-permute-done | bytes 262176 | tf_op jit(solution)/shard_map/ppermute | solution.py:295
  72.8 0.8 %add.15 = bf16[64,2048]{1,0:T(8,128)(2,1)} custom-call(f32[64,2048]{1,0:T(8,128)S(1)} %get-tuple-element.22.refs_0_, bf16[64,2048]{1,0:T(8,128)(2,1)S(1)} %collective-permute-done.1.refs_1_, bf16[64,2048]{1,0:T(8,128)(2,1)S(1)} %collective-permute-done.23.refs_2_, bf16[64,2048]{1,0:T(8,128)(2,1)S(1)} %collective-permute-done.26.refs_3_), custom_call_target="tpu_custom_call" | custom-call | tf_op jit(solution)/shard_map/add/pallas_call | solution.py:264
  (6 shorter events, 0.1 us)
Async XLA Ops:
  1.4 8.9 %collective-permute-start.2 = (bf16[65,16,128]{2,1,0:T(8,128)(2,1)S(1)}, bf16[65,16,128]{2,1,0:T(8,128)(2,1)S(1)}, u32[]{:S(2)}, u32[]{:S(2)}) collective-permute-start(bf16[65,16,128]{2,1,0:T(8,128)(2,1)S(1)} %get-tuple-element.21.refs_1_), channel_id=1, source_target_pairs={{0,4},{1,3},{4,8},{5,1},{8,12},{9,5},{12,14},{13,9},{14,10},{15,13... | collective-permute-start | bytes 798728 | tf_op jit(solution)/shard_map/ppermute | solution.py:295
  4.6 8.3 %collective-permute-start.3 = (bf16[65,16,128]{2,1,0:T(8,128)(2,1)S(1)}, bf16[65,16,128]{2,1,0:T(8,128)(2,1)S(1)}, u32[]{:S(2)}, u32[]{:S(2)}) collective-permute-start(bf16[65,16,128]{2,1,0:T(8,128)(2,1)S(1)} %get-tuple-element.21.refs_1_), channel_id=1, source_target_pairs={{1,4},{0,3},{5,8},{4,1},{9,12},{8,5},{13,14},{12,9},{15,10},{14,13... | collective-permute-start | bytes 798728 | tf_op jit(solution)/shard_map/ppermute | solution.py:295
  10.3 7.8 %collective-permute-start.7 = (bf16[65,16,128]{2,1,0:T(8,128)(2,1)S(1)}, bf16[65,16,128]{2,1,0:T(8,128)(2,1)S(1)}, u32[]{:S(2)}, u32[]{:S(2)}) collective-permute-start(bf16[65,16,128]{2,1,0:T(8,128)(2,1)S(1)} %collective-permute-done.2.refs_1_), channel_id=1, source_target_pairs={{0,4},{1,3},{4,8},{5,1},{8,12},{9,5},{12,14},{13,9},{14,10},{15,13... | collective-permute-start | bytes 798728 | tf_op jit(solution)/shard_map/ppermute | solution.py:295
  12.8 8.2 %collective-permute-start.8 = (bf16[65,16,128]{2,1,0:T(8,128)(2,1)S(1)}, bf16[65,16,128]{2,1,0:T(8,128)(2,1)S(1)}, u32[]{:S(2)}, u32[]{:S(2)}) collective-permute-start(bf16[65,16,128]{2,1,0:T(8,128)(2,1)S(1)} %collective-permute-done.3.refs_2_), channel_id=1, source_target_pairs={{0,4},{1,3},{4,8},{5,1},{8,12},{9,5},{12,14},{13,9},{14,10},{15,13... | collective-permute-start | bytes 798728 | tf_op jit(solution)/shard_map/ppermute | solution.py:295
  18.2 6.4 %collective-permute-start.12 = (bf16[65,16,128]{2,1,0:T(8,128)(2,1)S(1)}, bf16[65,16,128]{2,1,0:T(8,128)(2,1)S(1)}, u32[]{:S(2)}, u32[]{:S(2)}) collective-permute-start(bf16[65,16,128]{2,1,0:T(8,128)(2,1)S(1)} %collective-permute-done.7.refs_1_), channel_id=1, source_target_pairs={{0,4},{1,3},{4,8},{5,1},{8,12},{9,5},{12,14},{13,9},{14,10},{15,13... | collective-permute-start | bytes 798728 | tf_op jit(solution)/shard_map/ppermute | solution.py:295
  21.0 6.4 %collective-permute-start.13 = (bf16[65,16,128]{2,1,0:T(8,128)(2,1)S(1)}, bf16[65,16,128]{2,1,0:T(8,128)(2,1)S(1)}, u32[]{:S(2)}, u32[]{:S(2)}) collective-permute-start(bf16[65,16,128]{2,1,0:T(8,128)(2,1)S(1)} %collective-permute-done.8.refs_2_), channel_id=1, source_target_pairs={{0,4},{1,3},{4,8},{5,1},{8,12},{9,5},{12,14},{13,9},{14,10},{15,13... | collective-permute-start | bytes 798728 | tf_op jit(solution)/shard_map/ppermute | solution.py:295
  24.6 6.4 %collective-permute-start.17 = (bf16[65,16,128]{2,1,0:T(8,128)(2,1)S(1)}, bf16[65,16,128]{2,1,0:T(8,128)(2,1)S(1)}, u32[]{:S(2)}, u32[]{:S(2)}) collective-permute-start(bf16[65,16,128]{2,1,0:T(8,128)(2,1)S(1)} %collective-permute-done.12.refs_1_), channel_id=1, source_target_pairs={{0,4},{1,3},{4,8},{5,1},{8,12},{9,5},{12,14},{13,9},{14,10},{15,13... | collective-permute-start | bytes 798728 | tf_op jit(solution)/shard_map/ppermute | solution.py:295
  25.7 10.8 %collective-permute-start.14 = (bf16[65,16,128]{2,1,0:T(8,128)(2,1)S(1)}, bf16[65,16,128]{2,1,0:T(8,128)(2,1)S(1)}, u32[]{:S(2)}, u32[]{:S(2)}) collective-permute-start(bf16[65,16,128]{2,1,0:T(8,128)(2,1)S(1)} %collective-permute-done.12.refs_1_), channel_id=1, source_target_pairs={{0,1},{1,0},{2,3},{3,2},{4,5},{5,4},{6,7},{7,6},{8,9},{9,8},{10,11... | collective-permute-start | bytes 798728 | tf_op jit(solution)/shard_map/ppermute | solution.py:295
  27.4 9.0 %collective-permute-start.15 = (bf16[65,16,128]{2,1,0:T(8,128)(2,1)S(1)}, bf16[65,16,128]{2,1,0:T(8,128)(2,1)S(1)}, u32[]{:S(2)}, u32[]{:S(2)}) collective-permute-start(bf16[65,16,128]{2,1,0:T(8,128)(2,1)S(1)} %collective-permute-done.13.refs_2_), channel_id=1, source_target_pairs={{0,1},{1,0},{2,3},{3,2},{4,5},{5,4},{6,7},{7,6},{8,9},{9,8},{10,11... | collective-permute-start | bytes 798728 | tf_op jit(solution)/shard_map/ppermute | solution.py:295
  31.0 8.6 %collective-permute-start.18 = (bf16[65,16,128]{2,1,0:T(8,128)(2,1)S(1)}, bf16[65,16,128]{2,1,0:T(8,128)(2,1)S(1)}, u32[]{:S(2)}, u32[]{:S(2)}) collective-permute-start(bf16[65,16,128]{2,1,0:T(8,128)(2,1)S(1)} %collective-permute-done.17.refs_1_), channel_id=1, source_target_pairs={{0,1},{1,0},{2,3},{3,2},{4,5},{5,4},{6,7},{7,6},{8,9},{9,8},{10,11... | collective-permute-start | bytes 798728 | tf_op jit(solution)/shard_map/ppermute | solution.py:295
  35.8 6.4 %collective-permute-start.10 = (bf16[65,16,128]{2,1,0:T(8,128)(2,1)S(1)}, bf16[65,16,128]{2,1,0:T(8,128)(2,1)S(1)}, u32[]{:S(2)}, u32[]{:S(2)}) collective-permute-start(bf16[65,16,128]{2,1,0:T(8,128)(2,1)S(1)} %collective-permute-done.8.refs_2_), channel_id=1, source_target_pairs={{0,1},{1,0},{2,3},{3,2},{4,5},{5,4},{6,7},{7,6},{8,9},{9,8},{10,11... | collective-permute-start | bytes 798728 | tf_op jit(solution)/shard_map/ppermute | solution.py:295
  36.3 5.9 %collective-permute-start.9 = (bf16[65,16,128]{2,1,0:T(8,128)(2,1)S(1)}, bf16[65,16,128]{2,1,0:T(8,128)(2,1)S(1)}, u32[]{:S(2)}, u32[]{:S(2)}) collective-permute-start(bf16[65,16,128]{2,1,0:T(8,128)(2,1)S(1)} %collective-permute-done.7.refs_1_), channel_id=1, source_target_pairs={{0,1},{1,0},{2,3},{3,2},{4,5},{5,4},{6,7},{7,6},{8,9},{9,8},{10,11... | collective-permute-start | bytes 798728 | tf_op jit(solution)/shard_map/ppermute | solution.py:295
  39.1 11.1 %collective-permute-start.16 = (bf16[128,2048]{1,0:T(8,128)(2,1)S(1)}, bf16[128,2048]{1,0:T(8,128)(2,1)S(1)}, u32[]{:S(2)}, u32[]{:S(2)}) collective-permute-start(bf16[128,2048]{1,0:T(8,128)(2,1)S(1)} %get-tuple-element.29), channel_id=1, source_target_pairs={{0,1},{1,0},{2,3},{3,2},{4,5},{5,4},{6,7},{7,6},{8,9},{9,8},{10,11... | collective-permute-start | bytes 1572872 | tf_op jit(solution)/shard_map/ppermute | solution.py:295
  41.6 3.8 %collective-permute-start.19 = (bf16[64,2048]{1,0:T(8,128)(2,1)S(1)}, bf16[64,2048]{1,0:T(8,128)(2,1)S(1)}, u32[]{:S(2)}, u32[]{:S(2)}) collective-permute-start(bf16[64,2048]{1,0:T(8,128)(2,1)S(1)} %get-tuple-element.31), channel_id=1, source_target_pairs={{0,1},{1,0},{2,3},{3,2},{4,5},{5,4},{6,7},{7,6},{8,9},{9,8},{10,11... | collective-permute-start | bytes 786440 | tf_op jit(solution)/shard_map/ppermute | solution.py:295
  41.7 5.8 %collective-permute-start.4 = (bf16[65,16,128]{2,1,0:T(8,128)(2,1)S(1)}, bf16[65,16,128]{2,1,0:T(8,128)(2,1)S(1)}, u32[]{:S(2)}, u32[]{:S(2)}) collective-permute-start(bf16[65,16,128]{2,1,0:T(8,128)(2,1)S(1)} %collective-permute-done.2.refs_1_), channel_id=1, source_target_pairs={{0,1},{1,0},{2,3},{3,2},{4,5},{5,4},{6,7},{7,6},{8,9},{9,8},{10,11... | collective-permute-start | bytes 798728 | tf_op jit(solution)/shard_map/ppermute | solution.py:295
  42.2 5.3 %collective-permute-start.5 = (bf16[65,16,128]{2,1,0:T(8,128)(2,1)S(1)}, bf16[65,16,128]{2,1,0:T(8,128)(2,1)S(1)}, u32[]{:S(2)}, u32[]{:S(2)}) collective-permute-start(bf16[65,16,128]{2,1,0:T(8,128)(2,1)S(1)} %collective-permute-done.3.refs_2_), channel_id=1, source_target_pairs={{0,1},{1,0},{2,3},{3,2},{4,5},{5,4},{6,7},{7,6},{8,9},{9,8},{10,11... | collective-permute-start | bytes 798728 | tf_op jit(solution)/shard_map/ppermute | solution.py:295
  44.9 9.1 %collective-permute-start.11 = (bf16[128,2048]{1,0:T(8,128)(2,1)S(1)}, bf16[128,2048]{1,0:T(8,128)(2,1)S(1)}, u32[]{:S(2)}, u32[]{:S(2)}) collective-permute-start(bf16[128,2048]{1,0:T(8,128)(2,1)S(1)} %get-tuple-element.27), channel_id=1, source_target_pairs={{0,1},{1,0},{2,3},{3,2},{4,5},{5,4},{6,7},{7,6},{8,9},{9,8},{10,11... | collective-permute-start | bytes 1572872 | tf_op jit(solution)/shard_map/ppermute | solution.py:295
  45.4 6.5 %collective-permute-start.20 = (bf16[64,2048]{1,0:T(8,128)(2,1)S(1)}, bf16[64,2048]{1,0:T(8,128)(2,1)S(1)}, u32[]{:S(2)}, u32[]{:S(2)}) collective-permute-start(bf16[64,2048]{1,0:T(8,128)(2,1)S(1)} %add.8), channel_id=1, source_target_pairs={{4,0},{3,1},{8,4},{1,5},{12,8},{5,9},{14,12},{9,13},{10,14},{13,15... | collective-permute-start | bytes 786440 | tf_op jit(solution)/shard_map/ppermute | solution.py:295
  50.2 13.2 %collective-permute-start.6 = (bf16[128,2048]{1,0:T(8,128)(2,1)S(1)}, bf16[128,2048]{1,0:T(8,128)(2,1)S(1)}, u32[]{:S(2)}, u32[]{:S(2)}) collective-permute-start(bf16[128,2048]{1,0:T(8,128)(2,1)S(1)} %get-tuple-element.25), channel_id=1, source_target_pairs={{0,1},{1,0},{2,3},{3,2},{4,5},{5,4},{6,7},{7,6},{8,9},{9,8},{10,11... | collective-permute-start | bytes 1572872 | tf_op jit(solution)/shard_map/ppermute | solution.py:295
  50.3 6.4 %collective-permute-start.24 = (bf16[64,2048]{1,0:T(8,128)(2,1)S(1)}, bf16[64,2048]{1,0:T(8,128)(2,1)S(1)}, u32[]{:S(2)}, u32[]{:S(2)}) collective-permute-start(bf16[64,2048]{1,0:T(8,128)(2,1)S(1)} %add.12), channel_id=1, source_target_pairs={{4,0},{3,1},{8,4},{1,5},{12,8},{5,9},{14,12},{9,13},{10,14},{13,15... | collective-permute-start | bytes 786440 | tf_op jit(solution)/shard_map/ppermute | solution.py:295
  52.0 7.5 %collective-permute-start.21 = (bf16[64,2048]{1,0:T(8,128)(2,1)S(1)}, bf16[64,2048]{1,0:T(8,128)(2,1)S(1)}, u32[]{:S(2)}, u32[]{:S(2)}) collective-permute-start(bf16[64,2048]{1,0:T(8,128)(2,1)S(1)} %add.9), channel_id=1, source_target_pairs={{4,0},{3,1},{8,4},{1,5},{12,8},{5,9},{14,12},{9,13},{10,14},{13,15... | collective-permute-start | bytes 786440 | tf_op jit(solution)/shard_map/ppermute | solution.py:295
  54.0 7.2 %collective-permute-start = (bf16[65,16,128]{2,1,0:T(8,128)(2,1)S(1)}, bf16[65,16,128]{2,1,0:T(8,128)(2,1)S(1)}, u32[]{:S(2)}, u32[]{:S(2)}) collective-permute-start(bf16[65,16,128]{2,1,0:T(8,128)(2,1)S(1)} %get-tuple-element.21.refs_1_), channel_id=1, source_target_pairs={{0,1},{1,0},{2,3},{3,2},{4,5},{5,4},{6,7},{7,6},{8,9},{9,8},{10,11... | collective-permute-start | bytes 798728 | tf_op jit(solution)/shard_map/ppermute | solution.py:295
  56.8 6.5 %collective-permute-start.25 = (bf16[64,2048]{1,0:T(8,128)(2,1)S(1)}, bf16[64,2048]{1,0:T(8,128)(2,1)S(1)}, u32[]{:S(2)}, u32[]{:S(2)}) collective-permute-start(bf16[64,2048]{1,0:T(8,128)(2,1)S(1)} %add.13), channel_id=1, source_target_pairs={{4,0},{3,1},{8,4},{1,5},{12,8},{5,9},{14,12},{9,13},{10,14},{13,15... | collective-permute-start | bytes 786440 | tf_op jit(solution)/shard_map/ppermute | solution.py:295
  59.6 6.4 %collective-permute-start.22 = (bf16[64,2048]{1,0:T(8,128)(2,1)S(1)}, bf16[64,2048]{1,0:T(8,128)(2,1)S(1)}, u32[]{:S(2)}, u32[]{:S(2)}) collective-permute-start(bf16[64,2048]{1,0:T(8,128)(2,1)S(1)} %add.10), channel_id=1, source_target_pairs={{4,0},{3,1},{8,4},{1,5},{12,8},{5,9},{14,12},{9,13},{10,14},{13,15... | collective-permute-start | bytes 786440 | tf_op jit(solution)/shard_map/ppermute | solution.py:295
  63.3 4.5 %collective-permute-start.1 = (bf16[64,2048]{1,0:T(8,128)(2,1)S(1)}, bf16[64,2048]{1,0:T(8,128)(2,1)S(1)}, u32[]{:S(2)}, u32[]{:S(2)}) collective-permute-start(bf16[64,2048]{1,0:T(8,128)(2,1)S(1)} %get-tuple-element.23), channel_id=1, source_target_pairs={{0,1},{1,0},{2,3},{3,2},{4,5},{5,4},{6,7},{7,6},{8,9},{9,8},{10,11... | collective-permute-start | bytes 786440 | tf_op jit(solution)/shard_map/ppermute | solution.py:295
  63.5 5.9 %collective-permute-start.26 = (bf16[64,2048]{1,0:T(8,128)(2,1)S(1)}, bf16[64,2048]{1,0:T(8,128)(2,1)S(1)}, u32[]{:S(2)}, u32[]{:S(2)}) collective-permute-start(bf16[64,2048]{1,0:T(8,128)(2,1)S(1)} %add.14), channel_id=1, source_target_pairs={{4,1},{3,0},{8,5},{1,4},{12,9},{5,8},{14,13},{9,12},{10,15},{13,14... | collective-permute-start | bytes 786440 | tf_op jit(solution)/shard_map/ppermute | solution.py:295
  66.2 6.6 %collective-permute-start.23 = (bf16[64,2048]{1,0:T(8,128)(2,1)S(1)}, bf16[64,2048]{1,0:T(8,128)(2,1)S(1)}, u32[]{:S(2)}, u32[]{:S(2)}) collective-permute-start(bf16[64,2048]{1,0:T(8,128)(2,1)S(1)} %add.11), channel_id=1, source_target_pairs={{4,0},{3,1},{8,4},{1,5},{12,8},{5,9},{14,12},{9,13},{10,14},{13,15... | collective-permute-start | bytes 786440 | tf_op jit(solution)/shard_map/ppermute | solution.py:295

commit v6 on v5

--- a/solution.py
+++ b/solution.py
@@ -11,6 +11,7 @@
 SUBS = 16
 THIRD = 3
 COPIES = 8
+PARTS = 2
 VMEM = pl.BlockSpec(memory_space=pltpu.VMEM)
 SMEM = pl.BlockSpec(memory_space=pltpu.SMEM)
 HBM = pl.BlockSpec(memory_space=pltpu.HBM)
@@ -322,15 +323,23 @@
     gave[far] = send(give, pair)
 
     rows = local_tokens
-    a = add(rows, wire, [(keep_a, 0, 0), (gave[far], 0, 0)])
-    a, b = [(send(a, against), 0, 0)], []
-    for r in range(far - 1, 0, -1):
-        keep_a, keep_b = keep[r]
-        a = add(rows, wire, [(keep_a, 0, 0), (gave[r], 0, 0)] + a)
-        a = [(send(a, against), 0, 0)]
-        b = add(rows, wire, [(keep_b, 0, 0), (gave[r], rows, 0)] + b)
-        b = [(send(b, against if r > 1 else crossing_back), 0, 0)]
-    terms = [(keep_own, 0, 0), (gave[0], 0, 0)] + a + b
+    size = rows // PARTS
+    keep[far] = (keep_a, None)
+    sent = {"a": [[]] * PARTS, "b": [[]] * PARTS}
+    for r in range(far, 0, -1):
+        for chain, kept, first in (("a", keep[r][0], 0), ("b", keep[r][1], rows)):
+            if kept is None:
+                continue
+            route = crossing_back if chain == "b" and r == 1 else against
+            earlier, sent[chain] = sent[chain], []
+            for part in range(PARTS):
+                at = part * size
+                terms = [(kept, at, 0), (gave[r], first + at, 0)] + earlier[part]
+                total = add(size, wire, terms)
+                sent[chain].append([(send(total, route), 0, 0)])
+    terms = [(keep_own, 0, 0), (gave[0], 0, 0)]
+    for chain in sent.values():
+        terms += [(array, 0, part * size) for part, [(array, _, _)] in enumerate(chain)]
     return add(rows, jnp.bfloat16, terms)
 
 

time: 73.8 us -> 73.2 us (level)
  waiting for transfers between devices: 28.3 us -> 22.8 us
  starting transfers between devices: 25.7 us -> 30.5 us
    ppermute x27 -> x34, waiting for transfers between devices: 28.3 us -> 22.8 us  [send(): return lax.ppermute(x, 'ep', where)]
    ppermute x27 -> x34, starting transfers between devices: 25.7 us -> 30.5 us  [send(): return lax.ppermute(x, 'ep', where)]
  transfers between devices with their start and end apart: 27 -> 34, of which waited for: 11 -> 11; matrix products, arithmetic and copies ran while one was open for 0% -> 0% of each run, Pallas kernels for 23% -> 24%
where the time goes in v6:
time: 73.2 us; the launch traced here: 73 us
  starting transfers between devices  30.5 us (42%)
  waiting for transfers between devices  22.8 us (31%)
  Pallas kernels  19.5 us (27%)
    ppermute x34, starting transfers between devices, send(): return lax.ppermute(x, 'ep', where)  30.5 us
    ppermute x34, waiting for transfers between devices, send(): return lax.ppermute(x, 'ep', where)  22.8 us
    pallas_call x5, Pallas kernels, chunk(): pl.pallas_call(functools.partial(chunk_body, pk, parts), out_shape=[jax.S...  11.9 us
    pallas_call x2, Pallas kernels, fetch(): pl.pallas_call(functools.partial(fetch_body, columns), out_shape=pltpu.VM...  4.77 us
  transfers between devices with their start and end apart: 34, of which 11 were waited for; matrix products, arithmetic and copies ran while one was open for 0% of the time, Pallas kernels for 24%

profile of v6, /device:TPU:0, one launch (start us, length us, event | category | flops | bytes accessed | tf_op | source)
XLA Modules:
  0.0 73.0 jit_solution(13323738025832023929)
XLA Ops:
  0.0 1.4 %pack.1 = (bf16[65,16,128]{2,1,0:T(8,128)(2,1)S(1)}, s32[16,128]{1,0:T(8,128)S(1)}) custom-call(s32[1]{0:T(128)} %bitcast.me_ref, bf16[64,2048]{1,0:T(8,128)(2,1)} %refs_0_.1, s32[8,64]{1,0:T(8,128)} %bitcast.3, f32[8,64]{1,0:T(8,128)} %bitcast.4, s32[16]{0:T(128)} %refs_3_.1, s32[16]{0:T(128)} %refs_4_.1), custom_call_target="tpu_custom_call" | custom-call | tf_op jit(solution)/shard_map/pack/pallas_call | solution.py:116
  1.4 3.1 %collective-permute-start.2 = (bf16[65,16,128]{2,1,0:T(8,128)(2,1)S(1)}, bf16[65,16,128]{2,1,0:T(8,128)(2,1)S(1)}, u32[]{:S(2)}, u32[]{:S(2)}) collective-permute-start(bf16[65,16,128]{2,1,0:T(8,128)(2,1)S(1)} %get-tuple-element.21.refs_1_), channel_id=1, source_target_pairs={{0,4},{1,3},{4,8},{5,1},{8,12},{9,5},{12,14},{13,9},{14,10},{15,13... | collective-permute-start | bytes 798728 | tf_op jit(solution)/shard_map/ppermute | solution.py:296
  4.6 0.7 collective-permute-start.3
  5.2 5.1 %collective-permute-done.2.refs_1_ = bf16[65,16,128]{2,1,0:T(8,128)(2,1)S(1)} collective-permute-done((bf16[65,16,128]{2,1,0:T(8,128)(2,1)S(1)}, bf16[65,16,128]{2,1,0:T(8,128)(2,1)S(1)}, u32[]{:S(2)}, u32[]{:S(2)}) %collective-permute-start.2) | collective-permute-done | bytes 266272 | tf_op jit(solution)/shard_map/ppermute | solution.py:296
  10.3 2.5 %collective-permute-start.7 = (bf16[65,16,128]{2,1,0:T(8,128)(2,1)S(1)}, bf16[65,16,128]{2,1,0:T(8,128)(2,1)S(1)}, u32[]{:S(2)}, u32[]{:S(2)}) collective-permute-start(bf16[65,16,128]{2,1,0:T(8,128)(2,1)S(1)} %collective-permute-done.2.refs_1_), channel_id=1, source_target_pairs={{0,4},{1,3},{4,8},{5,1},{8,12},{9,5},{12,14},{13,9},{14,10},{15,13... | collective-permute-start | bytes 798728 | tf_op jit(solution)/shard_map/ppermute | solution.py:296
  12.8 1.6 %collective-permute-start.8 = (bf16[65,16,128]{2,1,0:T(8,128)(2,1)S(1)}, bf16[65,16,128]{2,1,0:T(8,128)(2,1)S(1)}, u32[]{:S(2)}, u32[]{:S(2)}) collective-permute-start(bf16[65,16,128]{2,1,0:T(8,128)(2,1)S(1)} %collective-permute-done.3.refs_2_), channel_id=1, source_target_pairs={{0,4},{1,3},{4,8},{5,1},{8,12},{9,5},{12,14},{13,9},{14,10},{15,13... | collective-permute-start | bytes 798728 | tf_op jit(solution)/shard_map/ppermute | solution.py:296
  14.4 3.8 %collective-permute-done.7.refs_1_ = bf16[65,16,128]{2,1,0:T(8,128)(2,1)S(1)} collective-permute-done((bf16[65,16,128]{2,1,0:T(8,128)(2,1)S(1)}, bf16[65,16,128]{2,1,0:T(8,128)(2,1)S(1)}, u32[]{:S(2)}, u32[]{:S(2)}) %collective-permute-start.7) | collective-permute-done | bytes 266272 | tf_op jit(solution)/shard_map/ppermute | solution.py:296
  18.2 1.1 %collective-permute-start.12 = (bf16[65,16,128]{2,1,0:T(8,128)(2,1)S(1)}, bf16[65,16,128]{2,1,0:T(8,128)(2,1)S(1)}, u32[]{:S(2)}, u32[]{:S(2)}) collective-permute-start(bf16[65,16,128]{2,1,0:T(8,128)(2,1)S(1)} %collective-permute-done.7.refs_1_), channel_id=1, source_target_pairs={{0,4},{1,3},{4,8},{5,1},{8,12},{9,5},{12,14},{13,9},{14,10},{15,13... | collective-permute-start | bytes 798728 | tf_op jit(solution)/shard_map/ppermute | solution.py:296
  19.2 1.8 %collective-permute-done.8.refs_2_ = bf16[65,16,128]{2,1,0:T(8,128)(2,1)S(1)} collective-permute-done((bf16[65,16,128]{2,1,0:T(8,128)(2,1)S(1)}, bf16[65,16,128]{2,1,0:T(8,128)(2,1)S(1)}, u32[]{:S(2)}, u32[]{:S(2)}) %collective-permute-start.8) | collective-permute-done | bytes 266272 | tf_op jit(solution)/shard_map/ppermute | solution.py:296
  21.0 1.1 %collective-permute-start.13 = (bf16[65,16,128]{2,1,0:T(8,128)(2,1)S(1)}, bf16[65,16,128]{2,1,0:T(8,128)(2,1)S(1)}, u32[]{:S(2)}, u32[]{:S(2)}) collective-permute-start(bf16[65,16,128]{2,1,0:T(8,128)(2,1)S(1)} %collective-permute-done.8.refs_2_), channel_id=1, source_target_pairs={{0,4},{1,3},{4,8},{5,1},{8,12},{9,5},{12,14},{13,9},{14,10},{15,13... | collective-permute-start | bytes 798728 | tf_op jit(solution)/shard_map/ppermute | solution.py:296
  22.1 0.5 collective-permute-start.9
  22.6 2.0 %collective-permute-done.12.refs_1_ = bf16[65,16,128]{2,1,0:T(8,128)(2,1)S(1)} collective-permute-done((bf16[65,16,128]{2,1,0:T(8,128)(2,1)S(1)}, bf16[65,16,128]{2,1,0:T(8,128)(2,1)S(1)}, u32[]{:S(2)}, u32[]{:S(2)}) %collective-permute-start.12) | collective-permute-done | bytes 266272 | tf_op jit(solution)/shard_map/ppermute | solution.py:296
  24.6 1.1 %collective-permute-start.17 = (bf16[65,16,128]{2,1,0:T(8,128)(2,1)S(1)}, bf16[65,16,128]{2,1,0:T(8,128)(2,1)S(1)}, u32[]{:S(2)}, u32[]{:S(2)}) collective-permute-start(bf16[65,16,128]{2,1,0:T(8,128)(2,1)S(1)} %collective-permute-done.12.refs_1_), channel_id=1, source_target_pairs={{0,4},{1,3},{4,8},{5,1},{8,12},{9,5},{12,14},{13,9},{14,10},{15,13... | collective-permute-start | bytes 798728 | tf_op jit(solution)/shard_map/ppermute | solution.py:296
  25.7 0.0 collective-permute-start.14
  25.7 1.8 %collective-permute-done.13.refs_2_ = bf16[65,16,128]{2,1,0:T(8,128)(2,1)S(1)} collective-permute-done((bf16[65,16,128]{2,1,0:T(8,128)(2,1)S(1)}, bf16[65,16,128]{2,1,0:T(8,128)(2,1)S(1)}, u32[]{:S(2)}, u32[]{:S(2)}) %collective-permute-start.13) | collective-permute-done | bytes 266272 | tf_op jit(solution)/shard_map/ppermute | solution.py:296
  27.4 0.0 collective-permute-start.15
  27.4 2.9 %fetch.2.refs_3_.refs_5_ = bf16[2048,1536]{1,0:T(8,128)(2,1)S(1)} custom-call(bf16[1,2048,3072]{2,1,0:T(8,128)(2,1)} %weights_ref.3), custom_call_target="tpu_custom_call" | custom-call | bytes 6291456 | tf_op jit(solution)/shard_map/fetch/pallas_call | solution.py:188
  30.3 1.9 %fetch.3.refs_4_.refs_6_ = bf16[2048,768]{1,0:T(8,128)(2,1)S(1)} custom-call(bf16[1,2048,3072]{2,1,0:T(8,128)(2,1)} %weights_ref.3), custom_call_target="tpu_custom_call" | custom-call | bytes 3145728 | tf_op jit(solution)/shard_map/fetch/pallas_call | solution.py:188
  32.2 0.0 collective-permute-done.10.refs_4_
  32.2 0.6 collective-permute-start.4
  32.8 0.1 collective-permute-start.5
  32.9 0.0 collective-permute-done.17.refs_1_
  32.9 0.4 collective-permute-start.18
  33.3 2.6 %chunk.7 = (f32[64,2048]{1,0:T(8,128)S(1)}, f32[64,2048]{1,0:T(8,128)S(1)}, bf16[128,2048]{1,0:T(8,128)(2,1)S(1)}) custom-call(s32[16,128]{1,0:T(8,128)S(1)} %get-tuple-element.20.refs_0_, bf16[65,16,128]{2,1,0:T(8,128)(2,1)S(1)} %collective-permute-done.7.refs_1_, bf16[65,16,128]{2,1,0:T(8,128)(2,1)S(1)} %collective-permute-done.8.refs_2_, ...), custom_call_target="tpu_custom_call" | custom-call | flops 2415919104 | bytes 9437184 | tf_op jit(solution)/shard_map/chunk/pallas_call | solution.py:229
  36.0 0.0 collective-permute-done.14.refs_3_
  36.0 0.1 collective-permute-start.11
  36.1 2.6 %chunk.8 = (f32[64,2048]{1,0:T(8,128)S(1)}, f32[64,2048]{1,0:T(8,128)S(1)}, bf16[128,2048]{1,0:T(8,128)(2,1)S(1)}) custom-call(s32[16,128]{1,0:T(8,128)S(1)} %get-tuple-element.20.refs_0_, bf16[65,16,128]{2,1,0:T(8,128)(2,1)S(1)} %collective-permute-done.12.refs_1_, bf16[65,16,128]{2,1,0:T(8,128)(2,1)S(1)} %collective-permute-done.13.refs_2_, ...), custom_call_target="tpu_custom_call" | custom-call | flops 2415919104 | bytes 9437184 | tf_op jit(solution)/shard_map/chunk/pallas_call | solution.py:229
  38.8 0.5 collective-permute-start.16
  39.3 2.0 %chunk.9 = (f32[64,2048]{1,0:T(8,128)S(1)}, bf16[64,2048]{1,0:T(8,128)(2,1)S(1)}) custom-call(s32[16,128]{1,0:T(8,128)S(1)} %get-tuple-element.20.refs_0_, bf16[65,16,128]{2,1,0:T(8,128)(2,1)S(1)} %collective-permute-done.17.refs_1_, bf16[65,16,128]{2,1,0:T(8,128)(2,1)S(1)} %collective-permute-done.18.refs_2_, bf16[2048,1536]{1,0:T(8,128)(2,1)S(1)} %fetch.2.refs_3_.refs_5_, ...), custom_call_target="tpu_custom_call" | custom-call | flops 1207959552 | bytes 9437184 | tf_op jit(solution)/shard_map/chunk/pallas_call | solution.py:229
  41.3 0.2 collective-permute-start.19
  41.4 0.0 collective-permute-done.4.refs_3_
  41.4 2.6 %chunk.6 = (f32[64,2048]{1,0:T(8,128)S(1)}, f32[64,2048]{1,0:T(8,128)S(1)}, bf16[128,2048]{1,0:T(8,128)(2,1)S(1)}) custom-call(s32[16,128]{1,0:T(8,128)S(1)} %get-tuple-element.20.refs_0_, bf16[65,16,128]{2,1,0:T(8,128)(2,1)S(1)} %collective-permute-done.2.refs_1_, bf16[65,16,128]{2,1,0:T(8,128)(2,1)S(1)} %collective-permute-done.3.refs_2_, ...), custom_call_target="tpu_custom_call" | custom-call | flops 2415919104 | bytes 9437184 | tf_op jit(solution)/shard_map/chunk/pallas_call | solution.py:229
  44.1 0.5 collective-permute-start.6
  44.6 0.1 collective-permute-start
  44.7 2.1 %collective-permute-start.24 = (bf16[32,2048]{1,0:T(8,128)(2,1)S(1)}, bf16[32,2048]{1,0:T(8,128)(2,1)S(1)}, u32[]{:S(2)}, u32[]{:S(2)}) collective-permute-start(bf16[32,2048]{1,0:T(8,128)(2,1)S(1)} %add.19), channel_id=1, source_target_pairs={{4,0},{3,1},{8,4},{1,5},{12,8},{5,9},{14,12},{9,13},{10,14},{13,15... | collective-permute-start | bytes 393224 | tf_op jit(solution)/shard_map/ppermute | solution.py:296
  46.8 0.0 collective-permute-done.16.refs_1_
  46.8 1.6 %collective-permute-start.20 = (bf16[32,2048]{1,0:T(8,128)(2,1)S(1)}, bf16[32,2048]{1,0:T(8,128)(2,1)S(1)}, u32[]{:S(2)}, u32[]{:S(2)}) collective-permute-start(bf16[32,2048]{1,0:T(8,128)(2,1)S(1)} %add.15), channel_id=1, source_target_pairs={{4,0},{3,1},{8,4},{1,5},{12,8},{5,9},{14,12},{9,13},{10,14},{13,15... | collective-permute-start | bytes 393224 | tf_op jit(solution)/shard_map/ppermute | solution.py:296
  48.5 0.0 collective-permute-done.refs_2_
  48.5 1.5 %collective-permute-start.31 = (bf16[32,2048]{1,0:T(8,128)(2,1)S(1)}, bf16[32,2048]{1,0:T(8,128)(2,1)S(1)}, u32[]{:S(2)}, u32[]{:S(2)}) collective-permute-start(bf16[32,2048]{1,0:T(8,128)(2,1)S(1)} %add.26), channel_id=1, source_target_pairs={{4,0},{3,1},{8,4},{1,5},{12,8},{5,9},{14,12},{9,13},{10,14},{13,15... | collective-permute-start | bytes 393224 | tf_op jit(solution)/shard_map/ppermute | solution.py:296
  50.0 1.7 %collective-permute-start.28 = (bf16[32,2048]{1,0:T(8,128)(2,1)S(1)}, bf16[32,2048]{1,0:T(8,128)(2,1)S(1)}, u32[]{:S(2)}, u32[]{:S(2)}) collective-permute-start(bf16[32,2048]{1,0:T(8,128)(2,1)S(1)} %add.23), channel_id=1, source_target_pairs={{4,0},{3,1},{8,4},{1,5},{12,8},{5,9},{14,12},{9,13},{10,14},{13,15... | collective-permute-start | bytes 393224 | tf_op jit(solution)/shard_map/ppermute | solution.py:296
  51.8 0.0 collective-permute-done.20.refs_2_
  51.8 1.6 %collective-permute-start.25 = (bf16[32,2048]{1,0:T(8,128)(2,1)S(1)}, bf16[32,2048]{1,0:T(8,128)(2,1)S(1)}, u32[]{:S(2)}, u32[]{:S(2)}) collective-permute-start(bf16[32,2048]{1,0:T(8,128)(2,1)S(1)} %add.20), channel_id=1, source_target_pairs={{4,0},{3,1},{8,4},{1,5},{12,8},{5,9},{14,12},{9,13},{10,14},{13,15... | collective-permute-start | bytes 393224 | tf_op jit(solution)/shard_map/ppermute | solution.py:296
  53.5 1.5 %collective-permute-start.21 = (bf16[32,2048]{1,0:T(8,128)(2,1)S(1)}, bf16[32,2048]{1,0:T(8,128)(2,1)S(1)}, u32[]{:S(2)}, u32[]{:S(2)}) collective-permute-start(bf16[32,2048]{1,0:T(8,128)(2,1)S(1)} %add.16), channel_id=1, source_target_pairs={{4,0},{3,1},{8,4},{1,5},{12,8},{5,9},{14,12},{9,13},{10,14},{13,15... | collective-permute-start | bytes 393224 | tf_op jit(solution)/shard_map/ppermute | solution.py:296
  55.0 2.0 %chunk.5 = (f32[64,2048]{1,0:T(8,128)S(1)}, bf16[64,2048]{1,0:T(8,128)(2,1)S(1)}) custom-call(s32[16,128]{1,0:T(8,128)S(1)} %get-tuple-element.20.refs_0_, bf16[65,16,128]{2,1,0:T(8,128)(2,1)S(1)} %get-tuple-element.21.refs_1_, bf16[65,16,128]{2,1,0:T(8,128)(2,1)S(1)} %collective-permute-done.refs_2_, bf16[2048,1536]{1,0:T(8,128)(2,1)S(1)} %fetch.2.refs_3_.refs_5_, ...), custom_call_target="tpu_custom_call" | custom-call | flops 1207959552 | bytes 9437184 | tf_op jit(solution)/shard_map/chunk/pallas_call | solution.py:229
  57.0 0.1 add.27
  57.1 1.6 %collective-permute-start.32 = (bf16[32,2048]{1,0:T(8,128)(2,1)S(1)}, bf16[32,2048]{1,0:T(8,128)(2,1)S(1)}, u32[]{:S(2)}, u32[]{:S(2)}) collective-permute-start(bf16[32,2048]{1,0:T(8,128)(2,1)S(1)} %add.27), channel_id=1, source_target_pairs={{4,0},{3,1},{8,4},{1,5},{12,8},{5,9},{14,12},{9,13},{10,14},{13,15... | collective-permute-start | bytes 393224 | tf_op jit(solution)/shard_map/ppermute | solution.py:296
  58.7 0.1 add.24
  58.7 1.4 %collective-permute-start.29 = (bf16[32,2048]{1,0:T(8,128)(2,1)S(1)}, bf16[32,2048]{1,0:T(8,128)(2,1)S(1)}, u32[]{:S(2)}, u32[]{:S(2)}) collective-permute-start(bf16[32,2048]{1,0:T(8,128)(2,1)S(1)} %add.24), channel_id=1, source_target_pairs={{4,0},{3,1},{8,4},{1,5},{12,8},{5,9},{14,12},{9,13},{10,14},{13,15... | collective-permute-start | bytes 393224 | tf_op jit(solution)/shard_map/ppermute | solution.py:296
  60.1 0.1 add.21
  60.2 0.1 collective-permute-start.26
  60.2 0.1 collective-permute-start.1
  60.4 0.1 collective-permute-start.22
  60.5 1.6 %collective-permute-done.32.refs_2_ = bf16[32,2048]{1,0:T(8,128)(2,1)S(1)} collective-permute-done((bf16[32,2048]{1,0:T(8,128)(2,1)S(1)}, bf16[32,2048]{1,0:T(8,128)(2,1)S(1)}, u32[]{:S(2)}, u32[]{:S(2)}) %collective-permute-start.32) | collective-permute-done | bytes 131104 | tf_op jit(solution)/shard_map/ppermute | solution.py:296
  62.1 0.3 collective-permute-start.33
  62.4 1.4 %collective-permute-done.29.refs_2_ = bf16[32,2048]{1,0:T(8,128)(2,1)S(1)} collective-permute-done((bf16[32,2048]{1,0:T(8,128)(2,1)S(1)}, bf16[32,2048]{1,0:T(8,128)(2,1)S(1)}, u32[]{:S(2)}, u32[]{:S(2)}) %collective-permute-start.29) | collective-permute-done | bytes 131104 | tf_op jit(solution)/shard_map/ppermute | solution.py:296
  63.8 0.2 collective-permute-start.30
  64.1 1.1 %collective-permute-done.26.refs_2_ = bf16[32,2048]{1,0:T(8,128)(2,1)S(1)} collective-permute-done((bf16[32,2048]{1,0:T(8,128)(2,1)S(1)}, bf16[32,2048]{1,0:T(8,128)(2,1)S(1)}, u32[]{:S(2)}, u32[]{:S(2)}) %collective-permute-start.26) | collective-permute-done | bytes 131104 | tf_op jit(solution)/shard_map/ppermute | solution.py:296
  65.2 1.3 %collective-permute-start.27 = (bf16[32,2048]{1,0:T(8,128)(2,1)S(1)}, bf16[32,2048]{1,0:T(8,128)(2,1)S(1)}, u32[]{:S(2)}, u32[]{:S(2)}) collective-permute-start(bf16[32,2048]{1,0:T(8,128)(2,1)S(1)} %add.22), channel_id=1, source_target_pairs={{4,0},{3,1},{8,4},{1,5},{12,8},{5,9},{14,12},{9,13},{10,14},{13,15... | collective-permute-start | bytes 393224 | tf_op jit(solution)/shard_map/ppermute | solution.py:296
  66.6 0.0 collective-permute-done.22.refs_2_
  66.6 1.3 %collective-permute-start.23 = (bf16[32,2048]{1,0:T(8,128)(2,1)S(1)}, bf16[32,2048]{1,0:T(8,128)(2,1)S(1)}, u32[]{:S(2)}, u32[]{:S(2)}) collective-permute-start(bf16[32,2048]{1,0:T(8,128)(2,1)S(1)} %add.18), channel_id=1, source_target_pairs={{4,0},{3,1},{8,4},{1,5},{12,8},{5,9},{14,12},{9,13},{10,14},{13,15... | collective-permute-start | bytes 393224 | tf_op jit(solution)/shard_map/ppermute | solution.py:296
  68.0 0.3 collective-permute-done.30.refs_4_
  68.3 2.5 %collective-permute-done.27.refs_3_ = bf16[32,2048]{1,0:T(8,128)(2,1)S(1)} collective-permute-done((bf16[32,2048]{1,0:T(8,128)(2,1)S(1)}, bf16[32,2048]{1,0:T(8,128)(2,1)S(1)}, u32[]{:S(2)}, u32[]{:S(2)}) %collective-permute-start.27) | collective-permute-done | bytes 131104 | tf_op jit(solution)/shard_map/ppermute | solution.py:296
  70.8 1.4 %collective-permute-done.23.refs_2_ = bf16[32,2048]{1,0:T(8,128)(2,1)S(1)} collective-permute-done((bf16[32,2048]{1,0:T(8,128)(2,1)S(1)}, bf16[32,2048]{1,0:T(8,128)(2,1)S(1)}, u32[]{:S(2)}, u32[]{:S(2)}) %collective-permute-start.23) | collective-permute-done | bytes 131104 | tf_op jit(solution)/shard_map/ppermute | solution.py:296
  72.2 0.8 %add.29 = bf16[64,2048]{1,0:T(8,128)(2,1)} custom-call(f32[64,2048]{1,0:T(8,128)S(1)} %get-tuple-element.22.refs_0_, bf16[64,2048]{1,0:T(8,128)(2,1)S(1)} %collective-permute-done.1.refs_1_, bf16[32,2048]{1,0:T(8,128)(2,1)S(1)} %collective-permute-done.23.refs_2_, bf16[32,2048]{1,0:T(8,128)(2,1)S(1)} %collective-permute-done.27.refs_3_, ...), custom_call_target="tpu_custom_call" | custom-call | tf_op jit(solution)/shard_map/add/pallas_call | solution.py:265
  (27 shorter events, 0.4 us)
Async XLA Ops:
  1.4 8.9 %collective-permute-start.2 = (bf16[65,16,128]{2,1,0:T(8,128)(2,1)S(1)}, bf16[65,16,128]{2,1,0:T(8,128)(2,1)S(1)}, u32[]{:S(2)}, u32[]{:S(2)}) collective-permute-start(bf16[65,16,128]{2,1,0:T(8,128)(2,1)S(1)} %get-tuple-element.21.refs_1_), channel_id=1, source_target_pairs={{0,4},{1,3},{4,8},{5,1},{8,12},{9,5},{12,14},{13,9},{14,10},{15,13... | collective-permute-start | bytes 798728 | tf_op jit(solution)/shard_map/ppermute | solution.py:296
  4.6 8.3 %collective-permute-start.3 = (bf16[65,16,128]{2,1,0:T(8,128)(2,1)S(1)}, bf16[65,16,128]{2,1,0:T(8,128)(2,1)S(1)}, u32[]{:S(2)}, u32[]{:S(2)}) collective-permute-start(bf16[65,16,128]{2,1,0:T(8,128)(2,1)S(1)} %get-tuple-element.21.refs_1_), channel_id=1, source_target_pairs={{1,4},{0,3},{5,8},{4,1},{9,12},{8,5},{13,14},{12,9},{15,10},{14,13... | collective-permute-start | bytes 798728 | tf_op jit(solution)/shard_map/ppermute | solution.py:296
  10.3 7.8 %collective-permute-start.7 = (bf16[65,16,128]{2,1,0:T(8,128)(2,1)S(1)}, bf16[65,16,128]{2,1,0:T(8,128)(2,1)S(1)}, u32[]{:S(2)}, u32[]{:S(2)}) collective-permute-start(bf16[65,16,128]{2,1,0:T(8,128)(2,1)S(1)} %collective-permute-done.2.refs_1_), channel_id=1, source_target_pairs={{0,4},{1,3},{4,8},{5,1},{8,12},{9,5},{12,14},{13,9},{14,10},{15,13... | collective-permute-start | bytes 798728 | tf_op jit(solution)/shard_map/ppermute | solution.py:296
  12.8 8.2 %collective-permute-start.8 = (bf16[65,16,128]{2,1,0:T(8,128)(2,1)S(1)}, bf16[65,16,128]{2,1,0:T(8,128)(2,1)S(1)}, u32[]{:S(2)}, u32[]{:S(2)}) collective-permute-start(bf16[65,16,128]{2,1,0:T(8,128)(2,1)S(1)} %collective-permute-done.3.refs_2_), channel_id=1, source_target_pairs={{0,4},{1,3},{4,8},{5,1},{8,12},{9,5},{12,14},{13,9},{14,10},{15,13... | collective-permute-start | bytes 798728 | tf_op jit(solution)/shard_map/ppermute | solution.py:296
  18.2 6.4 %collective-permute-start.12 = (bf16[65,16,128]{2,1,0:T(8,128)(2,1)S(1)}, bf16[65,16,128]{2,1,0:T(8,128)(2,1)S(1)}, u32[]{:S(2)}, u32[]{:S(2)}) collective-permute-start(bf16[65,16,128]{2,1,0:T(8,128)(2,1)S(1)} %collective-permute-done.7.refs_1_), channel_id=1, source_target_pairs={{0,4},{1,3},{4,8},{5,1},{8,12},{9,5},{12,14},{13,9},{14,10},{15,13... | collective-permute-start | bytes 798728 | tf_op jit(solution)/shard_map/ppermute | solution.py:296
  21.0 6.4 %collective-permute-start.13 = (bf16[65,16,128]{2,1,0:T(8,128)(2,1)S(1)}, bf16[65,16,128]{2,1,0:T(8,128)(2,1)S(1)}, u32[]{:S(2)}, u32[]{:S(2)}) collective-permute-start(bf16[65,16,128]{2,1,0:T(8,128)(2,1)S(1)} %collective-permute-done.8.refs_2_), channel_id=1, source_target_pairs={{0,4},{1,3},{4,8},{5,1},{8,12},{9,5},{12,14},{13,9},{14,10},{15,13... | collective-permute-start | bytes 798728 | tf_op jit(solution)/shard_map/ppermute | solution.py:296
  22.1 10.1 %collective-permute-start.10 = (bf16[65,16,128]{2,1,0:T(8,128)(2,1)S(1)}, bf16[65,16,128]{2,1,0:T(8,128)(2,1)S(1)}, u32[]{:S(2)}, u32[]{:S(2)}) collective-permute-start(bf16[65,16,128]{2,1,0:T(8,128)(2,1)S(1)} %collective-permute-done.8.refs_2_), channel_id=1, source_target_pairs={{0,1},{1,0},{2,3},{3,2},{4,5},{5,4},{6,7},{7,6},{8,9},{9,8},{10,11... | collective-permute-start | bytes 798728 | tf_op jit(solution)/shard_map/ppermute | solution.py:296
  22.1 10.7 %collective-permute-start.9 = (bf16[65,16,128]{2,1,0:T(8,128)(2,1)S(1)}, bf16[65,16,128]{2,1,0:T(8,128)(2,1)S(1)}, u32[]{:S(2)}, u32[]{:S(2)}) collective-permute-start(bf16[65,16,128]{2,1,0:T(8,128)(2,1)S(1)} %collective-permute-done.7.refs_1_), channel_id=1, source_target_pairs={{0,1},{1,0},{2,3},{3,2},{4,5},{5,4},{6,7},{7,6},{8,9},{9,8},{10,11... | collective-permute-start | bytes 798728 | tf_op jit(solution)/shard_map/ppermute | solution.py:296
  24.6 8.3 %collective-permute-start.17 = (bf16[65,16,128]{2,1,0:T(8,128)(2,1)S(1)}, bf16[65,16,128]{2,1,0:T(8,128)(2,1)S(1)}, u32[]{:S(2)}, u32[]{:S(2)}) collective-permute-start(bf16[65,16,128]{2,1,0:T(8,128)(2,1)S(1)} %collective-permute-done.12.refs_1_), channel_id=1, source_target_pairs={{0,4},{1,3},{4,8},{5,1},{8,12},{9,5},{12,14},{13,9},{14,10},{15,13... | collective-permute-start | bytes 798728 | tf_op jit(solution)/shard_map/ppermute | solution.py:296
  25.7 10.3 %collective-permute-start.14 = (bf16[65,16,128]{2,1,0:T(8,128)(2,1)S(1)}, bf16[65,16,128]{2,1,0:T(8,128)(2,1)S(1)}, u32[]{:S(2)}, u32[]{:S(2)}) collective-permute-start(bf16[65,16,128]{2,1,0:T(8,128)(2,1)S(1)} %collective-permute-done.12.refs_1_), channel_id=1, source_target_pairs={{0,1},{1,0},{2,3},{3,2},{4,5},{5,4},{6,7},{7,6},{8,9},{9,8},{10,11... | collective-permute-start | bytes 798728 | tf_op jit(solution)/shard_map/ppermute | solution.py:296
  27.4 8.7 %collective-permute-start.15 = (bf16[65,16,128]{2,1,0:T(8,128)(2,1)S(1)}, bf16[65,16,128]{2,1,0:T(8,128)(2,1)S(1)}, u32[]{:S(2)}, u32[]{:S(2)}) collective-permute-start(bf16[65,16,128]{2,1,0:T(8,128)(2,1)S(1)} %collective-permute-done.13.refs_2_), channel_id=1, source_target_pairs={{0,1},{1,0},{2,3},{3,2},{4,5},{5,4},{6,7},{7,6},{8,9},{9,8},{10,11... | collective-permute-start | bytes 798728 | tf_op jit(solution)/shard_map/ppermute | solution.py:296
  32.2 9.2 %collective-permute-start.4 = (bf16[65,16,128]{2,1,0:T(8,128)(2,1)S(1)}, bf16[65,16,128]{2,1,0:T(8,128)(2,1)S(1)}, u32[]{:S(2)}, u32[]{:S(2)}) collective-permute-start(bf16[65,16,128]{2,1,0:T(8,128)(2,1)S(1)} %collective-permute-done.2.refs_1_), channel_id=1, source_target_pairs={{0,1},{1,0},{2,3},{3,2},{4,5},{5,4},{6,7},{7,6},{8,9},{9,8},{10,11... | collective-permute-start | bytes 798728 | tf_op jit(solution)/shard_map/ppermute | solution.py:296
  32.8 8.6 %collective-permute-start.5 = (bf16[65,16,128]{2,1,0:T(8,128)(2,1)S(1)}, bf16[65,16,128]{2,1,0:T(8,128)(2,1)S(1)}, u32[]{:S(2)}, u32[]{:S(2)}) collective-permute-start(bf16[65,16,128]{2,1,0:T(8,128)(2,1)S(1)} %collective-permute-done.3.refs_2_), channel_id=1, source_target_pairs={{0,1},{1,0},{2,3},{3,2},{4,5},{5,4},{6,7},{7,6},{8,9},{9,8},{10,11... | collective-permute-start | bytes 798728 | tf_op jit(solution)/shard_map/ppermute | solution.py:296
  32.9 6.4 %collective-permute-start.18 = (bf16[65,16,128]{2,1,0:T(8,128)(2,1)S(1)}, bf16[65,16,128]{2,1,0:T(8,128)(2,1)S(1)}, u32[]{:S(2)}, u32[]{:S(2)}) collective-permute-start(bf16[65,16,128]{2,1,0:T(8,128)(2,1)S(1)} %collective-permute-done.17.refs_1_), channel_id=1, source_target_pairs={{0,1},{1,0},{2,3},{3,2},{4,5},{5,4},{6,7},{7,6},{8,9},{9,8},{10,11... | collective-permute-start | bytes 798728 | tf_op jit(solution)/shard_map/ppermute | solution.py:296
  36.0 17.5 %collective-permute-start.11 = (bf16[128,2048]{1,0:T(8,128)(2,1)S(1)}, bf16[128,2048]{1,0:T(8,128)(2,1)S(1)}, u32[]{:S(2)}, u32[]{:S(2)}) collective-permute-start(bf16[128,2048]{1,0:T(8,128)(2,1)S(1)} %get-tuple-element.27), channel_id=1, source_target_pairs={{0,1},{1,0},{2,3},{3,2},{4,5},{5,4},{6,7},{7,6},{8,9},{9,8},{10,11... | collective-permute-start | bytes 1572872 | tf_op jit(solution)/shard_map/ppermute | solution.py:296
  38.8 8.0 %collective-permute-start.16 = (bf16[128,2048]{1,0:T(8,128)(2,1)S(1)}, bf16[128,2048]{1,0:T(8,128)(2,1)S(1)}, u32[]{:S(2)}, u32[]{:S(2)}) collective-permute-start(bf16[128,2048]{1,0:T(8,128)(2,1)S(1)} %get-tuple-element.29), channel_id=1, source_target_pairs={{0,1},{1,0},{2,3},{3,2},{4,5},{5,4},{6,7},{7,6},{8,9},{9,8},{10,11... | collective-permute-start | bytes 1572872 | tf_op jit(solution)/shard_map/ppermute | solution.py:296
  41.3 3.4 %collective-permute-start.19 = (bf16[64,2048]{1,0:T(8,128)(2,1)S(1)}, bf16[64,2048]{1,0:T(8,128)(2,1)S(1)}, u32[]{:S(2)}, u32[]{:S(2)}) collective-permute-start(bf16[64,2048]{1,0:T(8,128)(2,1)S(1)} %get-tuple-element.31), channel_id=1, source_target_pairs={{0,1},{1,0},{2,3},{3,2},{4,5},{5,4},{6,7},{7,6},{8,9},{9,8},{10,11... | collective-permute-start | bytes 786440 | tf_op jit(solution)/shard_map/ppermute | solution.py:296
  44.1 16.3 %collective-permute-start.6 = (bf16[128,2048]{1,0:T(8,128)(2,1)S(1)}, bf16[128,2048]{1,0:T(8,128)(2,1)S(1)}, u32[]{:S(2)}, u32[]{:S(2)}) collective-permute-start(bf16[128,2048]{1,0:T(8,128)(2,1)S(1)} %get-tuple-element.25), channel_id=1, source_target_pairs={{0,1},{1,0},{2,3},{3,2},{4,5},{5,4},{6,7},{7,6},{8,9},{9,8},{10,11... | collective-permute-start | bytes 1572872 | tf_op jit(solution)/shard_map/ppermute | solution.py:296
  44.6 3.9 %collective-permute-start = (bf16[65,16,128]{2,1,0:T(8,128)(2,1)S(1)}, bf16[65,16,128]{2,1,0:T(8,128)(2,1)S(1)}, u32[]{:S(2)}, u32[]{:S(2)}) collective-permute-start(bf16[65,16,128]{2,1,0:T(8,128)(2,1)S(1)} %get-tuple-element.21.refs_1_), channel_id=1, source_target_pairs={{0,1},{1,0},{2,3},{3,2},{4,5},{5,4},{6,7},{7,6},{8,9},{9,8},{10,11... | collective-permute-start | bytes 798728 | tf_op jit(solution)/shard_map/ppermute | solution.py:296
  44.7 5.3 %collective-permute-start.24 = (bf16[32,2048]{1,0:T(8,128)(2,1)S(1)}, bf16[32,2048]{1,0:T(8,128)(2,1)S(1)}, u32[]{:S(2)}, u32[]{:S(2)}) collective-permute-start(bf16[32,2048]{1,0:T(8,128)(2,1)S(1)} %add.19), channel_id=1, source_target_pairs={{4,0},{3,1},{8,4},{1,5},{12,8},{5,9},{14,12},{9,13},{10,14},{13,15... | collective-permute-start | bytes 393224 | tf_op jit(solution)/shard_map/ppermute | solution.py:296
  46.8 5.0 %collective-permute-start.20 = (bf16[32,2048]{1,0:T(8,128)(2,1)S(1)}, bf16[32,2048]{1,0:T(8,128)(2,1)S(1)}, u32[]{:S(2)}, u32[]{:S(2)}) collective-permute-start(bf16[32,2048]{1,0:T(8,128)(2,1)S(1)} %add.15), channel_id=1, source_target_pairs={{4,0},{3,1},{8,4},{1,5},{12,8},{5,9},{14,12},{9,13},{10,14},{13,15... | collective-permute-start | bytes 393224 | tf_op jit(solution)/shard_map/ppermute | solution.py:296
  48.5 8.5 %collective-permute-start.31 = (bf16[32,2048]{1,0:T(8,128)(2,1)S(1)}, bf16[32,2048]{1,0:T(8,128)(2,1)S(1)}, u32[]{:S(2)}, u32[]{:S(2)}) collective-permute-start(bf16[32,2048]{1,0:T(8,128)(2,1)S(1)} %add.26), channel_id=1, source_target_pairs={{4,0},{3,1},{8,4},{1,5},{12,8},{5,9},{14,12},{9,13},{10,14},{13,15... | collective-permute-start | bytes 393224 | tf_op jit(solution)/shard_map/ppermute | solution.py:296
  50.0 8.7 %collective-permute-start.28 = (bf16[32,2048]{1,0:T(8,128)(2,1)S(1)}, bf16[32,2048]{1,0:T(8,128)(2,1)S(1)}, u32[]{:S(2)}, u32[]{:S(2)}) collective-permute-start(bf16[32,2048]{1,0:T(8,128)(2,1)S(1)} %add.23), channel_id=1, source_target_pairs={{4,0},{3,1},{8,4},{1,5},{12,8},{5,9},{14,12},{9,13},{10,14},{13,15... | collective-permute-start | bytes 393224 | tf_op jit(solution)/shard_map/ppermute | solution.py:296
  51.8 8.3 %collective-permute-start.25 = (bf16[32,2048]{1,0:T(8,128)(2,1)S(1)}, bf16[32,2048]{1,0:T(8,128)(2,1)S(1)}, u32[]{:S(2)}, u32[]{:S(2)}) collective-permute-start(bf16[32,2048]{1,0:T(8,128)(2,1)S(1)} %add.20), channel_id=1, source_target_pairs={{4,0},{3,1},{8,4},{1,5},{12,8},{5,9},{14,12},{9,13},{10,14},{13,15... | collective-permute-start | bytes 393224 | tf_op jit(solution)/shard_map/ppermute | solution.py:296
  53.5 6.8 %collective-permute-start.21 = (bf16[32,2048]{1,0:T(8,128)(2,1)S(1)}, bf16[32,2048]{1,0:T(8,128)(2,1)S(1)}, u32[]{:S(2)}, u32[]{:S(2)}) collective-permute-start(bf16[32,2048]{1,0:T(8,128)(2,1)S(1)} %add.16), channel_id=1, source_target_pairs={{4,0},{3,1},{8,4},{1,5},{12,8},{5,9},{14,12},{9,13},{10,14},{13,15... | collective-permute-start | bytes 393224 | tf_op jit(solution)/shard_map/ppermute | solution.py:296
  57.1 5.0 %collective-permute-start.32 = (bf16[32,2048]{1,0:T(8,128)(2,1)S(1)}, bf16[32,2048]{1,0:T(8,128)(2,1)S(1)}, u32[]{:S(2)}, u32[]{:S(2)}) collective-permute-start(bf16[32,2048]{1,0:T(8,128)(2,1)S(1)} %add.27), channel_id=1, source_target_pairs={{4,0},{3,1},{8,4},{1,5},{12,8},{5,9},{14,12},{9,13},{10,14},{13,15... | collective-permute-start | bytes 393224 | tf_op jit(solution)/shard_map/ppermute | solution.py:296
  58.7 5.0 %collective-permute-start.29 = (bf16[32,2048]{1,0:T(8,128)(2,1)S(1)}, bf16[32,2048]{1,0:T(8,128)(2,1)S(1)}, u32[]{:S(2)}, u32[]{:S(2)}) collective-permute-start(bf16[32,2048]{1,0:T(8,128)(2,1)S(1)} %add.24), channel_id=1, source_target_pairs={{4,0},{3,1},{8,4},{1,5},{12,8},{5,9},{14,12},{9,13},{10,14},{13,15... | collective-permute-start | bytes 393224 | tf_op jit(solution)/shard_map/ppermute | solution.py:296
  60.2 5.0 %collective-permute-start.26 = (bf16[32,2048]{1,0:T(8,128)(2,1)S(1)}, bf16[32,2048]{1,0:T(8,128)(2,1)S(1)}, u32[]{:S(2)}, u32[]{:S(2)}) collective-permute-start(bf16[32,2048]{1,0:T(8,128)(2,1)S(1)} %add.21), channel_id=1, source_target_pairs={{4,0},{3,1},{8,4},{1,5},{12,8},{5,9},{14,12},{9,13},{10,14},{13,15... | collective-permute-start | bytes 393224 | tf_op jit(solution)/shard_map/ppermute | solution.py:296
  60.2 7.7 %collective-permute-start.1 = (bf16[64,2048]{1,0:T(8,128)(2,1)S(1)}, bf16[64,2048]{1,0:T(8,128)(2,1)S(1)}, u32[]{:S(2)}, u32[]{:S(2)}) collective-permute-start(bf16[64,2048]{1,0:T(8,128)(2,1)S(1)} %get-tuple-element.23), channel_id=1, source_target_pairs={{0,1},{1,0},{2,3},{3,2},{4,5},{5,4},{6,7},{7,6},{8,9},{9,8},{10,11... | collective-permute-start | bytes 786440 | tf_op jit(solution)/shard_map/ppermute | solution.py:296
  60.4 6.2 %collective-permute-start.22 = (bf16[32,2048]{1,0:T(8,128)(2,1)S(1)}, bf16[32,2048]{1,0:T(8,128)(2,1)S(1)}, u32[]{:S(2)}, u32[]{:S(2)}) collective-permute-start(bf16[32,2048]{1,0:T(8,128)(2,1)S(1)} %add.17), channel_id=1, source_target_pairs={{4,0},{3,1},{8,4},{1,5},{12,8},{5,9},{14,12},{9,13},{10,14},{13,15... | collective-permute-start | bytes 393224 | tf_op jit(solution)/shard_map/ppermute | solution.py:296
  62.1 5.8 %collective-permute-start.33 = (bf16[32,2048]{1,0:T(8,128)(2,1)S(1)}, bf16[32,2048]{1,0:T(8,128)(2,1)S(1)}, u32[]{:S(2)}, u32[]{:S(2)}) collective-permute-start(bf16[32,2048]{1,0:T(8,128)(2,1)S(1)} %add.28), channel_id=1, source_target_pairs={{4,1},{3,0},{8,5},{1,4},{12,9},{5,8},{14,13},{9,12},{10,15},{13,14... | collective-permute-start | bytes 393224 | tf_op jit(solution)/shard_map/ppermute | solution.py:296
  63.8 4.5 %collective-permute-start.30 = (bf16[32,2048]{1,0:T(8,128)(2,1)S(1)}, bf16[32,2048]{1,0:T(8,128)(2,1)S(1)}, u32[]{:S(2)}, u32[]{:S(2)}) collective-permute-start(bf16[32,2048]{1,0:T(8,128)(2,1)S(1)} %add.25), channel_id=1, source_target_pairs={{4,1},{3,0},{8,5},{1,4},{12,9},{5,8},{14,13},{9,12},{10,15},{13,14... | collective-permute-start | bytes 393224 | tf_op jit(solution)/shard_map/ppermute | solution.py:296
  65.2 5.6 %collective-permute-start.27 = (bf16[32,2048]{1,0:T(8,128)(2,1)S(1)}, bf16[32,2048]{1,0:T(8,128)(2,1)S(1)}, u32[]{:S(2)}, u32[]{:S(2)}) collective-permute-start(bf16[32,2048]{1,0:T(8,128)(2,1)S(1)} %add.22), channel_id=1, source_target_pairs={{4,0},{3,1},{8,4},{1,5},{12,8},{5,9},{14,12},{9,13},{10,14},{13,15... | collective-permute-start | bytes 393224 | tf_op jit(solution)/shard_map/ppermute | solution.py:296
  66.6 5.6 %collective-permute-start.23 = (bf16[32,2048]{1,0:T(8,128)(2,1)S(1)}, bf16[32,2048]{1,0:T(8,128)(2,1)S(1)}, u32[]{:S(2)}, u32[]{:S(2)}) collective-permute-start(bf16[32,2048]{1,0:T(8,128)(2,1)S(1)} %add.18), channel_id=1, source_target_pairs={{4,0},{3,1},{8,4},{1,5},{12,8},{5,9},{14,12},{9,13},{10,14},{13,15... | collective-permute-start | bytes 393224 | tf_op jit(solution)/shard_map/ppermute | solution.py:296
